TPU v7x, 512 devices: a whole 4x4x16 slice. The times are simulated.
512 devices in a mesh: segment: 64 (over y, x, z_hi, core), fsdp: 8 (over z_lo).
Axes of the slice: x: 4, y: 4, z: 16 (z_hi: 2, z_lo: 8; z = z_hi * 8 + z_lo), core: 2. Of those that a mesh axis runs over, the one named last changes fastest.
Arguments:
- stream: bfloat16 [2, 64, 512, 4096], P(None, 'segment', 'fsdp'), may hold values from -60 to 60
- gain: bfloat16 [2, 64, 4096], P(None, 'segment'), may hold values from 0.099609375 to 1.8984375
- w_query: bfloat16 [2, 64, 32, 128, 128], P(None, 'segment', 'fsdp'), may hold values from -20 to 20
- w_key: bfloat16 [2, 64, 32, 128, 128], P(None, 'segment', 'fsdp'), may hold values from -20 to 20
- w_value: bfloat16 [2, 64, 32, 128, 128], P(None, 'segment', 'fsdp'), may hold values from -0.5 to 0.5
- w_mix: bfloat16 [2, 64, 128, 32, 32], P(None, 'segment', 'fsdp'), may hold values from -1 to 1
- active: int32 [2, 64], P(None, 'segment'), may hold values from 0 to 1
- random_blocks: int32 [2, 64, 8, 2], P(None, 'segment'), may hold values from 0 to 7
Outputs:
- advanced: bfloat16 [2, 64, 512, 4096], P(None, 'segment', 'fsdp')
All inputs are finite; a program needn't handle non-finite values.
Results may differ from a plain program's by a relative error of at most 0.009.
Values may be sent and summed in bfloat16 or wider, within the bound.
No kernel may reach another device: no remote copies, remote signals or barrier semaphores. Data moves between devices by JAX's collectives and lax.ppermute only.
A program may use at most 64 MiB of HBM per device.

v0:
```python
import jax
import jax.numpy as jnp
from jax import lax
from jax.sharding import PartitionSpec as P

BLK = 64
ROUNDS = 2


EPS = 1e-05


def shifted(value, axis, by):
    devices = lax.axis_size(axis)
    return lax.ppermute(value, axis, [(i, (i + by) % devices) for i in range(devices)])


def block_attention(query, keys, values, random_ids):
    heads, seq_len, head_width = query.shape
    count = seq_len // BLK
    query_blocks = query.reshape(heads, count, BLK, head_width)
    key_blocks = keys.reshape(heads, count, BLK, head_width)
    value_blocks = values.reshape(heads, count, BLK, head_width)
    block_ids = jnp.arange(count, dtype=jnp.int32)
    window = jnp.stack(
        [(block_ids - 1) % count, block_ids, (block_ids + 1) % count, jnp.zeros_like(block_ids)],
        axis=1,
    )
    chosen = jnp.concatenate([window, random_ids], axis=1)
    picked_keys = key_blocks[:, chosen].reshape(heads, count, chosen.shape[1] * BLK, head_width)
    picked_values = value_blocks[:, chosen].reshape(heads, count, chosen.shape[1] * BLK, head_width)
    scores = jnp.einsum(
        "hnqd,hnkd->hnqk", query_blocks, picked_keys, preferred_element_type=jnp.float32
    )
    row_max = jnp.max(scores, axis=-1, keepdims=True)
    powers = jnp.exp(scores - row_max)
    weights = (powers / jnp.sum(powers, axis=-1, keepdims=True)).astype(jnp.bfloat16)
    mixed = jnp.einsum(
        "hnqk,hnkd->hnqd", weights, picked_values, preferred_element_type=jnp.float32
    ).astype(jnp.bfloat16)
    return mixed.reshape(heads, seq_len, head_width)


def head_attention(view, queries_w, keys_w, values_w, random_ids):

    def one_segment(items):
        rows, weight_q, weight_k, weight_v, ids = items
        raw = jnp.einsum("thc,hcd->htd", rows, weight_q, preferred_element_type=jnp.float32)
        query = (raw * rows.shape[-1] ** (-0.5)).astype(jnp.bfloat16)
        keys = jnp.einsum(
            "thc,hcd->htd", rows, weight_k, preferred_element_type=jnp.float32
        ).astype(jnp.bfloat16)
        values = jnp.einsum(
            "thc,hcd->htd", rows, weight_v, preferred_element_type=jnp.float32
        ).astype(jnp.bfloat16)
        return block_attention(query, keys, values, ids)

    return lax.map(one_segment, (view, queries_w, keys_w, values_w, random_ids))


def mix_heads(attended, mix_w):
    return jnp.einsum(
        "vhtc,vchg->vtgc",
        attended,
        lax.all_gather(mix_w, "fsdp", axis=1, tiled=True),
        preferred_element_type=jnp.float32,
    ).astype(jnp.bfloat16)


def cycle(values):
    moved = shifted(values, "segment", 1)
    return jnp.where(lax.axis_index("segment") == 0, jnp.roll(moved, 1, axis=0), moved)


def token_layer(state, params):
    queries_w, keys_w, values_w, mix_w, gains, live, random_ids = params
    wide = state.astype(jnp.float32)
    mean_sq = jnp.mean(wide * wide, axis=2, keepdims=True)
    normed = (wide * lax.rsqrt(mean_sq + EPS) * gains[:, None, :].astype(jnp.float32)).astype(
        jnp.bfloat16
    )
    view = normed.reshape(state.shape[0], state.shape[1], -1, queries_w.shape[-1])
    gathered = lax.all_to_all(view, "fsdp", split_axis=2, concat_axis=1, tiled=True)
    attended = head_attention(gathered, queries_w, keys_w, values_w, random_ids)
    returned = lax.all_to_all(attended, "fsdp", split_axis=2, concat_axis=1, tiled=True)
    mixed = mix_heads(returned, mix_w)
    updated = (wide + mixed.reshape(wide.shape).astype(jnp.float32)).astype(jnp.bfloat16)
    return jnp.where(live[:, None, None] > 0, updated, state)


def shards(stream, gain, w_query, w_key, w_value, w_mix, active, random_blocks):
    params = (
        w_query[:, 0],
        w_key[:, 0],
        w_value[:, 0],
        w_mix[:, 0],
        gain[:, 0],
        active[:, 0],
        random_blocks[:, 0],
    )
    state = stream[:, 0]
    for round_index in range(ROUNDS):
        state = token_layer(state, params)
        state = cycle(state)
    return state[:, None]


def solution(mesh):
    in_specs = (
        P(None, "segment", "fsdp", None),
        P(None, "segment", None),
        P(None, "segment", "fsdp", None, None),
        P(None, "segment", "fsdp", None, None),
        P(None, "segment", "fsdp", None, None),
        P(None, "segment", "fsdp", None, None),
        P(None, "segment"),
        P(None, "segment", None, None),
    )
    out_specs = P(None, "segment", "fsdp", None)
    return jax.shard_map(shards, mesh=mesh, in_specs=in_specs, out_specs=out_specs, check_vma=False)
```

profile of v0, /device:TPU:32, one launch (start us, length us, event | category | flops | bytes accessed | tf_op | source)
XLA Modules:
  0.0 546.5 jit_solution(105183954423557872)
XLA Ops:
  5.5 12.8 %all-to-all-start = ((bf16[2,64,32,128]{3,1,0,2:T(8,128)(2,1)}), bf16[2,64,32,128]{3,1,0,2:T(8,128)(2,1)S(1)}, u32[]{:S(2)}, u32[]{:S(2)}) async-start(bf16[2,64,32,128]{3,1,0,2:T(8,128)(2,1)} %copy.69), calls=%async_computation | async-start | bytes 2097152 | tf_op jit(solution)/shard_map/all_to_all | solution.py:83
  18.3 48.3 %all-to-all-done = bf16[2,64,32,128]{3,1,0,2:T(8,128)(2,1)S(1)} async-done(((bf16[2,64,32,128]{3,1,0,2:T(8,128)(2,1)}), bf16[2,64,32,128]{3,1,0,2:T(8,128)(2,1)S(1)}, u32[]{:S(2)}, u32[]{:S(2)}) %all-to-all-start) | async-done | bytes 1048608 | tf_op jit(solution)/shard_map/all_to_all | solution.py:83
  68.9 56.5 %while.24 = (s32[]{:T(128)}, bf16[2,4,512,128]{3,1,0,2:T(4,128)(2,1)}, bf16[2,512,4,128]{3,1,2,0:T(8,128)(2,1)}, bf16[2,4,128,128]{3,2,1,0:T(8,128)(2,1)S(1)}, b...) while((s32[]{:T(128)}, ...), condition=%wide.region_4.5_spmd, body=%wide.region_1.4_spmd.sunk | while | flops 609226816 | bytes 59140032 | solution.py:58
  73.3 2.9 copy.106
  87.6 7.3 %fusion.139 = bf16[4,8,64,128]{3,2,1,0:T(8,128)(2,1)} fusion(bf16[4,8,384,128]{3,2,1,0:T(8,128)(2,1)S(1)} %bitcast.258, f32[4,8,64]{2,1,0:T(8,128)S(1)} %fusion.138, f32[4,8,64,384]{3,2,1,0:T(8,128)} %copy-done), kind=kOutput, calls=%fused_computation.9.clone.1 | convolution fusion | flops 203950464 | bytes 6823936 | tf_op jit(solution)/shard_map/while/body/eval_jaxpr/hnqk,hnkd->hnqd/dot_general | solution.py:38
  101.5 2.9 copy.106
  115.9 7.3 %fusion.139 = bf16[4,8,64,128]{3,2,1,0:T(8,128)(2,1)} fusion(bf16[4,8,384,128]{3,2,1,0:T(8,128)(2,1)S(1)} %bitcast.258, f32[4,8,64]{2,1,0:T(8,128)S(1)} %fusion.138, f32[4,8,64,384]{3,2,1,0:T(8,128)} %copy-done), kind=kOutput, calls=%fused_computation.9.clone.1 | convolution fusion | flops 203950464 | bytes 6823936 | tf_op jit(solution)/shard_map/while/body/eval_jaxpr/hnqk,hnkd->hnqd/dot_general | solution.py:38
  125.4 7.2 %all-to-all-start.1 = ((bf16[2,4,512,128]{3,1,0,2:T(4,128)(2,1)}), bf16[2,4,512,128]{3,1,0,2:T(4,128)(2,1)S(1)}, u32[]{:S(2)}, u32[]{:S(2)}) async-start(bf16[2,4,512,128]{3,1,0,2:T(4,128)(2,1)} %get-tuple-element.187), calls=%async_computation.1 | async-start | bytes 2097152 | tf_op jit(solution)/shard_map/all_to_all | solution.py:85
  134.4 89.3 %all-gather = bf16[2,1,128,32,32]{3,4,2,0,1:T(8,128)(2,1)S(1)} all-gather(bf16[2,1,16,32,32]{3,4,2,0,1:T(8,128)(2,1)} %copy.74), channel_id=2, replica_groups=mesh['segment'=64,'fsdp'=8] {'fsdp'}, dimensions={2}, use_global_device_ids=true | all-gather | bytes 589824 | tf_op jit(solution)/shard_map/all_gather | solution.py:65
  223.7 3.3 copy.73
  227.0 4.2 convert_bitcast_fusion.1
  231.2 5.3 copy.75
  241.7 51.0 %collective-permute-done = bf16[2,64,4096]{2,1,0:T(8,128)(2,1)S(1)} collective-permute-done((bf16[2,64,4096]{2,1,0:T(8,128)(2,1)}, bf16[2,64,4096]{2,1,0:T(8,128)(2,1)S(1)}, u32[]{:S(2)}, u32[]{:S(2)}) %collective-permute-start) | collective-permute-done | bytes 1048608 | tf_op jit(solution)/shard_map/ppermute | solution.py:15
  295.6 19.6 %all-to-all-start.2 = ((bf16[2,64,32,128]{3,1,0,2:T(8,128)(2,1)}), bf16[2,64,32,128]{3,1,0,2:T(8,128)(2,1)S(1)}, u32[]{:S(2)}, u32[]{:S(2)}) async-start(bf16[2,64,32,128]{3,1,0,2:T(8,128)(2,1)} %copy_bitcast_fusion), calls=%async_computation.2 | async-start | bytes 2097152 | tf_op jit(solution)/shard_map/all_to_all | solution.py:83
  315.2 38.3 %all-to-all-done.2 = bf16[2,64,32,128]{3,1,0,2:T(8,128)(2,1)S(1)} async-done(((bf16[2,64,32,128]{3,1,0,2:T(8,128)(2,1)}), bf16[2,64,32,128]{3,1,0,2:T(8,128)(2,1)S(1)}, u32[]{:S(2)}, u32[]{:S(2)}) %all-to-all-start.2) | async-done | bytes 1048608 | tf_op jit(solution)/shard_map/all_to_all | solution.py:83
  355.8 56.6 %while.25 = (s32[]{:T(128)}, bf16[2,4,512,128]{3,1,0,2:T(4,128)(2,1)}, bf16[2,512,4,128]{3,1,2,0:T(8,128)(2,1)}, bf16[2,4,128,128]{3,2,1,0:T(8,128)(2,1)S(1)}, b...) while((s32[]{:T(128)}, ...), condition=%wide.region_9.10_spmd, body=%wide.region_6.9_spmd.sunk | while | flops 609226816 | bytes 59140032 | solution.py:58
  360.1 2.9 copy.110
  374.5 7.3 %fusion.156 = bf16[4,8,64,128]{3,2,1,0:T(8,128)(2,1)} fusion(bf16[4,8,384,128]{3,2,1,0:T(8,128)(2,1)S(1)} %bitcast.259, f32[4,8,64]{2,1,0:T(8,128)S(1)} %fusion.155, f32[4,8,64,384]{3,2,1,0:T(8,128)} %copy-done.1), kind=kOutput, calls=%fused_computation.49.clone.1 | convolution fusion | flops 203950464 | bytes 6823936 | tf_op jit(solution)/shard_map/while/body/eval_jaxpr/hnqk,hnkd->hnqd/dot_general | solution.py:38
  402.8 7.3 %fusion.156 = bf16[4,8,64,128]{3,2,1,0:T(8,128)(2,1)} fusion(bf16[4,8,384,128]{3,2,1,0:T(8,128)(2,1)S(1)} %bitcast.259, f32[4,8,64]{2,1,0:T(8,128)S(1)} %fusion.155, f32[4,8,64,384]{3,2,1,0:T(8,128)} %copy-done.1), kind=kOutput, calls=%fused_computation.49.clone.1 | convolution fusion | flops 203950464 | bytes 6823936 | tf_op jit(solution)/shard_map/while/body/eval_jaxpr/hnqk,hnkd->hnqd/dot_general | solution.py:38
  412.4 55.1 %all_to_all.72 = bf16[2,4,512,128]{3,1,0,2:T(4,128)(2,1)S(1)} all-to-all(bf16[2,4,512,128]{3,1,0,2:T(4,128)(2,1)} %get-tuple-element.188), channel_id=1, replica_groups=mesh['segment'=64,'fsdp'=8] {'fsdp'}, dimensions={2} | all-to-all | bytes 2097152 | tf_op jit(solution)/shard_map/all_to_all | solution.py:85
  467.5 3.2 copy.79
  470.7 4.2 convert_bitcast_fusion
  474.9 4.5 copy.80
  484.9 60.4 %collective-permute-done.1 = bf16[2,64,4096]{2,1,0:T(8,128)(2,1)S(1)} collective-permute-done((bf16[2,64,4096]{2,1,0:T(8,128)(2,1)S(1)}, bf16[2,64,4096]{2,1,0:T(8,128)(2,1)S(1)}, u32[]{:S(2)}, u32[]{:S(2)}) %collective-permute-start.1) | collective-permute-done | bytes 1048608 | tf_op jit(solution)/shard_map/ppermute | solution.py:15
  (123 shorter events, 101.5 us)
Async XLA Ops:
  5.5 63.4 %copy-start.7 = (bf16[2,1,4,128,128]{4,3,2,1,0:T(8,128)(2,1)S(1)}, bf16[2,1,4,128,128]{4,3,2,1,0:T(8,128)(2,1)}, u32[]{:S(2)}) copy-start(bf16[2,1,4,128,128]{4,3,2,1,0:T(8,128)(2,1)} %param.14) | copy-start | bytes 786436
  5.5 63.4 %copy-start.8 = (s32[2,1,8,2]{2,3,1,0:T(2,128)S(1)}, s32[2,1,8,2]{2,3,1,0:T(2,128)}, u32[]{:S(2)}) copy-start(s32[2,1,8,2]{2,3,1,0:T(2,128)} %param.19) | copy-start | bytes 388
  5.5 61.1 %all-to-all-start = ((bf16[2,64,32,128]{3,1,0,2:T(8,128)(2,1)}), bf16[2,64,32,128]{3,1,0,2:T(8,128)(2,1)S(1)}, u32[]{:S(2)}, u32[]{:S(2)}) async-start(bf16[2,64,32,128]{3,1,0,2:T(8,128)(2,1)} %copy.69), calls=%async_computation | async-start | bytes 2097152 | tf_op jit(solution)/shard_map/all_to_all | solution.py:83
  68.9 65.4 %copy-start.9 = (s32[2,1]{0,1:T(1,128)S(1)}, s32[2,1]{0,1:T(1,128)}, u32[]{:S(2)}) copy-start(s32[2,1]{0,1:T(1,128)} %param.18) | copy-start | bytes 28
  79.0 1.7 copy-start
  107.3 1.7 copy-start
  125.4 98.2 %all-to-all-start.1 = ((bf16[2,4,512,128]{3,1,0,2:T(4,128)(2,1)}), bf16[2,4,512,128]{3,1,0,2:T(4,128)(2,1)S(1)}, u32[]{:S(2)}, u32[]{:S(2)}) async-start(bf16[2,4,512,128]{3,1,0,2:T(4,128)(2,1)} %get-tuple-element.187), calls=%async_computation.1 | async-start | bytes 2097152 | tf_op jit(solution)/shard_map/all_to_all | solution.py:85
  223.7 7.6 %copy-start.2 = (bf16[2,1,128,32,32]{3,4,2,0,1:T(8,128)(2,1)}, bf16[2,1,128,32,32]{3,4,2,0,1:T(8,128)(2,1)S(1)}, u32[]{:S(2)}) copy-start(bf16[2,1,128,32,32]{3,4,2,0,1:T(8,128)(2,1)S(1)} %all-gather) | copy-start | bytes 1572868
  236.5 1.9 copy-start.4
  239.8 52.9 %collective-permute-start = (bf16[2,64,4096]{2,1,0:T(8,128)(2,1)}, bf16[2,64,4096]{2,1,0:T(8,128)(2,1)S(1)}, u32[]{:S(2)}, u32[]{:S(2)}) collective-permute-start(bf16[2,64,4096]{2,1,0:T(8,128)(2,1)} %fusion.67), channel_id=1, source_target_pairs={{0,8},{8,16},{16,24},{24,32},{32,40},{40,48},{48,56},{56,64},{64,7... | collective-permute-start | bytes 3145736 | tf_op jit(solution)/shard_map/ppermute | solution.py:15
  293.2 1.0 copy-start.5
  295.6 57.8 %all-to-all-start.2 = ((bf16[2,64,32,128]{3,1,0,2:T(8,128)(2,1)}), bf16[2,64,32,128]{3,1,0,2:T(8,128)(2,1)S(1)}, u32[]{:S(2)}, u32[]{:S(2)}) async-start(bf16[2,64,32,128]{3,1,0,2:T(8,128)(2,1)} %copy_bitcast_fusion), calls=%async_computation.2 | async-start | bytes 2097152 | tf_op jit(solution)/shard_map/all_to_all | solution.py:83
  365.9 1.7 copy-start.1
  394.2 1.7 copy-start.1
  412.4 58.3 %copy-start.3 = (bf16[2,1,128,32,32]{3,4,2,0,1:T(8,128)(2,1)S(1)}, bf16[2,1,128,32,32]{3,4,2,0,1:T(8,128)(2,1)}, u32[]{:S(2)}) copy-start(bf16[2,1,128,32,32]{3,4,2,0,1:T(8,128)(2,1)} %copy-done.2) | copy-start | bytes 1572868
  479.4 1.6 copy-start.6
  483.0 62.3 %collective-permute-start.1 = (bf16[2,64,4096]{2,1,0:T(8,128)(2,1)S(1)}, bf16[2,64,4096]{2,1,0:T(8,128)(2,1)S(1)}, u32[]{:S(2)}, u32[]{:S(2)}) collective-permute-start(bf16[2,64,4096]{2,1,0:T(8,128)(2,1)S(1)} %fusion.66), channel_id=1, source_target_pairs={{0,8},{8,16},{16,24},{24,32},{32,40},{40,48},{48,56},{56,64},{64,7... | collective-permute-start | bytes 3145736 | tf_op jit(solution)/shard_map/ppermute | solution.py:15
where the time goes:
time: 548 us; the launch traced here: 547 us
  waiting for transfers between devices  198 us (36%)
  blocking collectives  144 us (26%)
  local copies, waits for them, and re-layouts  85.7 us (16%)
  matrix products  59.8 us (11%)
  starting transfers between devices  43.3 us (8%)
  other arithmetic  14.7 us (3%)
    ppermute x2, waiting for transfers between devices, shifted(): lax.ppermute(value, axis, [(i, (i + by) % devices) for i in range(devices)])  111 us
    all_gather x1, blocking collectives, mix_heads(): lax.all_gather(mix_w, 'fsdp', axis=1, tiled=True)  89.3 us
    all_to_all x2, waiting for transfers between devices, token_layer(): lax.all_to_all(view, 'fsdp', split_axis=2, concat_axis=1, tiled=True)  86.6 us
    all_to_all x1, blocking collectives, token_layer(): lax.all_to_all(attended, 'fsdp', split_axis=2, concat_axis=1, tiled=True)  55.1 us
    all_to_all x2, starting transfers between devices, token_layer(): lax.all_to_all(view, 'fsdp', split_axis=2, concat_axis=1, tiled=True)  32.4 us
    dot_general x4, matrix products, block_attention(): jnp.einsum('hnqk,hnkd->hnqd', weights, picked_values, preferred_element_t...  29.3 us
    gather x8, local copies, waits for them, and re-layouts, block_attention(): value_blocks[:, chosen]  22.4 us
    gather x8, local copies, waits for them, and re-layouts, block_attention(): key_blocks[:, chosen]  22.3 us
  transfers between devices with their start and end apart: 5, of which 4 were waited for; matrix products, arithmetic and copies ran while one was open for 0% of the time, Pallas kernels for 0%

commit v1 on v0

v1 whole, which is shorter than its diff:
```python
import jax
import jax.numpy as jnp
from jax import lax
from jax.experimental import pallas as pl
from jax.experimental.pallas import tpu as pltpu
from jax.sharding import PartitionSpec as P

BLK = 64
ROUNDS = 2
EPS = 1e-05
BF = jnp.bfloat16
F32 = jnp.float32


def norm_kernel(which, x_ref, gain_ref, out_ref):
    groups, rows, width = out_ref.shape
    for start in range(0, rows, 16):
        wide = x_ref[start : start + 16, :].astype(F32)
        mean_sq = jnp.mean(wide * wide, axis=1, keepdims=True)
        normed = wide * lax.rsqrt(mean_sq + EPS) * gain_ref[0].astype(F32)
        normed = normed.astype(BF)
        for group in range(groups):
            out_ref[group, start : start + 16, :] = normed[:, group * width : (group + 1) * width]


def norm(which, x, gain, groups):
    rows, features = x.shape
    out = jax.ShapeDtypeStruct((groups, rows, features // groups), BF)
    return pl.pallas_call(
        norm_kernel,
        out_shape=out,
        grid_spec=pltpu.PrefetchScalarGridSpec(
            num_scalar_prefetch=1,
            grid=(1,),
            in_specs=[
                pl.BlockSpec((rows, features), lambda i, which: (0, 0)),
                pl.BlockSpec((1, 1, features), lambda i, which: (which[0], 0, 0)),
            ],
            out_specs=pl.BlockSpec(out.shape, lambda i, which: (0, 0, 0)),
        ),
        cost_estimate=pl.CostEstimate(
            flops=rows * features * 6, bytes_accessed=rows * features * 4, transcendentals=rows
        ),
        name="norm",
    )(which, x, gain)


def attention_kernel(which, ids, rows_ref, wq_ref, wk_ref, wv_ref, out_ref, k_ref, v_ref):
    count, block, width = rows_ref.shape
    rows = rows_ref[...].reshape(count * block, width)
    query = jnp.dot(rows, wq_ref[0, 0], preferred_element_type=F32)
    query = (query * width ** (-0.5)).astype(BF)
    k_ref[...] = jnp.dot(rows, wk_ref[0, 0], preferred_element_type=F32).astype(BF)
    v_ref[...] = jnp.dot(rows, wv_ref[0, 0], preferred_element_type=F32).astype(BF)
    picks = ids.shape[0] // (2 * count)
    base = which[0] * count * picks
    for i in range(count):
        starts = [(i - 1) % count * block, i * block, (i + 1) % count * block, 0]
        for r in range(picks):
            starts.append(pl.multiple_of(ids[base + i * picks + r] * block, block))
        keys = jnp.concatenate([k_ref[pl.ds(s, block), :] for s in starts], axis=0)
        values = jnp.concatenate([v_ref[pl.ds(s, block), :] for s in starts], axis=0)
        scores = lax.dot_general(
            query[i * block : (i + 1) * block],
            keys,
            (((1,), (1,)), ((), ())),
            preferred_element_type=F32,
        )
        powers = jnp.exp(scores - jnp.max(scores, axis=1, keepdims=True))
        total = jnp.sum(powers, axis=1, keepdims=True)
        mixed = jnp.dot(powers.astype(BF), values, preferred_element_type=F32)
        out_ref[i] = (mixed / total).astype(BF)


def attention(which, ids, rows, wq, wk, wv):
    count, block, features = rows.shape
    heads, width = wq.shape[1], wq.shape[2]
    weight_spec = pl.BlockSpec((1, 1, width, width), lambda h, which, ids: (which[0], h, 0, 0))
    row_spec = pl.BlockSpec((count, block, width), lambda h, which, ids: (0, 0, h))
    return pl.pallas_call(
        attention_kernel,
        out_shape=jax.ShapeDtypeStruct(rows.shape, BF),
        grid_spec=pltpu.PrefetchScalarGridSpec(
            num_scalar_prefetch=2,
            grid=(heads,),
            in_specs=[row_spec, weight_spec, weight_spec, weight_spec],
            out_specs=row_spec,
            scratch_shapes=[pltpu.VMEM((count * block, width), BF)] * 2,
        ),
        cost_estimate=pl.CostEstimate(
            flops=heads * count * block * width * (6 * width + 4 * 6 * block),
            bytes_accessed=count * block * features * 4 + heads * width * width * 6,
            transcendentals=heads * count * block * 6 * block,
        ),
        name="attention",
    )(which, ids, rows, wq, wk, wv)


def mix_weights_kernel(place, gathered_ref, out_ref):
    groups = gathered_ref.shape[0]
    for v in range(out_ref.shape[0]):
        rows = jnp.concatenate([gathered_ref[place[j], v] for j in range(groups)], axis=0)
        out_ref[v] = rows.astype(F32).T


def gather_mix_weights(w_mix, size):
    me = lax.axis_index("fsdp")
    layers, mine, heads, _ = w_mix.shape
    held = w_mix.reshape(1, layers, mine, heads * heads)
    bits = size.bit_length() - 1
    order = [0]
    for b in reversed(range(bits)):
        other = lax.ppermute(held, "fsdp", [(i, i ^ (1 << b)) for i in range(size)])
        held = jnp.concatenate([held, other], axis=0)
        order = order + [o ^ (1 << b) for o in order]
    back = [0] * size
    for position, o in enumerate(order):
        back[o] = position
    place = jnp.array(back, jnp.int32)[jnp.arange(size, dtype=jnp.int32) ^ me]
    return pl.pallas_call(
        mix_weights_kernel,
        out_shape=jax.ShapeDtypeStruct((layers, heads * heads, mine * size), F32),
        grid_spec=pltpu.PrefetchScalarGridSpec(
            num_scalar_prefetch=1,
            grid=(1,),
            in_specs=[pl.BlockSpec(held.shape, lambda i, place: (0, 0, 0, 0))],
            out_specs=pl.BlockSpec(
                (layers, heads * heads, mine * size), lambda i, place: (0, 0, 0)
            ),
        ),
        name="mix_weights",
    )(place, held)


def mix_kernel(which, active, att_ref, w_ref, x_ref, out_ref, wide_ref):
    groups, rows, features = att_ref.shape
    width = w_ref.shape[2]
    per = features // width
    heads = groups * per
    for h in range(heads):
        lanes = pl.ds(h % per * width, width)
        wide_ref[h] = att_ref[h // per, :, lanes].astype(F32)
    live = active[which[0]] > 0
    step = 4

    def body(i, carry):
        totals = [jnp.zeros((rows, width), F32) for _ in range(step)]
        for h in range(heads):
            attended = wide_ref[h]
            for k in range(step):
                row = w_ref[0, pl.ds(h * heads + i * step + k, 1), :]
                totals[k] = totals[k] + attended * row
        for k in range(step):
            lanes = pl.ds(pl.multiple_of((i * step + k) * width, width), width)
            state = x_ref[:, lanes]
            updated = (state.astype(F32) + totals[k].astype(BF).astype(F32)).astype(BF)
            out_ref[:, lanes] = jnp.where(live, updated, state)
        return carry

    lax.fori_loop(0, heads // step, body, 0)


def mix(which, active, attended, weights, x):
    rows, features = x.shape
    heads2, width = weights.shape[1:]
    return pl.pallas_call(
        mix_kernel,
        out_shape=jax.ShapeDtypeStruct(x.shape, BF),
        grid_spec=pltpu.PrefetchScalarGridSpec(
            num_scalar_prefetch=2,
            grid=(1,),
            in_specs=[
                pl.BlockSpec(attended.shape, lambda i, which, active: (0, 0, 0)),
                pl.BlockSpec((1, heads2, width), lambda i, which, active: (which[0], 0, 0)),
                pl.BlockSpec((rows, features), lambda i, which, active: (0, 0)),
            ],
            out_specs=pl.BlockSpec((rows, features), lambda i, which, active: (0, 0)),
            scratch_shapes=[pltpu.VMEM((features // width, rows, width), F32)],
        ),
        cost_estimate=pl.CostEstimate(
            flops=rows * heads2 * width * 2,
            bytes_accessed=rows * features * 6 + heads2 * width * 4,
            transcendentals=0,
        ),
        name="mix",
    )(which, active, attended, weights, x)


def exchange(value):
    return lax.all_to_all(value, "fsdp", split_axis=0, concat_axis=0, tiled=True)


def shifted(value):
    devices = lax.axis_size("segment")
    return lax.ppermute(value, "segment", [(i, (i + 1) % devices) for i in range(devices)])


def shards(stream, gain, w_query, w_key, w_value, w_mix, active, random_blocks):
    segment = lax.axis_index("segment")
    size = lax.axis_size("fsdp")
    slots = stream.shape[0]
    wq, wk, wv = w_query[:, 0], w_key[:, 0], w_value[:, 0]
    live = active[:, 0]
    ids = random_blocks[:, 0].reshape(-1)
    states = [stream[k, 0] for k in range(slots)]
    mix_w = gather_mix_weights(w_mix[:, 0], size)
    for r in range(ROUNDS):
        for k in range(slots):
            turn = jnp.where(segment < r, 1, 0)
            which = ((k + turn) % slots).astype(jnp.int32).reshape(1)
            rows = exchange(norm(which, states[k], gain, size))
            attended = exchange(attention(which, ids, rows, wq, wk, wv))
            states[k] = shifted(mix(which, live, attended, mix_w, states[k]))
    first = segment < ROUNDS
    outs = [jnp.where(first, states[(k + 1) % slots], states[k]) for k in range(slots)]
    return jnp.stack(outs)[:, None]


def solution(mesh):
    in_specs = (
        P(None, "segment", "fsdp", None),
        P(None, "segment", None),
        P(None, "segment", "fsdp", None, None),
        P(None, "segment", "fsdp", None, None),
        P(None, "segment", "fsdp", None, None),
        P(None, "segment", "fsdp", None, None),
        P(None, "segment"),
        P(None, "segment", None, None),
    )
    out_specs = P(None, "segment", "fsdp", None)
    return jax.shard_map(shards, mesh=mesh, in_specs=in_specs, out_specs=out_specs, check_vma=False)
```

time: 548 us -> 428 us (0.78)
  the two profiles are of different devices: /device:TPU:32 before, /device:TPU:20 now
where the time goes in v1:
time: 428 us; the launch traced here: 427 us
  waiting for transfers between devices  263 us (61%)
  Pallas kernels  80.6 us (19%)
  starting transfers between devices  68.2 us (16%)
  local copies, waits for them, and re-layouts  13.1 us (3%)
    all_to_all x8, waiting for transfers between devices, exchange(): lax.all_to_all(value, 'fsdp', split_axis=0, concat_axis=0, tiled=True)  143 us
    ppermute x4, waiting for transfers between devices, shifted(): lax.ppermute(value, 'segment', [(i, (i + 1) % devices) for i in range(dev...  82.8 us
    all_to_all x8, starting transfers between devices, exchange(): lax.all_to_all(value, 'fsdp', split_axis=0, concat_axis=0, tiled=True)  48.9 us
    pallas_call x4, Pallas kernels, attention(): pl.pallas_call(attention_kernel, out_shape=jax.ShapeDtypeStruct(rows.shap...  47.8 us
    ppermute x3, waiting for transfers between devices, gather_mix_weights(): other = lax.ppermute(held, 'fsdp', [(i, i ^ 1 << b) for i in range(size)])  36.5 us
    pallas_call x4, Pallas kernels, mix(): pl.pallas_call(mix_kernel, out_shape=jax.ShapeDtypeStruct(x.shape, BF), g...  21.4 us
    ppermute x3, starting transfers between devices, gather_mix_weights(): other = lax.ppermute(held, 'fsdp', [(i, i ^ 1 << b) for i in range(size)])  11.7 us
    unnamed x30, local copies, waits for them, and re-layouts  8.68 us
  transfers between devices with their start and end apart: 15, of which 13 were waited for; matrix products, arithmetic and copies ran while one was open for 1% of the time, Pallas kernels for 18%

profile of v1, /device:TPU:20, one launch (start us, length us, event | category | flops | bytes accessed | tf_op | source)
XLA Modules:
  0.0 426.9 jit_solution(14015799004700983910)
XLA Ops:
  5.7 12.5 %all-to-all-start.4 = ((bf16[8,64,512]{2,1,0:T(8,128)(2,1)}), bf16[8,64,512]{2,1,0:T(8,128)(2,1)S(1)}, u32[]{:S(2)}, u32[]{:S(2)}) async-start(bf16[8,64,512]{2,1,0:T(8,128)(2,1)} %norm.6), calls=%async_computation.4 | async-start | bytes 1048576 | tf_op jit(solution)/shard_map/all_to_all | solution.py:190
  20.4 26.6 %all-to-all-done.4.rows_ref = bf16[8,64,512]{2,1,0:T(8,128)(2,1)S(1)} async-done(((bf16[8,64,512]{2,1,0:T(8,128)(2,1)}), bf16[8,64,512]{2,1,0:T(8,128)(2,1)S(1)}, u32[]{:S(2)}, u32[]{:S(2)}) %all-to-all-start.4) | async-done | bytes 524320 | tf_op jit(solution)/shard_map/all_to_all | solution.py:190
  52.0 11.9 %attention.6 = bf16[8,64,512]{2,1,0:T(8,128)(2,1)} custom-call(s32[1]{0:T(128)} %bitcast.9.which, s32[32]{0:T(128)} %reshape_squeeze.6.ids, bf16[8,64,512]{2,1,0:T(8,128)(2,1)} %copy-done.8, bf16[2,4,128,128]{3,2,1,0:T(8,128)(2,1)} %bitcast.32, bf16[2,4,128,128]{3,2,1,0:T(8,128)(2,1)} %bitcast.36, bf16[2,4,128,128]{3,2,1,0:T(8,128)(2,1)} %bitcast.40), custom_call_target="tpu_custom_call" | custom-call | flops 603979776 | bytes 1441792 | tf_op jit(solution)/shard_map/attention/pallas_call | solution.py:80
  63.9 15.7 %all-to-all-done.rows_ref = bf16[8,64,512]{2,1,0:T(8,128)(2,1)S(1)} async-done(((bf16[8,64,512]{2,1,0:T(8,128)(2,1)}), bf16[8,64,512]{2,1,0:T(8,128)(2,1)S(1)}, u32[]{:S(2)}, u32[]{:S(2)}) %all-to-all-start) | async-done | bytes 524320 | tf_op jit(solution)/shard_map/all_to_all | solution.py:190
  84.6 12.0 %attention.4 = bf16[8,64,512]{2,1,0:T(8,128)(2,1)} custom-call(s32[1]{0:T(128)} %bitcast.2.which, s32[32]{0:T(128)} %reshape_squeeze.6.ids, bf16[8,64,512]{2,1,0:T(8,128)(2,1)} %copy-done.9, bf16[2,4,128,128]{3,2,1,0:T(8,128)(2,1)} %bitcast.33, bf16[2,4,128,128]{3,2,1,0:T(8,128)(2,1)} %bitcast.37, bf16[2,4,128,128]{3,2,1,0:T(8,128)(2,1)} %bitcast.41), custom_call_target="tpu_custom_call" | custom-call | flops 603979776 | bytes 1441792 | tf_op jit(solution)/shard_map/attention/pallas_call | solution.py:80
  96.6 16.0 %all-to-all-done.5.att_ref = bf16[8,64,512]{2,1,0:T(8,128)(2,1)S(1)} async-done(((bf16[8,64,512]{2,1,0:T(8,128)(2,1)}), bf16[8,64,512]{2,1,0:T(8,128)(2,1)S(1)}, u32[]{:S(2)}, u32[]{:S(2)}) %all-to-all-start.5) | async-done | bytes 524320 | tf_op jit(solution)/shard_map/all_to_all | solution.py:190
  117.9 7.8 %collective-permute-start = (bf16[1,2,16,1024]{3,2,1,0:T(8,128)(2,1)S(1)}, bf16[1,2,16,1024]{3,2,1,0:T(8,128)(2,1)S(1)}, u32[]{:S(2)}, u32[]{:S(2)}) collective-permute-start(bf16[1,2,16,1024]{3,2,1,0:T(8,128)(2,1)S(1)} %reshape_squeeze.7), channel_id=1, source_target_pairs={{0,4},{1,5},{2,6},{3,7},{4,0},{5,1},{6,2},{7,3},{8,12},{9,13},{10,... | collective-permute-start | bytes 196616 | tf_op jit(solution)/shard_map/ppermute | solution.py:113
  125.8 25.4 %collective-permute-done = bf16[1,2,16,1024]{3,2,1,0:T(8,128)(2,1)S(1)} collective-permute-done((bf16[1,2,16,1024]{3,2,1,0:T(8,128)(2,1)S(1)}, bf16[1,2,16,1024]{3,2,1,0:T(8,128)(2,1)S(1)}, u32[]{:S(2)}, u32[]{:S(2)}) %collective-permute-start) | collective-permute-done | bytes 65568 | tf_op jit(solution)/shard_map/ppermute | solution.py:113
  153.1 5.8 %collective-permute-done.1 = bf16[2,2,16,1024]{3,2,1,0:T(8,128)(2,1)S(1)} collective-permute-done((bf16[2,2,16,1024]{3,2,1,0:T(8,128)(2,1)S(1)}, bf16[2,2,16,1024]{3,2,1,0:T(8,128)(2,1)S(1)}, u32[]{:S(2)}, u32[]{:S(2)}) %collective-permute-start.1) | collective-permute-done | bytes 131104 | tf_op jit(solution)/shard_map/ppermute | solution.py:113
  171.2 5.4 %mix.6 = bf16[64,4096]{1,0:T(8,128)(2,1)} custom-call(s32[1]{0:T(128)} %bitcast.9.which, s32[2]{0:T(128)} %bitcast.28, bf16[8,64,512]{2,1,0:T(8,128)(2,1)} %copy-done.2, f32[2,1024,128]{2,1,0:T(8,128)} %mix_weights.1.w_ref, bf16[64,4096]{1,0:T(8,128)(2,1)} %get-tuple-element.8.x_ref), custom_call_target="tpu_custom_call" | custom-call | flops 16777216 | bytes 2097152 | tf_op jit(solution)/shard_map/mix/pallas_call | solution.py:166
  178.5 35.4 %collective-permute-done.5.x_ref = bf16[64,4096]{1,0:T(8,128)(2,1)S(1)} collective-permute-done((bf16[64,4096]{1,0:T(8,128)(2,1)}, bf16[64,4096]{1,0:T(8,128)(2,1)S(1)}, u32[]{:S(2)}, u32[]{:S(2)}) %collective-permute-start.5) | collective-permute-done | bytes 524320 | tf_op jit(solution)/shard_map/ppermute | solution.py:195
  217.6 5.6 %all-to-all-start.6 = ((bf16[8,64,512]{2,1,0:T(8,128)(2,1)}), bf16[8,64,512]{2,1,0:T(8,128)(2,1)S(1)}, u32[]{:S(2)}, u32[]{:S(2)}) async-start(bf16[8,64,512]{2,1,0:T(8,128)(2,1)} %norm.7), calls=%async_computation.6 | async-start | bytes 1048576 | tf_op jit(solution)/shard_map/all_to_all | solution.py:190
  223.1 5.4 %mix.4 = bf16[64,4096]{1,0:T(8,128)(2,1)} custom-call(s32[1]{0:T(128)} %bitcast.2.which, s32[2]{0:T(128)} %bitcast.29, bf16[8,64,512]{2,1,0:T(8,128)(2,1)} %copy-done.1, f32[2,1024,128]{2,1,0:T(8,128)} %mix_weights.1.w_ref, bf16[64,4096]{1,0:T(8,128)(2,1)} %get-tuple-element.7.x_ref), custom_call_target="tpu_custom_call" | custom-call | flops 16777216 | bytes 2097152 | tf_op jit(solution)/shard_map/mix/pallas_call | solution.py:166
  230.4 18.6 %collective-permute-done.3.x_ref = bf16[64,4096]{1,0:T(8,128)(2,1)S(1)} collective-permute-done((bf16[64,4096]{1,0:T(8,128)(2,1)}, bf16[64,4096]{1,0:T(8,128)(2,1)S(1)}, u32[]{:S(2)}, u32[]{:S(2)}) %collective-permute-start.3) | collective-permute-done | bytes 524320 | tf_op jit(solution)/shard_map/ppermute | solution.py:195
  252.0 16.6 %all-to-all-done.6.rows_ref = bf16[8,64,512]{2,1,0:T(8,128)(2,1)S(1)} async-done(((bf16[8,64,512]{2,1,0:T(8,128)(2,1)}), bf16[8,64,512]{2,1,0:T(8,128)(2,1)S(1)}, u32[]{:S(2)}, u32[]{:S(2)}) %all-to-all-start.6) | async-done | bytes 524320 | tf_op jit(solution)/shard_map/all_to_all | solution.py:190
  269.3 9.5 %all-to-all-start.2 = ((bf16[8,64,512]{2,1,0:T(8,128)(2,1)}), bf16[8,64,512]{2,1,0:T(8,128)(2,1)S(1)}, u32[]{:S(2)}, u32[]{:S(2)}) async-start(bf16[8,64,512]{2,1,0:T(8,128)(2,1)} %norm.5), calls=%async_computation.2 | async-start | bytes 1048576 | tf_op jit(solution)/shard_map/all_to_all | solution.py:190
  278.8 11.9 %attention.7 = bf16[8,64,512]{2,1,0:T(8,128)(2,1)} custom-call(s32[1]{0:T(128)} %bitcast.8.which, s32[32]{0:T(128)} %reshape_squeeze.6.ids, bf16[8,64,512]{2,1,0:T(8,128)(2,1)} %copy-done.7, bf16[2,4,128,128]{3,2,1,0:T(8,128)(2,1)} %bitcast.34, bf16[2,4,128,128]{3,2,1,0:T(8,128)(2,1)} %bitcast.38, bf16[2,4,128,128]{3,2,1,0:T(8,128)(2,1)} %bitcast.42), custom_call_target="tpu_custom_call" | custom-call | flops 603979776 | bytes 1441792 | tf_op jit(solution)/shard_map/attention/pallas_call | solution.py:80
  290.8 11.0 %all-to-all-done.2.rows_ref = bf16[8,64,512]{2,1,0:T(8,128)(2,1)S(1)} async-done(((bf16[8,64,512]{2,1,0:T(8,128)(2,1)}), bf16[8,64,512]{2,1,0:T(8,128)(2,1)S(1)}, u32[]{:S(2)}, u32[]{:S(2)}) %all-to-all-start.2) | async-done | bytes 524320 | tf_op jit(solution)/shard_map/all_to_all | solution.py:190
  306.8 11.9 %attention.5 = bf16[8,64,512]{2,1,0:T(8,128)(2,1)} custom-call(s32[1]{0:T(128)} %bitcast.which, s32[32]{0:T(128)} %reshape_squeeze.6.ids, bf16[8,64,512]{2,1,0:T(8,128)(2,1)} %copy-done.10, bf16[2,4,128,128]{3,2,1,0:T(8,128)(2,1)} %bitcast.35, bf16[2,4,128,128]{3,2,1,0:T(8,128)(2,1)} %bitcast.39, bf16[2,4,128,128]{3,2,1,0:T(8,128)(2,1)} %bitcast.43), custom_call_target="tpu_custom_call" | custom-call | flops 603979776 | bytes 1441792 | tf_op jit(solution)/shard_map/attention/pallas_call | solution.py:80
  318.8 14.5 %all-to-all-done.7.att_ref = bf16[8,64,512]{2,1,0:T(8,128)(2,1)S(1)} async-done(((bf16[8,64,512]{2,1,0:T(8,128)(2,1)}), bf16[8,64,512]{2,1,0:T(8,128)(2,1)S(1)}, u32[]{:S(2)}, u32[]{:S(2)}) %all-to-all-start.7) | async-done | bytes 524320 | tf_op jit(solution)/shard_map/all_to_all | solution.py:190
  338.4 5.4 %mix.7 = bf16[64,4096]{1,0:T(8,128)(2,1)} custom-call(s32[1]{0:T(128)} %bitcast.8.which, s32[2]{0:T(128)} %bitcast.30, bf16[8,64,512]{2,1,0:T(8,128)(2,1)} %copy-done.4, f32[2,1024,128]{2,1,0:T(8,128)} %mix_weights.1.w_ref, bf16[64,4096]{1,0:T(8,128)(2,1)} %copy-done.5), custom_call_target="tpu_custom_call" | custom-call | flops 16777216 | bytes 2097152 | tf_op jit(solution)/shard_map/mix/pallas_call | solution.py:166
  345.6 43.1 %all-to-all-done.3.att_ref = bf16[8,64,512]{2,1,0:T(8,128)(2,1)S(1)} async-done(((bf16[8,64,512]{2,1,0:T(8,128)(2,1)}), bf16[8,64,512]{2,1,0:T(8,128)(2,1)S(1)}, u32[]{:S(2)}, u32[]{:S(2)}) %all-to-all-start.3) | async-done | bytes 524320 | tf_op jit(solution)/shard_map/all_to_all | solution.py:190
  389.6 5.4 %mix.5 = bf16[64,4096]{1,0:T(8,128)(2,1)} custom-call(s32[1]{0:T(128)} %bitcast.which, s32[2]{0:T(128)} %bitcast.31, bf16[8,64,512]{2,1,0:T(8,128)(2,1)} %copy-done.3, f32[2,1024,128]{2,1,0:T(8,128)} %mix_weights.1.w_ref, bf16[64,4096]{1,0:T(8,128)(2,1)} %copy-done.6), custom_call_target="tpu_custom_call" | custom-call | flops 16777216 | bytes 2097152 | tf_op jit(solution)/shard_map/mix/pallas_call | solution.py:166
  396.9 28.8 %collective-permute-done.4 = bf16[64,4096]{1,0:T(8,128)(2,1)S(1)} collective-permute-done((bf16[64,4096]{1,0:T(8,128)(2,1)}, bf16[64,4096]{1,0:T(8,128)(2,1)S(1)}, u32[]{:S(2)}, u32[]{:S(2)}) %collective-permute-start.4) | collective-permute-done | bytes 524320 | tf_op jit(solution)/shard_map/ppermute | solution.py:195
  (60 shorter events, 64.4 us)
Async XLA Ops:
  5.7 41.3 %all-to-all-start.4 = ((bf16[8,64,512]{2,1,0:T(8,128)(2,1)}), bf16[8,64,512]{2,1,0:T(8,128)(2,1)S(1)}, u32[]{:S(2)}, u32[]{:S(2)}) async-start(bf16[8,64,512]{2,1,0:T(8,128)(2,1)} %norm.6), calls=%async_computation.4 | async-start | bytes 1048576 | tf_op jit(solution)/shard_map/all_to_all | solution.py:190
  20.4 30.9 %copy-start.13 = (s32[2,1,8,2]{2,3,1,0:T(2,128)S(1)}, s32[2,1,8,2]{2,3,1,0:T(2,128)}, u32[]{:S(2)}) copy-start(s32[2,1,8,2]{2,3,1,0:T(2,128)} %param.16) | copy-start | bytes 388
  47.0 4.4 %copy-start.8 = (bf16[8,64,512]{2,1,0:T(8,128)(2,1)}, bf16[8,64,512]{2,1,0:T(8,128)(2,1)S(1)}, u32[]{:S(2)}) copy-start(bf16[8,64,512]{2,1,0:T(8,128)(2,1)S(1)} %all-to-all-done.4.rows_ref) | copy-start | bytes 1572868
  47.0 32.6 %all-to-all-start = ((bf16[8,64,512]{2,1,0:T(8,128)(2,1)}), bf16[8,64,512]{2,1,0:T(8,128)(2,1)S(1)}, u32[]{:S(2)}, u32[]{:S(2)}) async-start(bf16[8,64,512]{2,1,0:T(8,128)(2,1)} %norm.4), calls=%async_computation | async-start | bytes 1048576 | tf_op jit(solution)/shard_map/all_to_all | solution.py:190
  80.4 32.2 %all-to-all-start.5 = ((bf16[8,64,512]{2,1,0:T(8,128)(2,1)}), bf16[8,64,512]{2,1,0:T(8,128)(2,1)S(1)}, u32[]{:S(2)}, u32[]{:S(2)}) async-start(bf16[8,64,512]{2,1,0:T(8,128)(2,1)} %attention.6), calls=%async_computation.5 | async-start | bytes 1048576 | tf_op jit(solution)/shard_map/all_to_all | solution.py:190
  96.6 21.1 %copy-start.11 = (bf16[2,1,16,32,32]{4,3,2,1,0:T(8,128)(2,1)S(1)}, bf16[2,1,16,32,32]{4,3,2,1,0:T(8,128)(2,1)}, u32[]{:S(2)}) copy-start(bf16[2,1,16,32,32]{4,3,2,1,0:T(8,128)(2,1)} %param.14) | copy-start | bytes 196612
  112.6 0.8 copy-start.2
  113.4 103.4 %all-to-all-start.1 = ((bf16[8,64,512]{2,1,0:T(8,128)(2,1)}), bf16[8,64,512]{2,1,0:T(8,128)(2,1)S(1)}, u32[]{:S(2)}, u32[]{:S(2)}) async-start(bf16[8,64,512]{2,1,0:T(8,128)(2,1)} %attention.4), calls=%async_computation.1 | async-start | bytes 1048576 | tf_op jit(solution)/shard_map/all_to_all | solution.py:190
  117.9 33.3 %collective-permute-start = (bf16[1,2,16,1024]{3,2,1,0:T(8,128)(2,1)S(1)}, bf16[1,2,16,1024]{3,2,1,0:T(8,128)(2,1)S(1)}, u32[]{:S(2)}, u32[]{:S(2)}) collective-permute-start(bf16[1,2,16,1024]{3,2,1,0:T(8,128)(2,1)S(1)} %reshape_squeeze.7), channel_id=1, source_target_pairs={{0,4},{1,5},{2,6},{3,7},{4,0},{5,1},{6,2},{7,3},{8,12},{9,13},{10,... | collective-permute-start | bytes 196616 | tf_op jit(solution)/shard_map/ppermute | solution.py:113
  151.2 7.8 %collective-permute-start.1 = (bf16[2,2,16,1024]{3,2,1,0:T(8,128)(2,1)S(1)}, bf16[2,2,16,1024]{3,2,1,0:T(8,128)(2,1)S(1)}, u32[]{:S(2)}, u32[]{:S(2)}) collective-permute-start(bf16[2,2,16,1024]{3,2,1,0:T(8,128)(2,1)S(1)} %pad_maximum_fusion.2), channel_id=1, source_target_pairs={{0,2},{1,3},{2,0},{3,1},{4,6},{5,7},{6,4},{7,5},{8,10},{9,11},{10,... | collective-permute-start | bytes 393224 | tf_op jit(solution)/shard_map/ppermute | solution.py:113
  159.0 2.0 copy-start
  159.0 8.4 %collective-permute-start.2 = (bf16[4,2,16,1024]{3,2,1,0:T(8,128)(2,1)S(1)}, bf16[4,2,16,1024]{3,2,1,0:T(8,128)(2,1)S(1)}, u32[]{:S(2)}, u32[]{:S(2)}) collective-permute-start(bf16[4,2,16,1024]{3,2,1,0:T(8,128)(2,1)S(1)} %pad_maximum_fusion.1), channel_id=1, source_target_pairs={{0,1},{1,0},{2,3},{3,2},{4,5},{5,4},{6,7},{7,6},{8,9},{9,8},{10,11... | collective-permute-start | bytes 786440 | tf_op jit(solution)/shard_map/ppermute | solution.py:113
  176.5 37.3 %collective-permute-start.5 = (bf16[64,4096]{1,0:T(8,128)(2,1)}, bf16[64,4096]{1,0:T(8,128)(2,1)S(1)}, u32[]{:S(2)}, u32[]{:S(2)}) collective-permute-start(bf16[64,4096]{1,0:T(8,128)(2,1)} %mix.6), channel_id=1, source_target_pairs={{0,8},{8,16},{16,24},{24,32},{32,40},{40,48},{48,56},{56,64},{64,7... | collective-permute-start | bytes 1572872 | tf_op jit(solution)/shard_map/ppermute | solution.py:195
  216.7 0.8 copy-start.1
  217.6 51.0 %all-to-all-start.6 = ((bf16[8,64,512]{2,1,0:T(8,128)(2,1)}), bf16[8,64,512]{2,1,0:T(8,128)(2,1)S(1)}, u32[]{:S(2)}, u32[]{:S(2)}) async-start(bf16[8,64,512]{2,1,0:T(8,128)(2,1)} %norm.7), calls=%async_computation.6 | async-start | bytes 1048576 | tf_op jit(solution)/shard_map/all_to_all | solution.py:190
  228.5 20.6 %collective-permute-start.3 = (bf16[64,4096]{1,0:T(8,128)(2,1)}, bf16[64,4096]{1,0:T(8,128)(2,1)S(1)}, u32[]{:S(2)}, u32[]{:S(2)}) collective-permute-start(bf16[64,4096]{1,0:T(8,128)(2,1)} %mix.4), channel_id=1, source_target_pairs={{0,8},{8,16},{16,24},{24,32},{32,40},{40,48},{48,56},{56,64},{64,7... | collective-permute-start | bytes 1572872 | tf_op jit(solution)/shard_map/ppermute | solution.py:195
  268.5 0.8 copy-start.7
  269.3 32.4 %all-to-all-start.2 = ((bf16[8,64,512]{2,1,0:T(8,128)(2,1)}), bf16[8,64,512]{2,1,0:T(8,128)(2,1)S(1)}, u32[]{:S(2)}, u32[]{:S(2)}) async-start(bf16[8,64,512]{2,1,0:T(8,128)(2,1)} %norm.5), calls=%async_computation.2 | async-start | bytes 1048576 | tf_op jit(solution)/shard_map/all_to_all | solution.py:190
  301.7 0.8 copy-start.10
  302.6 30.7 %all-to-all-start.7 = ((bf16[8,64,512]{2,1,0:T(8,128)(2,1)}), bf16[8,64,512]{2,1,0:T(8,128)(2,1)S(1)}, u32[]{:S(2)}, u32[]{:S(2)}) async-start(bf16[8,64,512]{2,1,0:T(8,128)(2,1)} %attention.7), calls=%async_computation.7 | async-start | bytes 1048576 | tf_op jit(solution)/shard_map/all_to_all | solution.py:190
  333.3 0.8 copy-start.4
  334.1 54.7 %all-to-all-start.3 = ((bf16[8,64,512]{2,1,0:T(8,128)(2,1)}), bf16[8,64,512]{2,1,0:T(8,128)(2,1)S(1)}, u32[]{:S(2)}, u32[]{:S(2)}) async-start(bf16[8,64,512]{2,1,0:T(8,128)(2,1)} %attention.5), calls=%async_computation.3 | async-start | bytes 1048576 | tf_op jit(solution)/shard_map/all_to_all | solution.py:190
  343.7 53.1 %collective-permute-start.6 = (bf16[64,4096]{1,0:T(8,128)(2,1)}, bf16[64,4096]{1,0:T(8,128)(2,1)S(1)}, u32[]{:S(2)}, u32[]{:S(2)}) collective-permute-start(bf16[64,4096]{1,0:T(8,128)(2,1)} %mix.7), channel_id=1, source_target_pairs={{0,8},{8,16},{16,24},{24,32},{32,40},{40,48},{48,56},{56,64},{64,7... | collective-permute-start | bytes 1572872 | tf_op jit(solution)/shard_map/ppermute | solution.py:195
  395.0 30.8 %collective-permute-start.4 = (bf16[64,4096]{1,0:T(8,128)(2,1)}, bf16[64,4096]{1,0:T(8,128)(2,1)S(1)}, u32[]{:S(2)}, u32[]{:S(2)}) collective-permute-start(bf16[64,4096]{1,0:T(8,128)(2,1)} %mix.5), channel_id=1, source_target_pairs={{0,8},{8,16},{16,24},{24,32},{32,40},{40,48},{48,56},{56,64},{64,7... | collective-permute-start | bytes 1572872 | tf_op jit(solution)/shard_map/ppermute | solution.py:195
  (5 other events, 3.9 us)

commit v2 on v1

v2 whole, which is shorter than its diff:
```python
import jax
import jax.numpy as jnp
from jax import lax
from jax.experimental import pallas as pl
from jax.experimental.pallas import tpu as pltpu
from jax.sharding import PartitionSpec as P

BLK = 64
EPS = 1e-05
BF = jnp.bfloat16
F32 = jnp.float32
EARLY = 2


def norm_kernel(which, x_ref, gain_ref, out_ref):
    groups, rows, width = out_ref.shape
    for start in range(0, rows, 16):
        wide = x_ref[start : start + 16, :].astype(F32)
        mean_sq = jnp.mean(wide * wide, axis=1, keepdims=True)
        normed = wide * lax.rsqrt(mean_sq + EPS) * gain_ref[0].astype(F32)
        normed = normed.astype(BF)
        for group in range(groups):
            out_ref[group, start : start + 16, :] = normed[:, group * width : (group + 1) * width]


def norm(which, x, gain, groups):
    slots, rows, features = x.shape
    width = features // groups
    return pl.pallas_call(
        norm_kernel,
        out_shape=jax.ShapeDtypeStruct((groups, slots, rows, width), BF),
        grid_spec=pltpu.PrefetchScalarGridSpec(
            num_scalar_prefetch=1,
            grid=(slots,),
            in_specs=[
                pl.BlockSpec((None, rows, features), lambda k, which: (k, 0, 0)),
                pl.BlockSpec((1, 1, features), lambda k, which: (which[k], 0, 0)),
            ],
            out_specs=pl.BlockSpec((groups, None, rows, width), lambda k, which: (0, k, 0, 0)),
        ),
        cost_estimate=pl.CostEstimate(
            flops=slots * rows * features * 6,
            bytes_accessed=slots * rows * features * 4,
            transcendentals=slots * rows,
        ),
        name="norm",
    )(which, x, gain)


def attend(wq, wk, wv, rows_ref, s_ref, p_ref, block, ids, base):
    keys = s_ref.shape[1]
    width = rows_ref.shape[1]
    count = keys // block
    picks = ids.shape[0] // (2 * count)
    rows = rows_ref[...]
    query = jnp.dot(rows, wq, preferred_element_type=F32)
    query = (query * width ** (-0.5)).astype(BF)
    key = jnp.dot(rows, wk, preferred_element_type=F32).astype(BF)
    value = jnp.dot(rows, wv, preferred_element_type=F32).astype(BF)
    s_ref[...] = lax.dot_general(query, key, (((1,), (1,)), ((), ())), preferred_element_type=F32)
    listed = lax.broadcasted_iota(jnp.int32, (8, keys), 1) // block
    totals = []
    for i in range(count):
        times = jnp.zeros((8, keys), F32)
        near = [(i - 1) % count, i, (i + 1) % count, 0]
        for b in near + [ids[base + i * picks + r] for r in range(picks)]:
            times = times + (listed == b).astype(F32)
        times = times[:1]
        at = slice(i * block, (i + 1) * block)
        scores = jnp.where(times > 0, s_ref[at, :], -jnp.inf)
        powers = jnp.exp(scores - jnp.max(scores, axis=1, keepdims=True)) * times
        totals.append(jnp.sum(powers, axis=1, keepdims=True))
        p_ref[at, :] = powers.astype(BF)
    mixed = jnp.dot(p_ref[...], value, preferred_element_type=F32)
    return (mixed / jnp.concatenate(totals, axis=0)).astype(BF)


def attention_kernel(which, ids, in_ref, wq_ref, wk_ref, wv_ref, out_ref, *scratch):
    rows_ref = scratch[0]
    count, block, width = in_ref.shape
    rows_ref[...] = in_ref[...].reshape(count * block, width)
    base = which[pl.program_id(0)] * (ids.shape[0] // 2)
    mixed = attend(wq_ref[...], wk_ref[...], wv_ref[...], *scratch, block, ids, base)
    out_ref[...] = mixed.reshape(count, block, width)


def attention_scratch(rows, width):
    return [pltpu.VMEM((rows, width), BF), pltpu.VMEM((rows, rows), F32), pltpu.VMEM((rows, rows), BF)]


def attention_cost(slots, heads, count, block, width):
    return pl.CostEstimate(
        flops=slots * heads * count * block * width * (6 * width + 4 * 6 * block),
        bytes_accessed=slots * heads * (count * block * width * 4 + width * width * 6),
        transcendentals=slots * heads * count * block * 6 * block,
    )


def attention(which, ids, rows, wq, wk, wv):
    count, slots, block, features = rows.shape
    heads, width = wq.shape[1], wq.shape[2]
    weight_spec = pl.BlockSpec(
        (None, None, width, width), lambda k, h, which, ids: (which[k], h, 0, 0)
    )
    row_spec = pl.BlockSpec((count, None, block, width), lambda k, h, which, ids: (0, k, 0, h))
    return pl.pallas_call(
        attention_kernel,
        out_shape=jax.ShapeDtypeStruct(rows.shape, BF),
        grid_spec=pltpu.PrefetchScalarGridSpec(
            num_scalar_prefetch=2,
            grid=(slots, heads),
            in_specs=[row_spec, weight_spec, weight_spec, weight_spec],
            out_specs=row_spec,
            scratch_shapes=attention_scratch(count * block, width),
        ),
        cost_estimate=attention_cost(slots, heads, count, block, width),
        name="attention",
    )(which, ids, rows, wq, wk, wv)


def mix_weights_kernel(place, gathered_ref, out_ref):
    groups = gathered_ref.shape[0]
    for v in range(out_ref.shape[0]):
        rows = jnp.concatenate([gathered_ref[place[j], v] for j in range(groups)], axis=0)
        out_ref[v] = rows.astype(F32).T


def partner(value, bit):
    size = lax.axis_size("fsdp")
    other = lax.ppermute(value, "fsdp", [(i, i ^ bit) for i in range(size)])
    return jnp.concatenate([value, other], axis=0)


def gathered_place(bits):
    order = [0]
    for bit in bits:
        order = order + [o ^ bit for o in order]
    back = [0] * len(order)
    for position, o in enumerate(order):
        back[o] = position
    me = lax.axis_index("fsdp")
    return jnp.array(back, jnp.int32)[jnp.arange(len(order), dtype=jnp.int32) ^ me]


def mix_weights(place, held):
    size, layers, mine, pairs = held.shape
    return pl.pallas_call(
        mix_weights_kernel,
        out_shape=jax.ShapeDtypeStruct((layers, pairs, mine * size), F32),
        grid_spec=pltpu.PrefetchScalarGridSpec(
            num_scalar_prefetch=1,
            grid=(1,),
            in_specs=[pl.BlockSpec(held.shape, lambda i, place: (0, 0, 0, 0))],
            out_specs=pl.BlockSpec((layers, pairs, mine * size), lambda i, place: (0, 0, 0)),
        ),
        name="mix_weights",
    )(place, held)


def mix_totals(wide_ref, w_ref, i, step):
    heads, rows, width = wide_ref.shape
    totals = [jnp.zeros((rows, width), F32) for _ in range(step)]
    for h in range(heads):
        attended = wide_ref[h]
        for k in range(step):
            row = w_ref[0, pl.ds(h * heads + i * step + k, 1), :]
            totals[k] = totals[k] + attended * row
    return [total.astype(BF).astype(F32) for total in totals]


def mix_send_kernel(which, me, att_ref, w_ref, x_ref, *refs):
    out_refs, (wide_ref, state_ref) = refs[:-2], refs[-2:]
    groups, rows, features = att_ref.shape
    width = w_ref.shape[2]
    per = features // width
    heads = groups * per
    tile = out_refs[0].shape[1]
    tiles = rows // tile
    for h in range(heads):
        lanes = pl.ds(h % per * width, width)
        wide_ref[h] = att_ref[h // per, :, lanes].astype(F32)
    step = 4

    def body(i, squares):
        totals = mix_totals(wide_ref, w_ref, i, step)
        for k in range(step):
            g = i * step + k
            lanes = pl.ds(pl.multiple_of(g * width, width), width)
            updated = (x_ref[:, lanes].astype(F32) + totals[k]).astype(BF)
            state_ref[g] = updated
            wide = updated.astype(F32)
            squares = squares + wide * wide
        return squares

    squares = lax.fori_loop(0, heads // step, body, jnp.zeros((rows, width), F32))
    mean_sq = jnp.sum(squares, axis=1, keepdims=True) / (heads * width)
    scale = lax.rsqrt(mean_sq + EPS)
    lane = lax.broadcasted_iota(jnp.int32, (tile, width), 1)
    packed = jnp.zeros((tile, width), F32)
    for t in range(tiles):
        rest = scale[t * tile : (t + 1) * tile]
        for term in range(3):
            top = rest.astype(BF).astype(F32)
            packed = jnp.where(lane == t * 4 + term, top, packed)
            rest = rest - top
    packed = packed.astype(BF)
    for r, out_ref in enumerate(out_refs):
        group = me[0] ^ r
        for h in range(per):
            out_ref[h * tiles : (h + 1) * tiles] = state_ref[group * per + h].reshape(
                tiles, tile, width
            )
        out_ref[per * tiles] = packed


def mix_cost(slots, rows, features, pairs, width):
    return pl.CostEstimate(
        flops=slots * rows * pairs * width * 2,
        bytes_accessed=slots * (rows * features * 6 + pairs * width * 4),
        transcendentals=0,
    )


def mix_send(which, me, attended, weights, x):
    slots, rows, features = x.shape
    groups = attended.shape[0]
    pairs, width = weights.shape[1:]
    tile = 16
    share = features // groups
    block = (rows // tile * (share // width) + 1, tile, width)
    heads = features // width
    return pl.pallas_call(
        mix_send_kernel,
        out_shape=[jax.ShapeDtypeStruct((slots, *block), BF)] * groups,
        grid_spec=pltpu.PrefetchScalarGridSpec(
            num_scalar_prefetch=2,
            grid=(slots,),
            in_specs=[
                pl.BlockSpec((groups, None, rows, share), lambda k, which, me: (0, k, 0, 0)),
                pl.BlockSpec((1, pairs, width), lambda k, which, me: (which[k], 0, 0)),
                pl.BlockSpec((None, rows, features), lambda k, which, me: (k, 0, 0)),
            ],
            out_specs=[pl.BlockSpec((None, *block), lambda k, which, me: (k, 0, 0, 0))] * groups,
            scratch_shapes=[
                pltpu.VMEM((heads, rows, width), F32),
                pltpu.VMEM((heads, rows, width), BF),
            ],
        ),
        cost_estimate=mix_cost(slots, rows, features, pairs, width),
        name="mix_send",
    )(which, me, attended, weights, x)


def attention_send_kernel(which, me, ids, *refs):
    size = (len(refs) - 7) // 2
    in_refs, rest = refs[:size], refs[size:]
    gain_ref, wq_ref, wk_ref, wv_ref = rest[:4]
    out_refs, scratch = rest[4:-3], rest[-3:]
    rows_ref = scratch[0]
    slot, head = pl.program_id(0), pl.program_id(1)
    block, width = out_refs[0].shape
    tile = in_refs[0].shape[1]
    tiles = block // tile
    gain = gain_ref[0].astype(F32)
    for k, ref in enumerate(in_refs):
        start = pl.multiple_of((me[0] ^ k) * block, block)
        rows = ref[pl.ds(head * tiles, tiles)].reshape(block, width)
        packed = ref[ref.shape[0] - 1].astype(F32)
        scale = jnp.concatenate(
            [
                packed[:, 4 * t : 4 * t + 1]
                + packed[:, 4 * t + 1 : 4 * t + 2]
                + packed[:, 4 * t + 2 : 4 * t + 3]
                for t in range(tiles)
            ],
            axis=0,
        )
        rows_ref[pl.ds(start, block), :] = (rows.astype(F32) * scale * gain).astype(BF)
    base = which[slot] * (ids.shape[0] // 2)
    mixed = attend(wq_ref[...], wk_ref[...], wv_ref[...], *scratch, block, ids, base)
    rows_ref[...] = mixed
    for k, out_ref in enumerate(out_refs):
        start = pl.multiple_of((me[0] ^ k) * block, block)
        out_ref[...] = rows_ref[pl.ds(start, block), :]


def attention_send(which, me, ids, blocks, gain, wq, wk, wv):
    size = len(blocks)
    slots = blocks[0].shape[0]
    heads, width = wq.shape[1], wq.shape[2]
    weight_spec = pl.BlockSpec(
        (None, None, width, width), lambda k, h, which, me, ids: (which[k], h, 0, 0)
    )
    block_spec = pl.BlockSpec(
        (None, *blocks[0].shape[1:]), lambda k, h, which, me, ids: (k, 0, 0, 0)
    )
    return pl.pallas_call(
        attention_send_kernel,
        out_shape=[jax.ShapeDtypeStruct((slots, heads, BLK, width), BF)] * size,
        grid_spec=pltpu.PrefetchScalarGridSpec(
            num_scalar_prefetch=3,
            grid=(slots, heads),
            in_specs=[block_spec] * size
            + [
                pl.BlockSpec(
                    (1, 1, width),
                    lambda k, h, which, me, ids: (which[k], 0, me[0] * heads + h),
                ),
                weight_spec,
                weight_spec,
                weight_spec,
            ],
            out_specs=[
                pl.BlockSpec((None, None, BLK, width), lambda k, h, which, me, ids: (k, h, 0, 0))
            ]
            * size,
            scratch_shapes=attention_scratch(size * BLK, width),
        ),
        cost_estimate=attention_cost(slots, heads, size, BLK, width),
        name="attention_send",
    )(which, me, ids, *blocks, gain, wq, wk, wv)


def mix_final_kernel(which, me, target, *refs):
    size = (len(refs) - 4) // 2
    att_refs, x_refs, w_ref = refs[:size], refs[size : 2 * size], refs[2 * size]
    out_ref, wide_ref, state_ref = refs[-3:]
    heads, rows, width = wide_ref.shape
    per = att_refs[0].shape[0]
    tile = x_refs[0].shape[1]
    tiles = rows // tile
    for k in range(size):
        group = me[0] ^ k
        for h in range(per):
            wide_ref[group * per + h] = att_refs[k][h].astype(F32)
            state = x_refs[k][h * tiles : (h + 1) * tiles]
            state_ref[group * per + h] = state.reshape(rows, width)
    step = 4

    def body(i, carry):
        totals = mix_totals(wide_ref, w_ref, i, step)
        for k in range(step):
            g = i * step + k
            lanes = pl.ds(pl.multiple_of(g * width, width), width)
            out_ref[:, lanes] = (state_ref[g].astype(F32) + totals[k]).astype(BF)
        return carry

    lax.fori_loop(0, heads // step, body, 0)


def mix_final(which, me, target, attended, states, weights):
    size = len(attended)
    slots, per, rows, width = attended[0].shape
    heads = size * per
    pairs = weights.shape[1]
    return pl.pallas_call(
        mix_final_kernel,
        out_shape=jax.ShapeDtypeStruct((slots, rows, heads * width), BF),
        grid_spec=pltpu.PrefetchScalarGridSpec(
            num_scalar_prefetch=3,
            grid=(slots,),
            in_specs=[
                pl.BlockSpec((None, *array.shape[1:]), lambda k, which, me, target: (k, 0, 0, 0))
                for array in [*attended, *states]
            ]
            + [pl.BlockSpec((1, pairs, width), lambda k, which, me, target: (which[k], 0, 0))],
            out_specs=pl.BlockSpec(
                (None, rows, heads * width), lambda k, which, me, target: (target[k], 0, 0)
            ),
            scratch_shapes=[
                pltpu.VMEM((heads, rows, width), F32),
                pltpu.VMEM((heads, rows, width), BF),
            ],
        ),
        cost_estimate=mix_cost(slots, rows, heads * width, pairs, width),
        name="mix_final",
    )(which, me, target, *attended, *states, weights)


def exchange(value):
    return lax.all_to_all(value, "fsdp", split_axis=0, concat_axis=0, tiled=True)


def send_on(blocks):
    segments, size = lax.axis_size("segment"), lax.axis_size("fsdp")
    arrived = []
    for k, block in enumerate(blocks):
        pairs = []
        for s in range(segments):
            for f in range(size):
                pairs.append((s * size + f, (s + 1) % segments * size + (f ^ k)))
        arrived.append(lax.ppermute(block, ("segment", "fsdp"), pairs))
    return arrived


def shifted(value):
    devices = lax.axis_size("segment")
    return lax.ppermute(value, "segment", [(i, (i + 1) % devices) for i in range(devices)])


def tie(value, *others):
    return lax.optimization_barrier((value, *others))[0]


def shards(stream, gain, w_query, w_key, w_value, w_mix, active, random_blocks):
    segments = lax.axis_size("segment")
    segment = lax.axis_index("segment")
    size = lax.axis_size("fsdp")
    slots = stream.shape[0]
    me = lax.axis_index("fsdp").astype(jnp.int32).reshape(1)
    wq, wk, wv = w_query[:, 0], w_key[:, 0], w_value[:, 0]
    ids = random_blocks[:, 0].reshape(-1)
    whole = stream[:, 0]

    def layers_of(place, turn):
        turned = jnp.where(place < turn, 1, 0)
        return ((jnp.arange(slots, dtype=jnp.int32) + turned) % slots).astype(jnp.int32)

    first = layers_of(segment, 0)
    second = layers_of(segment, 1)
    mixing = layers_of((segment + segments - 1) % segments, 1)
    target = layers_of(segment, 2)

    live = (active[:, 0] > 0)[:, None, None, None]
    masked = jnp.where(live, w_mix[:, 0], jnp.zeros_like(w_mix[:, 0]))
    masked = masked.reshape(1, slots, masked.shape[1], -1)
    bits = [1 << b for b in reversed(range(size.bit_length() - 1))]
    place = gathered_place(bits)

    own = partner(masked, bits[0])
    left = shifted(masked)
    normed = norm(first, whole, gain, size)
    own = partner(own, bits[1])
    rows = exchange(tie(normed, own, left))
    own = partner(tie(own, rows), bits[2])
    left = partner(tie(left, rows), bits[0])
    attended = attention(first, ids, rows, wq, wk, wv)
    back = exchange(tie(attended, own, left))
    own = mix_weights(place, own)
    left = partner(tie(left, back), bits[1])
    sent = mix_send(first, me, back, own, whole)
    sent = list(lax.optimization_barrier((*sent, left))[:-1])
    here = send_on(sent)
    onward = send_on(here)
    left = partner(tie(left, *here), bits[2])
    ready = lax.optimization_barrier((*here, *onward[:EARLY]))[: len(here)]
    attended = attention_send(second, me, ids, ready, gain, wq, wk, wv)
    last = send_on(lax.optimization_barrier((*attended, left))[:-1])
    left = mix_weights(place, left)
    done = mix_final(mixing, me, target, last, onward, left)
    return done[:, None]


def solution(mesh):
    in_specs = (
        P(None, "segment", "fsdp", None),
        P(None, "segment", None),
        P(None, "segment", "fsdp", None, None),
        P(None, "segment", "fsdp", None, None),
        P(None, "segment", "fsdp", None, None),
        P(None, "segment", "fsdp", None, None),
        P(None, "segment"),
        P(None, "segment", None, None),
    )
    out_specs = P(None, "segment", "fsdp", None)
    return jax.shard_map(shards, mesh=mesh, in_specs=in_specs, out_specs=out_specs, check_vma=False)
```

time: 428 us -> 384 us (0.90)
  the two profiles are of different devices: /device:TPU:20 before, /device:TPU:32 now
where the time goes in v2:
time: 384 us; the launch traced here: 382 us
  starting transfers between devices  173 us (45%)
  waiting for transfers between devices  146 us (38%)
  Pallas kernels  53.5 us (14%)
  local copies, waits for them, and re-layouts  5.41 us (1%)
    ppermute x24, starting transfers between devices, send_on(): arrived.append(lax.ppermute(block, ('segment', 'fsdp'), pairs))  128 us
    all_to_all x2, waiting for transfers between devices, exchange(): lax.all_to_all(value, 'fsdp', split_axis=0, concat_axis=0, tiled=True)  85.2 us
    ppermute x24, waiting for transfers between devices, send_on(): arrived.append(lax.ppermute(block, ('segment', 'fsdp'), pairs))  43.1 us
    ppermute x6, starting transfers between devices, partner(): other = lax.ppermute(value, 'fsdp', [(i, i ^ bit) for i in range(size)])  24.2 us
    all_to_all x2, starting transfers between devices, exchange(): lax.all_to_all(value, 'fsdp', split_axis=0, concat_axis=0, tiled=True)  19.1 us
    pallas_call x1, Pallas kernels, attention_send(): pl.pallas_call(attention_send_kernel, out_shape=[jax.ShapeDtypeStruct((sl...  15 us
    ppermute x1, waiting for transfers between devices, shifted(): lax.ppermute(value, 'segment', [(i, (i + 1) % devices) for i in range(dev...  12.9 us
    pallas_call x1, Pallas kernels, attention(): pl.pallas_call(attention_kernel, out_shape=jax.ShapeDtypeStruct(rows.shap...  12.3 us
  transfers between devices with their start and end apart: 33, of which 13 were waited for; matrix products, arithmetic and copies ran while one was open for 1% of the time, Pallas kernels for 12%

profile of v2, /device:TPU:32, one launch (start us, length us, event | category | flops | bytes accessed | tf_op | source)
XLA Modules:
  0.0 382.2 jit_solution(2042226219630774011)
XLA Ops:
  2.0 9.1 %collective-permute-start = (bf16[1,2,16,1024]{3,2,1,0:T(8,128)(2,1)S(1)}, bf16[1,2,16,1024]{3,2,1,0:T(8,128)(2,1)S(1)}, u32[]{:S(2)}, u32[]{:S(2)}) collective-permute-start(bf16[1,2,16,1024]{3,2,1,0:T(8,128)(2,1)S(1)} %broadcast_select_fusion), channel_id=1, source_target_pairs={{0,4},{1,5},{2,6},{3,7},{4,0},{5,1},{6,2},{7,3},{8,12},{9,13},{10,... | collective-permute-start | bytes 196616 | tf_op jit(solution)/shard_map/ppermute | solution.py:130
  26.8 12.9 %collective-permute-done.2 = bf16[1,2,16,1024]{3,2,1,0:T(8,128)(2,1)S(1)} collective-permute-done((bf16[1,2,16,1024]{3,2,1,0:T(8,128)(2,1)S(1)}, bf16[1,2,16,1024]{3,2,1,0:T(8,128)(2,1)S(1)}, u32[]{:S(2)}, u32[]{:S(2)}) %collective-permute-start.2) | collective-permute-done | bytes 65568 | tf_op jit(solution)/shard_map/ppermute | solution.py:398
  39.7 10.5 %all-to-all-start = ((bf16[8,2,64,512]{3,2,1,0:T(8,128)(2,1)}), bf16[8,2,64,512]{3,2,1,0:T(8,128)(2,1)S(1)}, u32[]{:S(2)}, u32[]{:S(2)}) async-start(bf16[8,2,64,512]{3,2,1,0:T(8,128)(2,1)} %norm.1), calls=%async_computation | async-start | bytes 2097152 | tf_op jit(solution)/shard_map/all_to_all | solution.py:381
  50.9 42.4 %all-to-all-done.in_ref = bf16[8,2,64,512]{3,2,1,0:T(8,128)(2,1)S(1)} async-done(((bf16[8,2,64,512]{3,2,1,0:T(8,128)(2,1)}), bf16[8,2,64,512]{3,2,1,0:T(8,128)(2,1)S(1)}, u32[]{:S(2)}, u32[]{:S(2)}) %all-to-all-start) | async-done | bytes 1048608 | tf_op jit(solution)/shard_map/all_to_all | solution.py:381
  99.2 12.3 %attention.1 = bf16[8,2,64,512]{3,2,1,0:T(8,128)(2,1)} custom-call(s32[2]{0:T(128)} %and_select_fusion.which, s32[32]{0:T(128)} %reshape_squeeze.3.ids, bf16[8,2,64,512]{3,2,1,0:T(8,128)(2,1)} %copy-done.4, bf16[2,4,128,128]{3,2,1,0:T(8,128)(2,1)} %bitcast.20, bf16[2,4,128,128]{3,2,1,0:T(8,128)(2,1)} %bitcast.22, bf16[2,4,128,128]{3,2,1,0:T(8,128)(2,1)} %bitcast.24), custom_call_target="tpu_custom_call" | custom-call | flops 1207959552 | bytes 2883584 | tf_op jit(solution)/shard_map/attention/pallas_call | solution.py:106
  112.3 8.7 %all-to-all-start.1 = ((bf16[8,2,64,512]{3,2,1,0:T(8,128)(2,1)}), bf16[8,2,64,512]{3,2,1,0:T(8,128)(2,1)S(1)}, u32[]{:S(2)}, u32[]{:S(2)}) async-start(bf16[8,2,64,512]{3,2,1,0:T(8,128)(2,1)} %attention.1), calls=%async_computation.1 | async-start | bytes 2097152 | tf_op jit(solution)/shard_map/all_to_all | solution.py:381
  121.0 42.7 %all-to-all-done.1.att_ref = bf16[8,2,64,512]{3,2,1,0:T(8,128)(2,1)S(1)} async-done(((bf16[8,2,64,512]{3,2,1,0:T(8,128)(2,1)}), bf16[8,2,64,512]{3,2,1,0:T(8,128)(2,1)S(1)}, u32[]{:S(2)}, u32[]{:S(2)}) %all-to-all-start.1) | async-done | bytes 1048608 | tf_op jit(solution)/shard_map/all_to_all | solution.py:381
  169.7 9.1 %mix_send.1 = (bf16[2,17,16,128]{3,2,1,0:T(8,128)(2,1)}, bf16[2,17,16,128]{3,2,1,0:T(8,128)(2,1)}, bf16[2,17,16,128]{3,2,1,0:T(8,128)(2,1)}, bf16[2,17,16,128]{3...) custom-call(s32[2]{0:T(128)} %and_select_fusion.which, ...), custom_call_target="tpu_custom_call" | custom-call | flops 33554432 | bytes 4194304 | tf_op jit(solution)/shard_map/mix_send/pallas_call | solution.py:232
  181.0 8.5 %collective-permute-start.7 = (bf16[2,17,16,128]{3,2,1,0:T(8,128)(2,1)}, bf16[2,17,16,128]{3,2,1,0:T(8,128)(2,1)S(1)}, u32[]{:S(2)}, u32[]{:S(2)}) collective-permute-start(bf16[2,17,16,128]{3,2,1,0:T(8,128)(2,1)} %get-tuple-element.65), channel_id=1, source_target_pairs={{0,9},{1,8},{2,11},{3,10},{4,13},{5,12},{6,15},{7,14},{8,17},{9,16... | collective-permute-start | bytes 417800 | tf_op jit(solution)/shard_map/ppermute | solution.py:392
  192.9 6.0 %collective-permute-start.9 = (bf16[2,17,16,128]{3,2,1,0:T(8,128)(2,1)}, bf16[2,17,16,128]{3,2,1,0:T(8,128)(2,1)S(1)}, u32[]{:S(2)}, u32[]{:S(2)}) collective-permute-start(bf16[2,17,16,128]{3,2,1,0:T(8,128)(2,1)} %get-tuple-element.67), channel_id=1, source_target_pairs={{0,11},{1,10},{2,9},{3,8},{4,15},{5,14},{6,13},{7,12},{8,19},{9,18... | collective-permute-start | bytes 417800 | tf_op jit(solution)/shard_map/ppermute | solution.py:392
  198.9 6.3 %collective-permute-start.10 = (bf16[2,17,16,128]{3,2,1,0:T(8,128)(2,1)}, bf16[2,17,16,128]{3,2,1,0:T(8,128)(2,1)S(1)}, u32[]{:S(2)}, u32[]{:S(2)}) collective-permute-start(bf16[2,17,16,128]{3,2,1,0:T(8,128)(2,1)} %get-tuple-element.68), channel_id=1, source_target_pairs={{0,12},{1,13},{2,14},{3,15},{4,8},{5,9},{6,10},{7,11},{8,20},{9,21... | collective-permute-start | bytes 417800 | tf_op jit(solution)/shard_map/ppermute | solution.py:392
  209.5 9.1 %collective-permute-start.12 = (bf16[2,17,16,128]{3,2,1,0:T(8,128)(2,1)S(1)}, bf16[2,17,16,128]{3,2,1,0:T(8,128)(2,1)S(1)}, u32[]{:S(2)}, u32[]{:S(2)}) collective-permute-start(bf16[2,17,16,128]{3,2,1,0:T(8,128)(2,1)S(1)} %copy-done.33), channel_id=1, source_target_pairs={{0,14},{1,15},{2,12},{3,13},{4,10},{5,11},{6,8},{7,9},{8,22},{9,23... | collective-permute-start | bytes 417800 | tf_op jit(solution)/shard_map/ppermute | solution.py:392
  220.6 11.9 %collective-permute-done.9.refs_3_ = bf16[2,17,16,128]{3,2,1,0:T(8,128)(2,1)S(1)} collective-permute-done((bf16[2,17,16,128]{3,2,1,0:T(8,128)(2,1)}, bf16[2,17,16,128]{3,2,1,0:T(8,128)(2,1)S(1)}, u32[]{:S(2)}, u32[]{:S(2)}) %collective-permute-start.9) | collective-permute-done | bytes 139296 | tf_op jit(solution)/shard_map/ppermute | solution.py:392
  248.6 7.6 %collective-permute-start.25 = (bf16[2,17,16,128]{3,2,1,0:T(8,128)(2,1)S(1)}, bf16[2,17,16,128]{3,2,1,0:T(8,128)(2,1)S(1)}, u32[]{:S(2)}, u32[]{:S(2)}) collective-permute-start(bf16[2,17,16,128]{3,2,1,0:T(8,128)(2,1)S(1)} %collective-permute-done.8.refs_2_), channel_id=1, source_target_pairs={{0,10},{1,11},{2,8},{3,9},{4,14},{5,15},{6,12},{7,13},{8,18},{9,19... | collective-permute-start | bytes 417800 | tf_op jit(solution)/shard_map/ppermute | solution.py:392
  263.8 5.7 %collective-permute-start.27 = (bf16[2,17,16,128]{3,2,1,0:T(8,128)(2,1)S(1)}, bf16[2,17,16,128]{3,2,1,0:T(8,128)(2,1)S(1)}, u32[]{:S(2)}, u32[]{:S(2)}) collective-permute-start(bf16[2,17,16,128]{3,2,1,0:T(8,128)(2,1)S(1)} %collective-permute-done.10.refs_4_), channel_id=1, source_target_pairs={{0,12},{1,13},{2,14},{3,15},{4,8},{5,9},{6,10},{7,11},{8,20},{9,21... | collective-permute-start | bytes 417800 | tf_op jit(solution)/shard_map/ppermute | solution.py:392
  271.5 15.0 %attention_send.1 = (bf16[2,4,64,128]{3,2,1,0:T(8,128)(2,1)}, bf16[2,4,64,128]{3,2,1,0:T(8,128)(2,1)}, bf16[2,4,64,128]{3,2,1,0:T(8,128)(2,1)}, bf16[2,4,64,128]...) custom-call(s32[2]{0:T(128)} %and_select_fusion.1.which, ...), custom_call_target="tpu_custom_call" | custom-call | flops 1207959552 | bytes 2883584 | tf_op jit(solution)/shard_map/attention_send/pallas_call | solution.py:297
  286.6 9.7 %collective-permute-start.29 = (bf16[2,17,16,128]{3,2,1,0:T(8,128)(2,1)S(1)}, bf16[2,17,16,128]{3,2,1,0:T(8,128)(2,1)S(1)}, u32[]{:S(2)}, u32[]{:S(2)}) collective-permute-start(bf16[2,17,16,128]{3,2,1,0:T(8,128)(2,1)S(1)} %copy-done.26), channel_id=1, source_target_pairs={{0,14},{1,15},{2,12},{3,13},{4,10},{5,11},{6,8},{7,9},{8,22},{9,23... | collective-permute-start | bytes 417800 | tf_op jit(solution)/shard_map/ppermute | solution.py:392
  296.4 12.5 %collective-permute-start.30 = (bf16[2,17,16,128]{3,2,1,0:T(8,128)(2,1)}, bf16[2,17,16,128]{3,2,1,0:T(8,128)(2,1)S(1)}, u32[]{:S(2)}, u32[]{:S(2)}) collective-permute-start(bf16[2,17,16,128]{3,2,1,0:T(8,128)(2,1)} %copy-done.27), channel_id=1, source_target_pairs={{0,15},{1,14},{2,13},{3,12},{4,11},{5,10},{6,9},{7,8},{8,23},{9,22... | collective-permute-start | bytes 417800 | tf_op jit(solution)/shard_map/ppermute | solution.py:392
  310.9 7.7 %collective-permute-start.18 = (bf16[2,4,64,128]{3,2,1,0:T(8,128)(2,1)}, bf16[2,4,64,128]{3,2,1,0:T(8,128)(2,1)S(1)}, u32[]{:S(2)}, u32[]{:S(2)}) collective-permute-start(bf16[2,4,64,128]{3,2,1,0:T(8,128)(2,1)} %get-tuple-element.90), channel_id=1, source_target_pairs={{0,9},{1,8},{2,11},{3,10},{4,13},{5,12},{6,15},{7,14},{8,17},{9,16... | collective-permute-start | bytes 393224 | tf_op jit(solution)/shard_map/ppermute | solution.py:392
  320.6 6.0 %collective-permute-start.20 = (bf16[2,4,64,128]{3,2,1,0:T(8,128)(2,1)}, bf16[2,4,64,128]{3,2,1,0:T(8,128)(2,1)S(1)}, u32[]{:S(2)}, u32[]{:S(2)}) collective-permute-start(bf16[2,4,64,128]{3,2,1,0:T(8,128)(2,1)} %get-tuple-element.92), channel_id=1, source_target_pairs={{0,11},{1,10},{2,9},{3,8},{4,15},{5,14},{6,13},{7,12},{8,19},{9,18... | collective-permute-start | bytes 393224 | tf_op jit(solution)/shard_map/ppermute | solution.py:392
  326.6 10.0 %collective-permute-start.21 = (bf16[2,4,64,128]{3,2,1,0:T(8,128)(2,1)S(1)}, bf16[2,4,64,128]{3,2,1,0:T(8,128)(2,1)S(1)}, u32[]{:S(2)}, u32[]{:S(2)}) collective-permute-start(bf16[2,4,64,128]{3,2,1,0:T(8,128)(2,1)S(1)} %copy-done.38), channel_id=1, source_target_pairs={{0,12},{1,13},{2,14},{3,15},{4,8},{5,9},{6,10},{7,11},{8,20},{9,21... | collective-permute-start | bytes 393224 | tf_op jit(solution)/shard_map/ppermute | solution.py:392
  339.0 11.0 %collective-permute-start.23 = (bf16[2,4,64,128]{3,2,1,0:T(8,128)(2,1)S(1)}, bf16[2,4,64,128]{3,2,1,0:T(8,128)(2,1)S(1)}, u32[]{:S(2)}, u32[]{:S(2)}) collective-permute-start(bf16[2,4,64,128]{3,2,1,0:T(8,128)(2,1)S(1)} %copy-done.36), channel_id=1, source_target_pairs={{0,14},{1,15},{2,12},{3,13},{4,10},{5,11},{6,8},{7,9},{8,22},{9,23... | collective-permute-start | bytes 393224 | tf_op jit(solution)/shard_map/ppermute | solution.py:392
  359.3 13.9 %collective-permute-done.23.refs_6_ = bf16[2,4,64,128]{3,2,1,0:T(8,128)(2,1)S(1)} collective-permute-done((bf16[2,4,64,128]{3,2,1,0:T(8,128)(2,1)S(1)}, bf16[2,4,64,128]{3,2,1,0:T(8,128)(2,1)S(1)}, u32[]{:S(2)}, u32[]{:S(2)}) %collective-permute-start.23) | collective-permute-done | bytes 131104 | tf_op jit(solution)/shard_map/ppermute | solution.py:392
  373.9 8.2 %mix_final.1 = bf16[2,64,4096]{2,1,0:T(8,128)(2,1)} custom-call(s32[2]{0:T(128)} %get-tuple-element.98.which, s32[1]{0:T(128)} %bitcast.me, s32[2]{0:T(128)} %get-tuple-element.97.target, bf16[2,4,64,128]{3,2,1,0:T(8,128)(2,1)} %copy-done.13, bf16[2,4,64,128]{3,2,1,0:T(8,128)(2,1)} %copy-done.14, bf16[2,4,64,128]{3,2,1,0:T(8,128)(2,1)} %copy-done.15, ...), custom_call_target="tpu_custom_call" | custom-call | flops 33554432 | bytes 4194304 | tf_op jit(solution)/shard_map/mix_final/pallas_call | solution.py:356
  (149 shorter events, 84.3 us)
Async XLA Ops:
  39.7 53.6 %all-to-all-start = ((bf16[8,2,64,512]{3,2,1,0:T(8,128)(2,1)}), bf16[8,2,64,512]{3,2,1,0:T(8,128)(2,1)S(1)}, u32[]{:S(2)}, u32[]{:S(2)}) async-start(bf16[8,2,64,512]{3,2,1,0:T(8,128)(2,1)} %norm.1), calls=%async_computation | async-start | bytes 2097152 | tf_op jit(solution)/shard_map/all_to_all | solution.py:381
  112.3 51.4 %all-to-all-start.1 = ((bf16[8,2,64,512]{3,2,1,0:T(8,128)(2,1)}), bf16[8,2,64,512]{3,2,1,0:T(8,128)(2,1)S(1)}, u32[]{:S(2)}, u32[]{:S(2)}) async-start(bf16[8,2,64,512]{3,2,1,0:T(8,128)(2,1)} %attention.1), calls=%async_computation.1 | async-start | bytes 2097152 | tf_op jit(solution)/shard_map/all_to_all | solution.py:381
  178.9 26.3 %collective-permute-start.6 = (bf16[2,17,16,128]{3,2,1,0:T(8,128)(2,1)}, bf16[2,17,16,128]{3,2,1,0:T(8,128)(2,1)S(1)}, u32[]{:S(2)}, u32[]{:S(2)}) collective-permute-start(bf16[2,17,16,128]{3,2,1,0:T(8,128)(2,1)} %get-tuple-element.64), channel_id=1, source_target_pairs={{0,8},{1,9},{2,10},{3,11},{4,12},{5,13},{6,14},{7,15},{8,16},{9,17... | collective-permute-start | bytes 417800 | tf_op jit(solution)/shard_map/ppermute | solution.py:392
  181.0 28.5 %collective-permute-start.7 = (bf16[2,17,16,128]{3,2,1,0:T(8,128)(2,1)}, bf16[2,17,16,128]{3,2,1,0:T(8,128)(2,1)S(1)}, u32[]{:S(2)}, u32[]{:S(2)}) collective-permute-start(bf16[2,17,16,128]{3,2,1,0:T(8,128)(2,1)} %get-tuple-element.65), channel_id=1, source_target_pairs={{0,9},{1,8},{2,11},{3,10},{4,13},{5,12},{6,15},{7,14},{8,17},{9,16... | collective-permute-start | bytes 417800 | tf_op jit(solution)/shard_map/ppermute | solution.py:392
  189.5 29.1 %collective-permute-start.8 = (bf16[2,17,16,128]{3,2,1,0:T(8,128)(2,1)}, bf16[2,17,16,128]{3,2,1,0:T(8,128)(2,1)S(1)}, u32[]{:S(2)}, u32[]{:S(2)}) collective-permute-start(bf16[2,17,16,128]{3,2,1,0:T(8,128)(2,1)} %get-tuple-element.66), channel_id=1, source_target_pairs={{0,10},{1,11},{2,8},{3,9},{4,14},{5,15},{6,12},{7,13},{8,18},{9,19... | collective-permute-start | bytes 417800 | tf_op jit(solution)/shard_map/ppermute | solution.py:392
  192.9 39.6 %collective-permute-start.9 = (bf16[2,17,16,128]{3,2,1,0:T(8,128)(2,1)}, bf16[2,17,16,128]{3,2,1,0:T(8,128)(2,1)S(1)}, u32[]{:S(2)}, u32[]{:S(2)}) collective-permute-start(bf16[2,17,16,128]{3,2,1,0:T(8,128)(2,1)} %get-tuple-element.67), channel_id=1, source_target_pairs={{0,11},{1,10},{2,9},{3,8},{4,15},{5,14},{6,13},{7,12},{8,19},{9,18... | collective-permute-start | bytes 417800 | tf_op jit(solution)/shard_map/ppermute | solution.py:392
  198.9 33.6 %collective-permute-start.10 = (bf16[2,17,16,128]{3,2,1,0:T(8,128)(2,1)}, bf16[2,17,16,128]{3,2,1,0:T(8,128)(2,1)S(1)}, u32[]{:S(2)}, u32[]{:S(2)}) collective-permute-start(bf16[2,17,16,128]{3,2,1,0:T(8,128)(2,1)} %get-tuple-element.68), channel_id=1, source_target_pairs={{0,12},{1,13},{2,14},{3,15},{4,8},{5,9},{6,10},{7,11},{8,20},{9,21... | collective-permute-start | bytes 417800 | tf_op jit(solution)/shard_map/ppermute | solution.py:392
  205.3 27.2 %collective-permute-start.11 = (bf16[2,17,16,128]{3,2,1,0:T(8,128)(2,1)S(1)}, bf16[2,17,16,128]{3,2,1,0:T(8,128)(2,1)S(1)}, u32[]{:S(2)}, u32[]{:S(2)}) collective-permute-start(bf16[2,17,16,128]{3,2,1,0:T(8,128)(2,1)S(1)} %copy-done.34), channel_id=1, source_target_pairs={{0,13},{1,12},{2,15},{3,14},{4,9},{5,8},{6,11},{7,10},{8,21},{9,20... | collective-permute-start | bytes 417800 | tf_op jit(solution)/shard_map/ppermute | solution.py:392
  209.5 28.8 %collective-permute-start.12 = (bf16[2,17,16,128]{3,2,1,0:T(8,128)(2,1)S(1)}, bf16[2,17,16,128]{3,2,1,0:T(8,128)(2,1)S(1)}, u32[]{:S(2)}, u32[]{:S(2)}) collective-permute-start(bf16[2,17,16,128]{3,2,1,0:T(8,128)(2,1)S(1)} %copy-done.33), channel_id=1, source_target_pairs={{0,14},{1,15},{2,12},{3,13},{4,10},{5,11},{6,8},{7,9},{8,22},{9,23... | collective-permute-start | bytes 417800 | tf_op jit(solution)/shard_map/ppermute | solution.py:392
  218.6 22.4 %collective-permute-start.13 = (bf16[2,17,16,128]{3,2,1,0:T(8,128)(2,1)S(1)}, bf16[2,17,16,128]{3,2,1,0:T(8,128)(2,1)S(1)}, u32[]{:S(2)}, u32[]{:S(2)}) collective-permute-start(bf16[2,17,16,128]{3,2,1,0:T(8,128)(2,1)S(1)} %copy-done.32), channel_id=1, source_target_pairs={{0,15},{1,14},{2,13},{3,12},{4,11},{5,10},{6,9},{7,8},{8,23},{9,22... | collective-permute-start | bytes 417800 | tf_op jit(solution)/shard_map/ppermute | solution.py:392
  241.0 55.3 %collective-permute-start.16 = (bf16[4,2,16,1024]{3,2,1,0:T(8,128)(2,1)S(1)}, bf16[4,2,16,1024]{3,2,1,0:T(8,128)(2,1)S(1)}, u32[]{:S(2)}, u32[]{:S(2)}) collective-permute-start(bf16[4,2,16,1024]{3,2,1,0:T(8,128)(2,1)S(1)} %constant_dynamic-update-slice_fusion.4), channel_id=1, source_target_pairs={{0,1},{1,0},{2,3},{3,2},{4,5},{5,4},{6,7},{7,6},{8,9},{9,8},{10,11... | collective-permute-start | bytes 786440 | tf_op jit(solution)/shard_map/ppermute | solution.py:130
  246.1 23.4 %collective-permute-start.15 = (bf16[2,17,16,128]{3,2,1,0:T(8,128)(2,1)S(1)}, bf16[2,17,16,128]{3,2,1,0:T(8,128)(2,1)S(1)}, u32[]{:S(2)}, u32[]{:S(2)}) collective-permute-start(bf16[2,17,16,128]{3,2,1,0:T(8,128)(2,1)S(1)} %collective-permute-done.7.refs_1_), channel_id=1, source_target_pairs={{0,9},{1,8},{2,11},{3,10},{4,13},{5,12},{6,15},{7,14},{8,17},{9,16... | collective-permute-start | bytes 417800 | tf_op jit(solution)/shard_map/ppermute | solution.py:392
  248.6 38.0 %collective-permute-start.25 = (bf16[2,17,16,128]{3,2,1,0:T(8,128)(2,1)S(1)}, bf16[2,17,16,128]{3,2,1,0:T(8,128)(2,1)S(1)}, u32[]{:S(2)}, u32[]{:S(2)}) collective-permute-start(bf16[2,17,16,128]{3,2,1,0:T(8,128)(2,1)S(1)} %collective-permute-done.8.refs_2_), channel_id=1, source_target_pairs={{0,10},{1,11},{2,8},{3,9},{4,14},{5,15},{6,12},{7,13},{8,18},{9,19... | collective-permute-start | bytes 417800 | tf_op jit(solution)/shard_map/ppermute | solution.py:392
  256.3 52.7 %collective-permute-start.26 = (bf16[2,17,16,128]{3,2,1,0:T(8,128)(2,1)S(1)}, bf16[2,17,16,128]{3,2,1,0:T(8,128)(2,1)S(1)}, u32[]{:S(2)}, u32[]{:S(2)}) collective-permute-start(bf16[2,17,16,128]{3,2,1,0:T(8,128)(2,1)S(1)} %collective-permute-done.9.refs_3_), channel_id=1, source_target_pairs={{0,11},{1,10},{2,9},{3,8},{4,15},{5,14},{6,13},{7,12},{8,19},{9,18... | collective-permute-start | bytes 417800 | tf_op jit(solution)/shard_map/ppermute | solution.py:392
  263.8 47.2 %collective-permute-start.27 = (bf16[2,17,16,128]{3,2,1,0:T(8,128)(2,1)S(1)}, bf16[2,17,16,128]{3,2,1,0:T(8,128)(2,1)S(1)}, u32[]{:S(2)}, u32[]{:S(2)}) collective-permute-start(bf16[2,17,16,128]{3,2,1,0:T(8,128)(2,1)S(1)} %collective-permute-done.10.refs_4_), channel_id=1, source_target_pairs={{0,12},{1,13},{2,14},{3,15},{4,8},{5,9},{6,10},{7,11},{8,20},{9,21... | collective-permute-start | bytes 417800 | tf_op jit(solution)/shard_map/ppermute | solution.py:392
  269.5 49.1 %collective-permute-start.28 = (bf16[2,17,16,128]{3,2,1,0:T(8,128)(2,1)S(1)}, bf16[2,17,16,128]{3,2,1,0:T(8,128)(2,1)S(1)}, u32[]{:S(2)}, u32[]{:S(2)}) collective-permute-start(bf16[2,17,16,128]{3,2,1,0:T(8,128)(2,1)S(1)} %collective-permute-done.11.refs_5_), channel_id=1, source_target_pairs={{0,13},{1,12},{2,15},{3,14},{4,9},{5,8},{6,11},{7,10},{8,21},{9,20... | collective-permute-start | bytes 417800 | tf_op jit(solution)/shard_map/ppermute | solution.py:392
  286.6 34.0 %collective-permute-start.29 = (bf16[2,17,16,128]{3,2,1,0:T(8,128)(2,1)S(1)}, bf16[2,17,16,128]{3,2,1,0:T(8,128)(2,1)S(1)}, u32[]{:S(2)}, u32[]{:S(2)}) collective-permute-start(bf16[2,17,16,128]{3,2,1,0:T(8,128)(2,1)S(1)} %copy-done.26), channel_id=1, source_target_pairs={{0,14},{1,15},{2,12},{3,13},{4,10},{5,11},{6,8},{7,9},{8,22},{9,23... | collective-permute-start | bytes 417800 | tf_op jit(solution)/shard_map/ppermute | solution.py:392
  296.4 30.3 %collective-permute-start.30 = (bf16[2,17,16,128]{3,2,1,0:T(8,128)(2,1)}, bf16[2,17,16,128]{3,2,1,0:T(8,128)(2,1)S(1)}, u32[]{:S(2)}, u32[]{:S(2)}) collective-permute-start(bf16[2,17,16,128]{3,2,1,0:T(8,128)(2,1)} %copy-done.27), channel_id=1, source_target_pairs={{0,15},{1,14},{2,13},{3,12},{4,11},{5,10},{6,9},{7,8},{8,23},{9,22... | collective-permute-start | bytes 417800 | tf_op jit(solution)/shard_map/ppermute | solution.py:392
  309.0 28.0 %collective-permute-start.17 = (bf16[2,4,64,128]{3,2,1,0:T(8,128)(2,1)}, bf16[2,4,64,128]{3,2,1,0:T(8,128)(2,1)S(1)}, u32[]{:S(2)}, u32[]{:S(2)}) collective-permute-start(bf16[2,4,64,128]{3,2,1,0:T(8,128)(2,1)} %get-tuple-element.89), channel_id=1, source_target_pairs={{0,8},{1,9},{2,10},{3,11},{4,12},{5,13},{6,14},{7,15},{8,16},{9,17... | collective-permute-start | bytes 393224 | tf_op jit(solution)/shard_map/ppermute | solution.py:392
  310.9 28.0 %collective-permute-start.18 = (bf16[2,4,64,128]{3,2,1,0:T(8,128)(2,1)}, bf16[2,4,64,128]{3,2,1,0:T(8,128)(2,1)S(1)}, u32[]{:S(2)}, u32[]{:S(2)}) collective-permute-start(bf16[2,4,64,128]{3,2,1,0:T(8,128)(2,1)} %get-tuple-element.90), channel_id=1, source_target_pairs={{0,9},{1,8},{2,11},{3,10},{4,13},{5,12},{6,15},{7,14},{8,17},{9,16... | collective-permute-start | bytes 393224 | tf_op jit(solution)/shard_map/ppermute | solution.py:392
  318.7 33.5 %collective-permute-start.19 = (bf16[2,4,64,128]{3,2,1,0:T(8,128)(2,1)}, bf16[2,4,64,128]{3,2,1,0:T(8,128)(2,1)S(1)}, u32[]{:S(2)}, u32[]{:S(2)}) collective-permute-start(bf16[2,4,64,128]{3,2,1,0:T(8,128)(2,1)} %get-tuple-element.91), channel_id=1, source_target_pairs={{0,10},{1,11},{2,8},{3,9},{4,14},{5,15},{6,12},{7,13},{8,18},{9,19... | collective-permute-start | bytes 393224 | tf_op jit(solution)/shard_map/ppermute | solution.py:392
  320.6 38.6 %collective-permute-start.20 = (bf16[2,4,64,128]{3,2,1,0:T(8,128)(2,1)}, bf16[2,4,64,128]{3,2,1,0:T(8,128)(2,1)S(1)}, u32[]{:S(2)}, u32[]{:S(2)}) collective-permute-start(bf16[2,4,64,128]{3,2,1,0:T(8,128)(2,1)} %get-tuple-element.92), channel_id=1, source_target_pairs={{0,11},{1,10},{2,9},{3,8},{4,15},{5,14},{6,13},{7,12},{8,19},{9,18... | collective-permute-start | bytes 393224 | tf_op jit(solution)/shard_map/ppermute | solution.py:392
  326.6 32.6 %collective-permute-start.21 = (bf16[2,4,64,128]{3,2,1,0:T(8,128)(2,1)S(1)}, bf16[2,4,64,128]{3,2,1,0:T(8,128)(2,1)S(1)}, u32[]{:S(2)}, u32[]{:S(2)}) collective-permute-start(bf16[2,4,64,128]{3,2,1,0:T(8,128)(2,1)S(1)} %copy-done.38), channel_id=1, source_target_pairs={{0,12},{1,13},{2,14},{3,15},{4,8},{5,9},{6,10},{7,11},{8,20},{9,21... | collective-permute-start | bytes 393224 | tf_op jit(solution)/shard_map/ppermute | solution.py:392
  339.0 34.3 %collective-permute-start.23 = (bf16[2,4,64,128]{3,2,1,0:T(8,128)(2,1)S(1)}, bf16[2,4,64,128]{3,2,1,0:T(8,128)(2,1)S(1)}, u32[]{:S(2)}, u32[]{:S(2)}) collective-permute-start(bf16[2,4,64,128]{3,2,1,0:T(8,128)(2,1)S(1)} %copy-done.36), channel_id=1, source_target_pairs={{0,14},{1,15},{2,12},{3,13},{4,10},{5,11},{6,8},{7,9},{8,22},{9,23... | collective-permute-start | bytes 393224 | tf_op jit(solution)/shard_map/ppermute | solution.py:392
  (48 other events, 1318.9 us)

commit v3 on v2

--- a/solution.py
+++ b/solution.py
@@ -9,7 +9,6 @@
 EPS = 1e-05
 BF = jnp.bfloat16
 F32 = jnp.float32
-EARLY = 2
 
 
 def norm_kernel(which, x_ref, gain_ref, out_ref):
@@ -258,13 +257,14 @@
     out_refs, scratch = rest[4:-3], rest[-3:]
     rows_ref = scratch[0]
     slot, head = pl.program_id(0), pl.program_id(1)
-    block, width = out_refs[0].shape
+    block, width = out_refs[0].shape[1:]
     tile = in_refs[0].shape[1]
     tiles = block // tile
     gain = gain_ref[0].astype(F32)
     for k, ref in enumerate(in_refs):
         start = pl.multiple_of((me[0] ^ k) * block, block)
         rows = ref[pl.ds(head * tiles, tiles)].reshape(block, width)
+        out_refs[k][1] = rows
         packed = ref[ref.shape[0] - 1].astype(F32)
         scale = jnp.concatenate(
             [
@@ -281,7 +281,7 @@
     rows_ref[...] = mixed
     for k, out_ref in enumerate(out_refs):
         start = pl.multiple_of((me[0] ^ k) * block, block)
-        out_ref[...] = rows_ref[pl.ds(start, block), :]
+        out_ref[0] = rows_ref[pl.ds(start, block), :]
 
 
 def attention_send(which, me, ids, blocks, gain, wq, wk, wv):
@@ -296,7 +296,7 @@
     )
     return pl.pallas_call(
         attention_send_kernel,
-        out_shape=[jax.ShapeDtypeStruct((slots, heads, BLK, width), BF)] * size,
+        out_shape=[jax.ShapeDtypeStruct((slots, 2, heads, BLK, width), BF)] * size,
         grid_spec=pltpu.PrefetchScalarGridSpec(
             num_scalar_prefetch=3,
             grid=(slots, heads),
@@ -311,7 +311,9 @@
                 weight_spec,
             ],
             out_specs=[
-                pl.BlockSpec((None, None, BLK, width), lambda k, h, which, me, ids: (k, h, 0, 0))
+                pl.BlockSpec(
+                    (None, 2, None, BLK, width), lambda k, h, which, me, ids: (k, 0, h, 0, 0)
+                )
             ]
             * size,
             scratch_shapes=attention_scratch(size * BLK, width),
@@ -322,19 +324,15 @@
 
 
 def mix_final_kernel(which, me, target, *refs):
-    size = (len(refs) - 4) // 2
-    att_refs, x_refs, w_ref = refs[:size], refs[size : 2 * size], refs[2 * size]
-    out_ref, wide_ref, state_ref = refs[-3:]
-    heads, rows, width = wide_ref.shape
-    per = att_refs[0].shape[0]
-    tile = x_refs[0].shape[1]
-    tiles = rows // tile
-    for k in range(size):
+    in_refs, (w_ref, out_ref, wide_ref, state_ref) = refs[:-4], refs[-4:]
+    heads = wide_ref.shape[0]
+    width = wide_ref.shape[2]
+    per = in_refs[0].shape[1]
+    for k, in_ref in enumerate(in_refs):
         group = me[0] ^ k
         for h in range(per):
-            wide_ref[group * per + h] = att_refs[k][h].astype(F32)
-            state = x_refs[k][h * tiles : (h + 1) * tiles]
-            state_ref[group * per + h] = state.reshape(rows, width)
+            wide_ref[group * per + h] = in_ref[0, h].astype(F32)
+            state_ref[group * per + h] = in_ref[1, h]
     step = 4
 
     def body(i, carry):
@@ -348,9 +346,9 @@
     lax.fori_loop(0, heads // step, body, 0)
 
 
-def mix_final(which, me, target, attended, states, weights):
-    size = len(attended)
-    slots, per, rows, width = attended[0].shape
+def mix_final(which, me, target, blocks, weights):
+    size = len(blocks)
+    slots, _, per, rows, width = blocks[0].shape
     heads = size * per
     pairs = weights.shape[1]
     return pl.pallas_call(
@@ -360,9 +358,11 @@
             num_scalar_prefetch=3,
             grid=(slots,),
             in_specs=[
-                pl.BlockSpec((None, *array.shape[1:]), lambda k, which, me, target: (k, 0, 0, 0))
-                for array in [*attended, *states]
+                pl.BlockSpec(
+                    (None, *blocks[0].shape[1:]), lambda k, which, me, target: (k, 0, 0, 0, 0)
+                )
             ]
+            * size
             + [pl.BlockSpec((1, pairs, width), lambda k, which, me, target: (which[k], 0, 0))],
             out_specs=pl.BlockSpec(
                 (None, rows, heads * width), lambda k, which, me, target: (target[k], 0, 0)
@@ -374,7 +374,7 @@
         ),
         cost_estimate=mix_cost(slots, rows, heads * width, pairs, width),
         name="mix_final",
-    )(which, me, target, *attended, *states, weights)
+    )(which, me, target, *blocks, weights)
 
 
 def exchange(value):
@@ -428,26 +428,26 @@
     place = gathered_place(bits)
 
     own = partner(masked, bits[0])
-    left = shifted(masked)
     normed = norm(first, whole, gain, size)
+    rows = exchange(tie(normed, own))
     own = partner(own, bits[1])
-    rows = exchange(tie(normed, own, left))
+    left = shifted(tie(masked, normed))
+    rows = tie(rows, own, left)
     own = partner(tie(own, rows), bits[2])
     left = partner(tie(left, rows), bits[0])
     attended = attention(first, ids, rows, wq, wk, wv)
     back = exchange(tie(attended, own, left))
     own = mix_weights(place, own)
-    left = partner(tie(left, back), bits[1])
+    left = partner(left, bits[1])
+    back = tie(back, left, own)
+    left = partner(tie(left, back), bits[2])
     sent = mix_send(first, me, back, own, whole)
     sent = list(lax.optimization_barrier((*sent, left))[:-1])
     here = send_on(sent)
-    onward = send_on(here)
-    left = partner(tie(left, *here), bits[2])
-    ready = lax.optimization_barrier((*here, *onward[:EARLY]))[: len(here)]
-    attended = attention_send(second, me, ids, ready, gain, wq, wk, wv)
-    last = send_on(lax.optimization_barrier((*attended, left))[:-1])
+    attended = attention_send(second, me, ids, here, gain, wq, wk, wv)
     left = mix_weights(place, left)
-    done = mix_final(mixing, me, target, last, onward, left)
+    last = send_on(attended)
+    done = mix_final(mixing, me, target, last, left)
     return done[:, None]
 
 

time: 384 us -> 361 us (0.940)
  the two profiles are of different devices: /device:TPU:32 before, /device:TPU:64 now
where the time goes in v3:
time: 361 us; the launch traced here: 360 us
  waiting for transfers between devices  176 us (49%)
  starting transfers between devices  120 us (33%)
  Pallas kernels  53.8 us (15%)
  local copies, waits for them, and re-layouts  6.14 us (2%)
    ppermute x16, waiting for transfers between devices, send_on(): arrived.append(lax.ppermute(block, ('segment', 'fsdp'), pairs))  89 us
    ppermute x16, starting transfers between devices, send_on(): arrived.append(lax.ppermute(block, ('segment', 'fsdp'), pairs))  77.1 us
    ppermute x1, waiting for transfers between devices, shifted(): lax.ppermute(value, 'segment', [(i, (i + 1) % devices) for i in range(dev...  34.5 us
    ppermute x6, waiting for transfers between devices, partner(): other = lax.ppermute(value, 'fsdp', [(i, i ^ bit) for i in range(size)])  30.6 us
    all_to_all x2, waiting for transfers between devices, exchange(): lax.all_to_all(value, 'fsdp', split_axis=0, concat_axis=0, tiled=True)  22.3 us
    all_to_all x2, starting transfers between devices, exchange(): lax.all_to_all(value, 'fsdp', split_axis=0, concat_axis=0, tiled=True)  22.3 us
    ppermute x6, starting transfers between devices, partner(): other = lax.ppermute(value, 'fsdp', [(i, i ^ bit) for i in range(size)])  18.6 us
    pallas_call x1, Pallas kernels, attention_send(): pl.pallas_call(attention_send_kernel, out_shape=[jax.ShapeDtypeStruct((sl...  15.3 us
  transfers between devices with their start and end apart: 25, of which 13 were waited for; matrix products, arithmetic and copies ran while one was open for 1% of the time, Pallas kernels for 8%

profile of v3, /device:TPU:64, one launch (start us, length us, event | category | flops | bytes accessed | tf_op | source)
XLA Modules:
  0.0 359.6 jit_solution(7005652093775205450)
XLA Ops:
  2.0 9.1 %collective-permute-start = (bf16[1,2,16,1024]{3,2,1,0:T(8,128)(2,1)S(1)}, bf16[1,2,16,1024]{3,2,1,0:T(8,128)(2,1)S(1)}, u32[]{:S(2)}, u32[]{:S(2)}) collective-permute-start(bf16[1,2,16,1024]{3,2,1,0:T(8,128)(2,1)S(1)} %broadcast_select_fusion), channel_id=1, source_target_pairs={{0,4},{1,5},{2,6},{3,7},{4,0},{5,1},{6,2},{7,3},{8,12},{9,13},{10,... | collective-permute-start | bytes 196616 | tf_op jit(solution)/shard_map/ppermute | solution.py:129
  15.4 11.3 %all-to-all-start = ((bf16[8,2,64,512]{3,2,1,0:T(8,128)(2,1)}), bf16[8,2,64,512]{3,2,1,0:T(8,128)(2,1)S(1)}, u32[]{:S(2)}, u32[]{:S(2)}) async-start(bf16[8,2,64,512]{3,2,1,0:T(8,128)(2,1)} %norm.1), calls=%async_computation | async-start | bytes 2097152 | tf_op jit(solution)/shard_map/all_to_all | solution.py:381
  31.2 20.2 %collective-permute-done.1 = bf16[2,2,16,1024]{3,2,1,0:T(8,128)(2,1)S(1)} collective-permute-done((bf16[2,2,16,1024]{3,2,1,0:T(8,128)(2,1)S(1)}, bf16[2,2,16,1024]{3,2,1,0:T(8,128)(2,1)S(1)}, u32[]{:S(2)}, u32[]{:S(2)}) %collective-permute-start.1) | collective-permute-done | bytes 131104 | tf_op jit(solution)/shard_map/ppermute | solution.py:129
  51.5 34.5 %collective-permute-done.2 = bf16[1,2,16,1024]{3,2,1,0:T(8,128)(2,1)S(1)} collective-permute-done((bf16[1,2,16,1024]{3,2,1,0:T(8,128)(2,1)S(1)}, bf16[1,2,16,1024]{3,2,1,0:T(8,128)(2,1)S(1)}, u32[]{:S(2)}, u32[]{:S(2)}) %collective-permute-start.2) | collective-permute-done | bytes 65568 | tf_op jit(solution)/shard_map/ppermute | solution.py:398
  89.9 12.3 %attention.1 = bf16[8,2,64,512]{3,2,1,0:T(8,128)(2,1)} custom-call(s32[2]{0:T(128)} %and_select_fusion.which, s32[32]{0:T(128)} %reshape_squeeze.3.ids, bf16[8,2,64,512]{3,2,1,0:T(8,128)(2,1)} %copy-done.4, bf16[2,4,128,128]{3,2,1,0:T(8,128)(2,1)} %bitcast.20, bf16[2,4,128,128]{3,2,1,0:T(8,128)(2,1)} %bitcast.22, bf16[2,4,128,128]{3,2,1,0:T(8,128)(2,1)} %bitcast.24), custom_call_target="tpu_custom_call" | custom-call | flops 1207959552 | bytes 2883584 | tf_op jit(solution)/shard_map/attention/pallas_call | solution.py:105
  103.1 11.0 %all-to-all-start.1 = ((bf16[8,2,64,512]{3,2,1,0:T(8,128)(2,1)}), bf16[8,2,64,512]{3,2,1,0:T(8,128)(2,1)S(1)}, u32[]{:S(2)}, u32[]{:S(2)}) async-start(bf16[8,2,64,512]{3,2,1,0:T(8,128)(2,1)} %attention.1), calls=%async_computation.1 | async-start | bytes 2097152 | tf_op jit(solution)/shard_map/all_to_all | solution.py:381
  117.3 10.4 %collective-permute-done.5 = bf16[2,2,16,1024]{3,2,1,0:T(8,128)(2,1)S(1)} collective-permute-done((bf16[2,2,16,1024]{3,2,1,0:T(8,128)(2,1)S(1)}, bf16[2,2,16,1024]{3,2,1,0:T(8,128)(2,1)S(1)}, u32[]{:S(2)}, u32[]{:S(2)}) %collective-permute-start.5) | collective-permute-done | bytes 131104 | tf_op jit(solution)/shard_map/ppermute | solution.py:129
  130.6 22.3 %all-to-all-done.1.att_ref = bf16[8,2,64,512]{3,2,1,0:T(8,128)(2,1)S(1)} async-done(((bf16[8,2,64,512]{3,2,1,0:T(8,128)(2,1)}), bf16[8,2,64,512]{3,2,1,0:T(8,128)(2,1)S(1)}, u32[]{:S(2)}, u32[]{:S(2)}) %all-to-all-start.1) | async-done | bytes 1048608 | tf_op jit(solution)/shard_map/all_to_all | solution.py:381
  154.9 9.1 %mix_send.1 = (bf16[2,17,16,128]{3,2,1,0:T(8,128)(2,1)}, bf16[2,17,16,128]{3,2,1,0:T(8,128)(2,1)}, bf16[2,17,16,128]{3,2,1,0:T(8,128)(2,1)}, bf16[2,17,16,128]{3...) custom-call(s32[2]{0:T(128)} %and_select_fusion.which, ...), custom_call_target="tpu_custom_call" | custom-call | flops 33554432 | bytes 4194304 | tf_op jit(solution)/shard_map/mix_send/pallas_call | solution.py:231
  166.2 9.9 %collective-permute-start.8 = (bf16[2,17,16,128]{3,2,1,0:T(8,128)(2,1)S(1)}, bf16[2,17,16,128]{3,2,1,0:T(8,128)(2,1)S(1)}, u32[]{:S(2)}, u32[]{:S(2)}) collective-permute-start(bf16[2,17,16,128]{3,2,1,0:T(8,128)(2,1)S(1)} %copy-done.28), channel_id=1, source_target_pairs={{0,9},{1,8},{2,11},{3,10},{4,13},{5,12},{6,15},{7,14},{8,17},{9,16... | collective-permute-start | bytes 417800 | tf_op jit(solution)/shard_map/ppermute | solution.py:392
  184.1 6.8 %collective-permute-start.11 = (bf16[2,17,16,128]{3,2,1,0:T(8,128)(2,1)S(1)}, bf16[2,17,16,128]{3,2,1,0:T(8,128)(2,1)S(1)}, u32[]{:S(2)}, u32[]{:S(2)}) collective-permute-start(bf16[2,17,16,128]{3,2,1,0:T(8,128)(2,1)S(1)} %copy-done.21), channel_id=1, source_target_pairs={{0,12},{1,13},{2,14},{3,15},{4,8},{5,9},{6,10},{7,11},{8,20},{9,21... | collective-permute-start | bytes 417800 | tf_op jit(solution)/shard_map/ppermute | solution.py:392
  190.9 6.0 %collective-permute-start.12 = (bf16[2,17,16,128]{3,2,1,0:T(8,128)(2,1)S(1)}, bf16[2,17,16,128]{3,2,1,0:T(8,128)(2,1)S(1)}, u32[]{:S(2)}, u32[]{:S(2)}) collective-permute-start(bf16[2,17,16,128]{3,2,1,0:T(8,128)(2,1)S(1)} %copy-done.19), channel_id=1, source_target_pairs={{0,13},{1,12},{2,15},{3,14},{4,9},{5,8},{6,11},{7,10},{8,21},{9,20... | collective-permute-start | bytes 417800 | tf_op jit(solution)/shard_map/ppermute | solution.py:392
  196.9 7.3 %collective-permute-start.13 = (bf16[2,17,16,128]{3,2,1,0:T(8,128)(2,1)S(1)}, bf16[2,17,16,128]{3,2,1,0:T(8,128)(2,1)S(1)}, u32[]{:S(2)}, u32[]{:S(2)}) collective-permute-start(bf16[2,17,16,128]{3,2,1,0:T(8,128)(2,1)S(1)} %copy-done.17), channel_id=1, source_target_pairs={{0,14},{1,15},{2,12},{3,13},{4,10},{5,11},{6,8},{7,9},{8,22},{9,23... | collective-permute-start | bytes 417800 | tf_op jit(solution)/shard_map/ppermute | solution.py:392
  204.3 6.7 %collective-permute-start.14 = (bf16[2,17,16,128]{3,2,1,0:T(8,128)(2,1)S(1)}, bf16[2,17,16,128]{3,2,1,0:T(8,128)(2,1)S(1)}, u32[]{:S(2)}, u32[]{:S(2)}) collective-permute-start(bf16[2,17,16,128]{3,2,1,0:T(8,128)(2,1)S(1)} %copy-done.15), channel_id=1, source_target_pairs={{0,15},{1,14},{2,13},{3,12},{4,11},{5,10},{6,9},{7,8},{8,23},{9,22... | collective-permute-start | bytes 417800 | tf_op jit(solution)/shard_map/ppermute | solution.py:392
  211.6 16.4 %collective-permute-done.13.refs_6_ = bf16[2,17,16,128]{3,2,1,0:T(8,128)(2,1)S(1)} collective-permute-done((bf16[2,17,16,128]{3,2,1,0:T(8,128)(2,1)S(1)}, bf16[2,17,16,128]{3,2,1,0:T(8,128)(2,1)S(1)}, u32[]{:S(2)}, u32[]{:S(2)}) %collective-permute-start.13) | collective-permute-done | bytes 139296 | tf_op jit(solution)/shard_map/ppermute | solution.py:392
  232.8 15.3 %attention_send.1 = (bf16[2,2,4,64,128]{4,3,2,1,0:T(8,128)(2,1)}, bf16[2,2,4,64,128]{4,3,2,1,0:T(8,128)(2,1)}, bf16[2,2,4,64,128]{4,3,2,1,0:T(8,128)(2,1)}, bf16...) custom-call(s32[2]{0:T(128)} %and_select_fusion.1.which, ...), custom_call_target="tpu_custom_call" | custom-call | flops 1207959552 | bytes 2883584 | tf_op jit(solution)/shard_map/attention_send/pallas_call | solution.py:297
  250.0 5.0 %collective-permute-start.16 = (bf16[2,2,4,64,128]{4,3,2,1,0:T(8,128)(2,1)}, bf16[2,2,4,64,128]{4,3,2,1,0:T(8,128)(2,1)S(1)}, u32[]{:S(2)}, u32[]{:S(2)}) collective-permute-start(bf16[2,2,4,64,128]{4,3,2,1,0:T(8,128)(2,1)} %get-tuple-element.62), channel_id=1, source_target_pairs={{0,9},{1,8},{2,11},{3,10},{4,13},{5,12},{6,15},{7,14},{8,17},{9,16... | collective-permute-start | bytes 786440 | tf_op jit(solution)/shard_map/ppermute | solution.py:392
  257.0 6.7 %collective-permute-start.18 = (bf16[2,2,4,64,128]{4,3,2,1,0:T(8,128)(2,1)}, bf16[2,2,4,64,128]{4,3,2,1,0:T(8,128)(2,1)S(1)}, u32[]{:S(2)}, u32[]{:S(2)}) collective-permute-start(bf16[2,2,4,64,128]{4,3,2,1,0:T(8,128)(2,1)} %get-tuple-element.64), channel_id=1, source_target_pairs={{0,11},{1,10},{2,9},{3,8},{4,15},{5,14},{6,13},{7,12},{8,19},{9,18... | collective-permute-start | bytes 786440 | tf_op jit(solution)/shard_map/ppermute | solution.py:392
  265.7 12.8 %collective-permute-done.15.refs_0_ = bf16[2,2,4,64,128]{4,3,2,1,0:T(8,128)(2,1)S(1)} collective-permute-done((bf16[2,2,4,64,128]{4,3,2,1,0:T(8,128)(2,1)}, bf16[2,2,4,64,128]{4,3,2,1,0:T(8,128)(2,1)S(1)}, u32[]{:S(2)}, u32[]{:S(2)}) %collective-permute-start.15) | collective-permute-done | bytes 262176 | tf_op jit(solution)/shard_map/ppermute | solution.py:392
  284.7 9.9 %collective-permute-done.17.refs_2_ = bf16[2,2,4,64,128]{4,3,2,1,0:T(8,128)(2,1)S(1)} collective-permute-done((bf16[2,2,4,64,128]{4,3,2,1,0:T(8,128)(2,1)}, bf16[2,2,4,64,128]{4,3,2,1,0:T(8,128)(2,1)S(1)}, u32[]{:S(2)}, u32[]{:S(2)}) %collective-permute-start.17) | collective-permute-done | bytes 262176 | tf_op jit(solution)/shard_map/ppermute | solution.py:392
  294.6 9.0 %collective-permute-start.22 = (bf16[2,2,4,64,128]{4,3,2,1,0:T(8,128)(2,1)}, bf16[2,2,4,64,128]{4,3,2,1,0:T(8,128)(2,1)S(1)}, u32[]{:S(2)}, u32[]{:S(2)}) collective-permute-start(bf16[2,2,4,64,128]{4,3,2,1,0:T(8,128)(2,1)} %get-tuple-element.68), channel_id=1, source_target_pairs={{0,15},{1,14},{2,13},{3,12},{4,11},{5,10},{6,9},{7,8},{8,23},{9,22... | collective-permute-start | bytes 786440 | tf_op jit(solution)/shard_map/ppermute | solution.py:392
  307.3 18.0 %collective-permute-done.20.refs_5_ = bf16[2,2,4,64,128]{4,3,2,1,0:T(8,128)(2,1)S(1)} collective-permute-done((bf16[2,2,4,64,128]{4,3,2,1,0:T(8,128)(2,1)}, bf16[2,2,4,64,128]{4,3,2,1,0:T(8,128)(2,1)S(1)}, u32[]{:S(2)}, u32[]{:S(2)}) %collective-permute-start.20) | collective-permute-done | bytes 262176 | tf_op jit(solution)/shard_map/ppermute | solution.py:392
  329.0 21.7 %collective-permute-done.22.refs_7_ = bf16[2,2,4,64,128]{4,3,2,1,0:T(8,128)(2,1)S(1)} collective-permute-done((bf16[2,2,4,64,128]{4,3,2,1,0:T(8,128)(2,1)}, bf16[2,2,4,64,128]{4,3,2,1,0:T(8,128)(2,1)S(1)}, u32[]{:S(2)}, u32[]{:S(2)}) %collective-permute-start.22) | collective-permute-done | bytes 262176 | tf_op jit(solution)/shard_map/ppermute | solution.py:392
  351.4 8.2 %mix_final.1 = bf16[2,64,4096]{2,1,0:T(8,128)(2,1)} custom-call(s32[2]{0:T(128)} %get-tuple-element.74.which, s32[1]{0:T(128)} %bitcast.me, s32[2]{0:T(128)} %get-tuple-element.73.target, bf16[2,2,4,64,128]{4,3,2,1,0:T(8,128)(2,1)} %copy-done.5, bf16[2,2,4,64,128]{4,3,2,1,0:T(8,128)(2,1)} %copy-done.6, bf16[2,2,4,64,128]{4,3,2,1,0:T(8,128)(2,1)} %copy-done.7, ...), custom_call_target="tpu_custom_call" | custom-call | flops 33554432 | bytes 4194304 | tf_op jit(solution)/shard_map/mix_final/pallas_call | solution.py:354
  (114 shorter events, 59.0 us)
Async XLA Ops:
  2.0 13.4 %collective-permute-start = (bf16[1,2,16,1024]{3,2,1,0:T(8,128)(2,1)S(1)}, bf16[1,2,16,1024]{3,2,1,0:T(8,128)(2,1)S(1)}, u32[]{:S(2)}, u32[]{:S(2)}) collective-permute-start(bf16[1,2,16,1024]{3,2,1,0:T(8,128)(2,1)S(1)} %broadcast_select_fusion), channel_id=1, source_target_pairs={{0,4},{1,5},{2,6},{3,7},{4,0},{5,1},{6,2},{7,3},{8,12},{9,13},{10,... | collective-permute-start | bytes 196616 | tf_op jit(solution)/shard_map/ppermute | solution.py:129
  15.4 70.6 %all-to-all-start = ((bf16[8,2,64,512]{3,2,1,0:T(8,128)(2,1)}), bf16[8,2,64,512]{3,2,1,0:T(8,128)(2,1)S(1)}, u32[]{:S(2)}, u32[]{:S(2)}) async-start(bf16[8,2,64,512]{3,2,1,0:T(8,128)(2,1)} %norm.1), calls=%async_computation | async-start | bytes 2097152 | tf_op jit(solution)/shard_map/all_to_all | solution.py:381
  26.7 24.8 %collective-permute-start.1 = (bf16[2,2,16,1024]{3,2,1,0:T(8,128)(2,1)S(1)}, bf16[2,2,16,1024]{3,2,1,0:T(8,128)(2,1)S(1)}, u32[]{:S(2)}, u32[]{:S(2)}) collective-permute-start(bf16[2,2,16,1024]{3,2,1,0:T(8,128)(2,1)S(1)} %pad_maximum_fusion.1), channel_id=1, source_target_pairs={{0,2},{1,3},{2,0},{3,1},{4,6},{5,7},{6,4},{7,5},{8,10},{9,11},{10,... | collective-permute-start | bytes 393224 | tf_op jit(solution)/shard_map/ppermute | solution.py:129
  28.6 57.4 %collective-permute-start.2 = (bf16[1,2,16,1024]{3,2,1,0:T(8,128)(2,1)S(1)}, bf16[1,2,16,1024]{3,2,1,0:T(8,128)(2,1)S(1)}, u32[]{:S(2)}, u32[]{:S(2)}) collective-permute-start(bf16[1,2,16,1024]{3,2,1,0:T(8,128)(2,1)S(1)} %broadcast_select_fusion), channel_id=1, source_target_pairs={{0,8},{8,16},{16,24},{24,32},{32,40},{40,48},{48,56},{56,64},{64,7... | collective-permute-start | bytes 196616 | tf_op jit(solution)/shard_map/ppermute | solution.py:398
  86.0 16.2 %collective-permute-start.3 = (bf16[4,2,16,1024]{3,2,1,0:T(8,128)(2,1)S(1)}, bf16[4,2,16,1024]{3,2,1,0:T(8,128)(2,1)S(1)}, u32[]{:S(2)}, u32[]{:S(2)}) collective-permute-start(bf16[4,2,16,1024]{3,2,1,0:T(8,128)(2,1)S(1)} %pad_maximum_fusion), channel_id=1, source_target_pairs={{0,1},{1,0},{2,3},{3,2},{4,5},{5,4},{6,7},{7,6},{8,9},{9,8},{10,11... | collective-permute-start | bytes 786440 | tf_op jit(solution)/shard_map/ppermute | solution.py:129
  88.0 14.2 %collective-permute-start.4 = (bf16[1,2,16,1024]{3,2,1,0:T(8,128)(2,1)S(1)}, bf16[1,2,16,1024]{3,2,1,0:T(8,128)(2,1)S(1)}, u32[]{:S(2)}, u32[]{:S(2)}) collective-permute-start(bf16[1,2,16,1024]{3,2,1,0:T(8,128)(2,1)S(1)} %collective-permute-done.2), channel_id=1, source_target_pairs={{0,4},{1,5},{2,6},{3,7},{4,0},{5,1},{6,2},{7,3},{8,12},{9,13},{10,... | collective-permute-start | bytes 196616 | tf_op jit(solution)/shard_map/ppermute | solution.py:129
  103.1 49.9 %all-to-all-start.1 = ((bf16[8,2,64,512]{3,2,1,0:T(8,128)(2,1)}), bf16[8,2,64,512]{3,2,1,0:T(8,128)(2,1)S(1)}, u32[]{:S(2)}, u32[]{:S(2)}) async-start(bf16[8,2,64,512]{3,2,1,0:T(8,128)(2,1)} %attention.1), calls=%async_computation.1 | async-start | bytes 2097152 | tf_op jit(solution)/shard_map/all_to_all | solution.py:381
  114.1 13.6 %collective-permute-start.5 = (bf16[2,2,16,1024]{3,2,1,0:T(8,128)(2,1)S(1)}, bf16[2,2,16,1024]{3,2,1,0:T(8,128)(2,1)S(1)}, u32[]{:S(2)}, u32[]{:S(2)}) collective-permute-start(bf16[2,2,16,1024]{3,2,1,0:T(8,128)(2,1)S(1)} %get-tuple-element.70), channel_id=1, source_target_pairs={{0,2},{1,3},{2,0},{3,1},{4,6},{5,7},{6,4},{7,5},{8,10},{9,11},{10,... | collective-permute-start | bytes 393224 | tf_op jit(solution)/shard_map/ppermute | solution.py:129
  164.1 26.8 %collective-permute-start.7 = (bf16[2,17,16,128]{3,2,1,0:T(8,128)(2,1)}, bf16[2,17,16,128]{3,2,1,0:T(8,128)(2,1)S(1)}, u32[]{:S(2)}, u32[]{:S(2)}) collective-permute-start(bf16[2,17,16,128]{3,2,1,0:T(8,128)(2,1)} %get-tuple-element.53), channel_id=1, source_target_pairs={{0,8},{1,9},{2,10},{3,11},{4,12},{5,13},{6,14},{7,15},{8,16},{9,17... | collective-permute-start | bytes 417800 | tf_op jit(solution)/shard_map/ppermute | solution.py:392
  166.2 30.7 %collective-permute-start.8 = (bf16[2,17,16,128]{3,2,1,0:T(8,128)(2,1)S(1)}, bf16[2,17,16,128]{3,2,1,0:T(8,128)(2,1)S(1)}, u32[]{:S(2)}, u32[]{:S(2)}) collective-permute-start(bf16[2,17,16,128]{3,2,1,0:T(8,128)(2,1)S(1)} %copy-done.28), channel_id=1, source_target_pairs={{0,9},{1,8},{2,11},{3,10},{4,13},{5,12},{6,15},{7,14},{8,17},{9,16... | collective-permute-start | bytes 417800 | tf_op jit(solution)/shard_map/ppermute | solution.py:392
  176.0 28.2 %collective-permute-start.9 = (bf16[2,17,16,128]{3,2,1,0:T(8,128)(2,1)S(1)}, bf16[2,17,16,128]{3,2,1,0:T(8,128)(2,1)S(1)}, u32[]{:S(2)}, u32[]{:S(2)}) collective-permute-start(bf16[2,17,16,128]{3,2,1,0:T(8,128)(2,1)S(1)} %copy-done.26), channel_id=1, source_target_pairs={{0,10},{1,11},{2,8},{3,9},{4,14},{5,15},{6,12},{7,13},{8,18},{9,19... | collective-permute-start | bytes 417800 | tf_op jit(solution)/shard_map/ppermute | solution.py:392
  180.4 31.2 %collective-permute-start.10 = (bf16[2,17,16,128]{3,2,1,0:T(8,128)(2,1)S(1)}, bf16[2,17,16,128]{3,2,1,0:T(8,128)(2,1)S(1)}, u32[]{:S(2)}, u32[]{:S(2)}) collective-permute-start(bf16[2,17,16,128]{3,2,1,0:T(8,128)(2,1)S(1)} %copy-done.23), channel_id=1, source_target_pairs={{0,11},{1,10},{2,9},{3,8},{4,15},{5,14},{6,13},{7,12},{8,19},{9,18... | collective-permute-start | bytes 417800 | tf_op jit(solution)/shard_map/ppermute | solution.py:392
  184.1 27.5 %collective-permute-start.11 = (bf16[2,17,16,128]{3,2,1,0:T(8,128)(2,1)S(1)}, bf16[2,17,16,128]{3,2,1,0:T(8,128)(2,1)S(1)}, u32[]{:S(2)}, u32[]{:S(2)}) collective-permute-start(bf16[2,17,16,128]{3,2,1,0:T(8,128)(2,1)S(1)} %copy-done.21), channel_id=1, source_target_pairs={{0,12},{1,13},{2,14},{3,15},{4,8},{5,9},{6,10},{7,11},{8,20},{9,21... | collective-permute-start | bytes 417800 | tf_op jit(solution)/shard_map/ppermute | solution.py:392
  190.9 20.7 %collective-permute-start.12 = (bf16[2,17,16,128]{3,2,1,0:T(8,128)(2,1)S(1)}, bf16[2,17,16,128]{3,2,1,0:T(8,128)(2,1)S(1)}, u32[]{:S(2)}, u32[]{:S(2)}) collective-permute-start(bf16[2,17,16,128]{3,2,1,0:T(8,128)(2,1)S(1)} %copy-done.19), channel_id=1, source_target_pairs={{0,13},{1,12},{2,15},{3,14},{4,9},{5,8},{6,11},{7,10},{8,21},{9,20... | collective-permute-start | bytes 417800 | tf_op jit(solution)/shard_map/ppermute | solution.py:392
  196.9 31.1 %collective-permute-start.13 = (bf16[2,17,16,128]{3,2,1,0:T(8,128)(2,1)S(1)}, bf16[2,17,16,128]{3,2,1,0:T(8,128)(2,1)S(1)}, u32[]{:S(2)}, u32[]{:S(2)}) collective-permute-start(bf16[2,17,16,128]{3,2,1,0:T(8,128)(2,1)S(1)} %copy-done.17), channel_id=1, source_target_pairs={{0,14},{1,15},{2,12},{3,13},{4,10},{5,11},{6,8},{7,9},{8,22},{9,23... | collective-permute-start | bytes 417800 | tf_op jit(solution)/shard_map/ppermute | solution.py:392
  204.3 27.8 %collective-permute-start.14 = (bf16[2,17,16,128]{3,2,1,0:T(8,128)(2,1)S(1)}, bf16[2,17,16,128]{3,2,1,0:T(8,128)(2,1)S(1)}, u32[]{:S(2)}, u32[]{:S(2)}) collective-permute-start(bf16[2,17,16,128]{3,2,1,0:T(8,128)(2,1)S(1)} %copy-done.15), channel_id=1, source_target_pairs={{0,15},{1,14},{2,13},{3,12},{4,11},{5,10},{6,9},{7,8},{8,23},{9,22... | collective-permute-start | bytes 417800 | tf_op jit(solution)/shard_map/ppermute | solution.py:392
  248.1 30.5 %collective-permute-start.15 = (bf16[2,2,4,64,128]{4,3,2,1,0:T(8,128)(2,1)}, bf16[2,2,4,64,128]{4,3,2,1,0:T(8,128)(2,1)S(1)}, u32[]{:S(2)}, u32[]{:S(2)}) collective-permute-start(bf16[2,2,4,64,128]{4,3,2,1,0:T(8,128)(2,1)} %get-tuple-element.61), channel_id=1, source_target_pairs={{0,8},{1,9},{2,10},{3,11},{4,12},{5,13},{6,14},{7,15},{8,16},{9,17... | collective-permute-start | bytes 786440 | tf_op jit(solution)/shard_map/ppermute | solution.py:392
  250.0 32.7 %collective-permute-start.16 = (bf16[2,2,4,64,128]{4,3,2,1,0:T(8,128)(2,1)}, bf16[2,2,4,64,128]{4,3,2,1,0:T(8,128)(2,1)S(1)}, u32[]{:S(2)}, u32[]{:S(2)}) collective-permute-start(bf16[2,2,4,64,128]{4,3,2,1,0:T(8,128)(2,1)} %get-tuple-element.62), channel_id=1, source_target_pairs={{0,9},{1,8},{2,11},{3,10},{4,13},{5,12},{6,15},{7,14},{8,17},{9,16... | collective-permute-start | bytes 786440 | tf_op jit(solution)/shard_map/ppermute | solution.py:392
  255.1 39.5 %collective-permute-start.17 = (bf16[2,2,4,64,128]{4,3,2,1,0:T(8,128)(2,1)}, bf16[2,2,4,64,128]{4,3,2,1,0:T(8,128)(2,1)S(1)}, u32[]{:S(2)}, u32[]{:S(2)}) collective-permute-start(bf16[2,2,4,64,128]{4,3,2,1,0:T(8,128)(2,1)} %get-tuple-element.63), channel_id=1, source_target_pairs={{0,10},{1,11},{2,8},{3,9},{4,14},{5,15},{6,12},{7,13},{8,18},{9,19... | collective-permute-start | bytes 786440 | tf_op jit(solution)/shard_map/ppermute | solution.py:392
  257.0 50.2 %collective-permute-start.18 = (bf16[2,2,4,64,128]{4,3,2,1,0:T(8,128)(2,1)}, bf16[2,2,4,64,128]{4,3,2,1,0:T(8,128)(2,1)S(1)}, u32[]{:S(2)}, u32[]{:S(2)}) collective-permute-start(bf16[2,2,4,64,128]{4,3,2,1,0:T(8,128)(2,1)} %get-tuple-element.64), channel_id=1, source_target_pairs={{0,11},{1,10},{2,9},{3,8},{4,15},{5,14},{6,13},{7,12},{8,19},{9,18... | collective-permute-start | bytes 786440 | tf_op jit(solution)/shard_map/ppermute | solution.py:392
  263.7 43.5 %collective-permute-start.19 = (bf16[2,2,4,64,128]{4,3,2,1,0:T(8,128)(2,1)}, bf16[2,2,4,64,128]{4,3,2,1,0:T(8,128)(2,1)S(1)}, u32[]{:S(2)}, u32[]{:S(2)}) collective-permute-start(bf16[2,2,4,64,128]{4,3,2,1,0:T(8,128)(2,1)} %get-tuple-element.65), channel_id=1, source_target_pairs={{0,12},{1,13},{2,14},{3,15},{4,8},{5,9},{6,10},{7,11},{8,20},{9,21... | collective-permute-start | bytes 786440 | tf_op jit(solution)/shard_map/ppermute | solution.py:392
  278.6 46.7 %collective-permute-start.20 = (bf16[2,2,4,64,128]{4,3,2,1,0:T(8,128)(2,1)}, bf16[2,2,4,64,128]{4,3,2,1,0:T(8,128)(2,1)S(1)}, u32[]{:S(2)}, u32[]{:S(2)}) collective-permute-start(bf16[2,2,4,64,128]{4,3,2,1,0:T(8,128)(2,1)} %get-tuple-element.66), channel_id=1, source_target_pairs={{0,13},{1,12},{2,15},{3,14},{4,9},{5,8},{6,11},{7,10},{8,21},{9,20... | collective-permute-start | bytes 786440 | tf_op jit(solution)/shard_map/ppermute | solution.py:392
  282.8 46.3 %collective-permute-start.21 = (bf16[2,2,4,64,128]{4,3,2,1,0:T(8,128)(2,1)}, bf16[2,2,4,64,128]{4,3,2,1,0:T(8,128)(2,1)S(1)}, u32[]{:S(2)}, u32[]{:S(2)}) collective-permute-start(bf16[2,2,4,64,128]{4,3,2,1,0:T(8,128)(2,1)} %get-tuple-element.67), channel_id=1, source_target_pairs={{0,14},{1,15},{2,12},{3,13},{4,10},{5,11},{6,8},{7,9},{8,22},{9,23... | collective-permute-start | bytes 786440 | tf_op jit(solution)/shard_map/ppermute | solution.py:392
  294.6 56.1 %collective-permute-start.22 = (bf16[2,2,4,64,128]{4,3,2,1,0:T(8,128)(2,1)}, bf16[2,2,4,64,128]{4,3,2,1,0:T(8,128)(2,1)S(1)}, u32[]{:S(2)}, u32[]{:S(2)}) collective-permute-start(bf16[2,2,4,64,128]{4,3,2,1,0:T(8,128)(2,1)} %get-tuple-element.68), channel_id=1, source_target_pairs={{0,15},{1,14},{2,13},{3,12},{4,11},{5,10},{6,9},{7,8},{8,23},{9,22... | collective-permute-start | bytes 786440 | tf_op jit(solution)/shard_map/ppermute | solution.py:392
  (31 other events, 661.3 us)

commit v4 on v3

--- a/solution.py
+++ b/solution.py
@@ -52,13 +52,12 @@
     count = keys // block
     picks = ids.shape[0] // (2 * count)
     rows = rows_ref[...]
-    query = jnp.dot(rows, wq, preferred_element_type=F32)
-    query = (query * width ** (-0.5)).astype(BF)
-    key = jnp.dot(rows, wk, preferred_element_type=F32).astype(BF)
-    value = jnp.dot(rows, wv, preferred_element_type=F32).astype(BF)
+    raw = jnp.dot(rows, jnp.concatenate([wq, wk, wv], axis=1), preferred_element_type=F32)
+    query = (raw[:, :width] * width ** (-0.5)).astype(BF)
+    key = raw[:, width : 2 * width].astype(BF)
+    value = raw[:, 2 * width :].astype(BF)
     s_ref[...] = lax.dot_general(query, key, (((1,), (1,)), ((), ())), preferred_element_type=F32)
     listed = lax.broadcasted_iota(jnp.int32, (8, keys), 1) // block
-    totals = []
     for i in range(count):
         times = jnp.zeros((8, keys), F32)
         near = [(i - 1) % count, i, (i + 1) % count, 0]
@@ -68,10 +67,10 @@
         at = slice(i * block, (i + 1) * block)
         scores = jnp.where(times > 0, s_ref[at, :], -jnp.inf)
         powers = jnp.exp(scores - jnp.max(scores, axis=1, keepdims=True)) * times
-        totals.append(jnp.sum(powers, axis=1, keepdims=True))
         p_ref[at, :] = powers.astype(BF)
+    value = jnp.concatenate([value, jnp.ones_like(value)], axis=1)
     mixed = jnp.dot(p_ref[...], value, preferred_element_type=F32)
-    return (mixed / jnp.concatenate(totals, axis=0)).astype(BF)
+    return (mixed[:, :width] / mixed[:, width:]).astype(BF)
 
 
 def attention_kernel(which, ids, in_ref, wq_ref, wk_ref, wv_ref, out_ref, *scratch):
@@ -440,10 +439,8 @@
     own = mix_weights(place, own)
     left = partner(left, bits[1])
     back = tie(back, left, own)
-    left = partner(tie(left, back), bits[2])
-    sent = mix_send(first, me, back, own, whole)
-    sent = list(lax.optimization_barrier((*sent, left))[:-1])
-    here = send_on(sent)
+    here = send_on(mix_send(first, me, back, own, whole))
+    left = partner(tie(left, *here), bits[2])
     attended = attention_send(second, me, ids, here, gain, wq, wk, wv)
     left = mix_weights(place, left)
     last = send_on(attended)

time: 361 us -> 358 us (level)
  the two profiles are of different devices: /device:TPU:64 before, /device:TPU:128 now
where the time goes in v4:
time: 358 us; the launch traced here: 357 us
  waiting for transfers between devices  189 us (53%)
  starting transfers between devices  107 us (30%)
  Pallas kernels  49.9 us (14%)
  local copies, waits for them, and re-layouts  7.07 us (2%)
    ppermute x16, waiting for transfers between devices, send_on(): arrived.append(lax.ppermute(block, ('segment', 'fsdp'), pairs))  109 us
    ppermute x6, waiting for transfers between devices, partner(): other = lax.ppermute(value, 'fsdp', [(i, i ^ bit) for i in range(size)])  64.6 us
    ppermute x16, starting transfers between devices, send_on(): arrived.append(lax.ppermute(block, ('segment', 'fsdp'), pairs))  61.2 us
    all_to_all x2, starting transfers between devices, exchange(): lax.all_to_all(value, 'fsdp', split_axis=0, concat_axis=0, tiled=True)  23.2 us
    ppermute x6, starting transfers between devices, partner(): other = lax.ppermute(value, 'fsdp', [(i, i ^ bit) for i in range(size)])  21 us
    ppermute x1, waiting for transfers between devices, shifted(): lax.ppermute(value, 'segment', [(i, (i + 1) % devices) for i in range(dev...  15.4 us
    pallas_call x1, Pallas kernels, attention_send(): pl.pallas_call(attention_send_kernel, out_shape=[jax.ShapeDtypeStruct((sl...  13.3 us
    pallas_call x1, Pallas kernels, attention(): pl.pallas_call(attention_kernel, out_shape=jax.ShapeDtypeStruct(rows.shap...  10.4 us
  transfers between devices with their start and end apart: 25, of which 14 were waited for; matrix products, arithmetic and copies ran while one was open for 1% of the time, Pallas kernels for 5%

profile of v4, /device:TPU:128, one launch (start us, length us, event | category | flops | bytes accessed | tf_op | source)
XLA Modules:
  0.0 356.8 jit_solution(12888948369035640870)
XLA Ops:
  1.4 6.0 %collective-permute-start = (bf16[1,2,16,1024]{3,2,1,0:T(8,128)(2,1)S(1)}, bf16[1,2,16,1024]{3,2,1,0:T(8,128)(2,1)S(1)}, u32[]{:S(2)}, u32[]{:S(2)}) collective-permute-start(bf16[1,2,16,1024]{3,2,1,0:T(8,128)(2,1)S(1)} %broadcast_select_fusion), channel_id=1, source_target_pairs={{0,4},{1,5},{2,6},{3,7},{4,0},{5,1},{6,2},{7,3},{8,12},{9,13},{10,... | collective-permute-start | bytes 196616 | tf_op jit(solution)/shard_map/ppermute | solution.py:128
  11.7 13.4 %all-to-all-start = ((bf16[8,2,64,512]{3,2,1,0:T(8,128)(2,1)}), bf16[8,2,64,512]{3,2,1,0:T(8,128)(2,1)S(1)}, u32[]{:S(2)}, u32[]{:S(2)}) async-start(bf16[8,2,64,512]{3,2,1,0:T(8,128)(2,1)} %norm.1), calls=%async_computation | async-start | bytes 2097152 | tf_op jit(solution)/shard_map/all_to_all | solution.py:380
  25.1 4.3 %collective-permute-start.1 = (bf16[2,2,16,1024]{3,2,1,0:T(8,128)(2,1)S(1)}, bf16[2,2,16,1024]{3,2,1,0:T(8,128)(2,1)S(1)}, u32[]{:S(2)}, u32[]{:S(2)}) collective-permute-start(bf16[2,2,16,1024]{3,2,1,0:T(8,128)(2,1)S(1)} %pad_maximum_fusion.2), channel_id=1, source_target_pairs={{0,2},{1,3},{2,0},{3,1},{4,6},{5,7},{6,4},{7,5},{8,10},{9,11},{10,... | collective-permute-start | bytes 393224 | tf_op jit(solution)/shard_map/ppermute | solution.py:128
  32.1 37.4 %collective-permute-done.1 = bf16[2,2,16,1024]{3,2,1,0:T(8,128)(2,1)S(1)} collective-permute-done((bf16[2,2,16,1024]{3,2,1,0:T(8,128)(2,1)S(1)}, bf16[2,2,16,1024]{3,2,1,0:T(8,128)(2,1)S(1)}, u32[]{:S(2)}, u32[]{:S(2)}) %collective-permute-start.1) | collective-permute-done | bytes 131104 | tf_op jit(solution)/shard_map/ppermute | solution.py:128
  69.6 15.4 %collective-permute-done.2 = bf16[1,2,16,1024]{3,2,1,0:T(8,128)(2,1)S(1)} collective-permute-done((bf16[1,2,16,1024]{3,2,1,0:T(8,128)(2,1)S(1)}, bf16[1,2,16,1024]{3,2,1,0:T(8,128)(2,1)S(1)}, u32[]{:S(2)}, u32[]{:S(2)}) %collective-permute-start.2) | collective-permute-done | bytes 65568 | tf_op jit(solution)/shard_map/ppermute | solution.py:397
  89.6 10.4 %attention.1 = bf16[8,2,64,512]{3,2,1,0:T(8,128)(2,1)} custom-call(s32[2]{0:T(128)} %and_select_fusion.which, s32[32]{0:T(128)} %reshape_squeeze.3.ids, bf16[8,2,64,512]{3,2,1,0:T(8,128)(2,1)} %copy-done.3, bf16[2,4,128,128]{3,2,1,0:T(8,128)(2,1)} %bitcast.20, bf16[2,4,128,128]{3,2,1,0:T(8,128)(2,1)} %bitcast.22, bf16[2,4,128,128]{3,2,1,0:T(8,128)(2,1)} %bitcast.24), custom_call_target="tpu_custom_call" | custom-call | flops 1207959552 | bytes 2883584 | tf_op jit(solution)/shard_map/attention/pallas_call | solution.py:104
  100.8 9.8 %all-to-all-start.1 = ((bf16[8,2,64,512]{3,2,1,0:T(8,128)(2,1)}), bf16[8,2,64,512]{3,2,1,0:T(8,128)(2,1)S(1)}, u32[]{:S(2)}, u32[]{:S(2)}) async-start(bf16[8,2,64,512]{3,2,1,0:T(8,128)(2,1)} %attention.1), calls=%async_computation.1 | async-start | bytes 2097152 | tf_op jit(solution)/shard_map/all_to_all | solution.py:380
  110.7 4.3 %collective-permute-start.5 = (bf16[2,2,16,1024]{3,2,1,0:T(8,128)(2,1)S(1)}, bf16[2,2,16,1024]{3,2,1,0:T(8,128)(2,1)S(1)}, u32[]{:S(2)}, u32[]{:S(2)}) collective-permute-start(bf16[2,2,16,1024]{3,2,1,0:T(8,128)(2,1)S(1)} %get-tuple-element.54), channel_id=1, source_target_pairs={{0,2},{1,3},{2,0},{3,1},{4,6},{5,7},{6,4},{7,5},{8,10},{9,11},{10,... | collective-permute-start | bytes 393224 | tf_op jit(solution)/shard_map/ppermute | solution.py:128
  116.2 27.2 %collective-permute-done.5 = bf16[2,2,16,1024]{3,2,1,0:T(8,128)(2,1)S(1)} collective-permute-done((bf16[2,2,16,1024]{3,2,1,0:T(8,128)(2,1)S(1)}, bf16[2,2,16,1024]{3,2,1,0:T(8,128)(2,1)S(1)}, u32[]{:S(2)}, u32[]{:S(2)}) %collective-permute-start.5) | collective-permute-done | bytes 131104 | tf_op jit(solution)/shard_map/ppermute | solution.py:128
  147.2 9.1 %mix_send.1 = (bf16[2,17,16,128]{3,2,1,0:T(8,128)(2,1)}, bf16[2,17,16,128]{3,2,1,0:T(8,128)(2,1)}, bf16[2,17,16,128]{3,2,1,0:T(8,128)(2,1)}, bf16[2,17,16,128]{3...) custom-call(s32[2]{0:T(128)} %and_select_fusion.which, ...), custom_call_target="tpu_custom_call" | custom-call | flops 33554432 | bytes 4194304 | tf_op jit(solution)/shard_map/mix_send/pallas_call | solution.py:230
  158.2 9.2 %collective-permute-start.7 = (bf16[2,17,16,128]{3,2,1,0:T(8,128)(2,1)}, bf16[2,17,16,128]{3,2,1,0:T(8,128)(2,1)S(1)}, u32[]{:S(2)}, u32[]{:S(2)}) collective-permute-start(bf16[2,17,16,128]{3,2,1,0:T(8,128)(2,1)} %get-tuple-element.37), channel_id=1, source_target_pairs={{0,9},{1,8},{2,11},{3,10},{4,13},{5,12},{6,15},{7,14},{8,17},{9,16... | collective-permute-start | bytes 417800 | tf_op jit(solution)/shard_map/ppermute | solution.py:391
  170.9 6.2 %collective-permute-start.9 = (bf16[2,17,16,128]{3,2,1,0:T(8,128)(2,1)}, bf16[2,17,16,128]{3,2,1,0:T(8,128)(2,1)S(1)}, u32[]{:S(2)}, u32[]{:S(2)}) collective-permute-start(bf16[2,17,16,128]{3,2,1,0:T(8,128)(2,1)} %get-tuple-element.39), channel_id=1, source_target_pairs={{0,11},{1,10},{2,9},{3,8},{4,15},{5,14},{6,13},{7,12},{8,19},{9,18... | collective-permute-start | bytes 417800 | tf_op jit(solution)/shard_map/ppermute | solution.py:391
  177.1 6.5 %collective-permute-start.10 = (bf16[2,17,16,128]{3,2,1,0:T(8,128)(2,1)}, bf16[2,17,16,128]{3,2,1,0:T(8,128)(2,1)S(1)}, u32[]{:S(2)}, u32[]{:S(2)}) collective-permute-start(bf16[2,17,16,128]{3,2,1,0:T(8,128)(2,1)} %get-tuple-element.40), channel_id=1, source_target_pairs={{0,12},{1,13},{2,14},{3,15},{4,8},{5,9},{6,10},{7,11},{8,20},{9,21... | collective-permute-start | bytes 417800 | tf_op jit(solution)/shard_map/ppermute | solution.py:391
  186.8 5.5 %collective-permute-start.12 = (bf16[2,17,16,128]{3,2,1,0:T(8,128)(2,1)}, bf16[2,17,16,128]{3,2,1,0:T(8,128)(2,1)S(1)}, u32[]{:S(2)}, u32[]{:S(2)}) collective-permute-start(bf16[2,17,16,128]{3,2,1,0:T(8,128)(2,1)} %get-tuple-element.42), channel_id=1, source_target_pairs={{0,14},{1,15},{2,12},{3,13},{4,10},{5,11},{6,8},{7,9},{8,22},{9,23... | collective-permute-start | bytes 417800 | tf_op jit(solution)/shard_map/ppermute | solution.py:391
  197.6 13.1 %collective-permute-done.10.refs_4_ = bf16[2,17,16,128]{3,2,1,0:T(8,128)(2,1)S(1)} collective-permute-done((bf16[2,17,16,128]{3,2,1,0:T(8,128)(2,1)}, bf16[2,17,16,128]{3,2,1,0:T(8,128)(2,1)S(1)}, u32[]{:S(2)}, u32[]{:S(2)}) %collective-permute-start.10) | collective-permute-done | bytes 139296 | tf_op jit(solution)/shard_map/ppermute | solution.py:391
  210.7 12.5 %collective-permute-done.13.refs_7_ = bf16[2,17,16,128]{3,2,1,0:T(8,128)(2,1)S(1)} collective-permute-done((bf16[2,17,16,128]{3,2,1,0:T(8,128)(2,1)}, bf16[2,17,16,128]{3,2,1,0:T(8,128)(2,1)S(1)}, u32[]{:S(2)}, u32[]{:S(2)}) %collective-permute-start.13) | collective-permute-done | bytes 139296 | tf_op jit(solution)/shard_map/ppermute | solution.py:391
  223.9 13.3 %attention_send.1 = (bf16[2,2,4,64,128]{4,3,2,1,0:T(8,128)(2,1)}, bf16[2,2,4,64,128]{4,3,2,1,0:T(8,128)(2,1)}, bf16[2,2,4,64,128]{4,3,2,1,0:T(8,128)(2,1)}, bf16...) custom-call(s32[2]{0:T(128)} %and_select_fusion.1.which, ...), custom_call_target="tpu_custom_call" | custom-call | flops 1207959552 | bytes 2883584 | tf_op jit(solution)/shard_map/attention_send/pallas_call | solution.py:296
  241.1 4.8 %collective-permute-start.16 = (bf16[2,2,4,64,128]{4,3,2,1,0:T(8,128)(2,1)}, bf16[2,2,4,64,128]{4,3,2,1,0:T(8,128)(2,1)S(1)}, u32[]{:S(2)}, u32[]{:S(2)}) collective-permute-start(bf16[2,2,4,64,128]{4,3,2,1,0:T(8,128)(2,1)} %get-tuple-element.46), channel_id=1, source_target_pairs={{0,10},{1,11},{2,8},{3,9},{4,14},{5,15},{6,12},{7,13},{8,18},{9,19... | collective-permute-start | bytes 786440 | tf_op jit(solution)/shard_map/ppermute | solution.py:391
  247.8 5.2 %collective-permute-start.17 = (bf16[2,2,4,64,128]{4,3,2,1,0:T(8,128)(2,1)}, bf16[2,2,4,64,128]{4,3,2,1,0:T(8,128)(2,1)S(1)}, u32[]{:S(2)}, u32[]{:S(2)}) collective-permute-start(bf16[2,2,4,64,128]{4,3,2,1,0:T(8,128)(2,1)} %get-tuple-element.47), channel_id=1, source_target_pairs={{0,11},{1,10},{2,9},{3,8},{4,15},{5,14},{6,13},{7,12},{8,19},{9,18... | collective-permute-start | bytes 786440 | tf_op jit(solution)/shard_map/ppermute | solution.py:391
  253.0 35.8 %collective-permute-done.14.refs_0_ = bf16[2,2,4,64,128]{4,3,2,1,0:T(8,128)(2,1)S(1)} collective-permute-done((bf16[2,2,4,64,128]{4,3,2,1,0:T(8,128)(2,1)}, bf16[2,2,4,64,128]{4,3,2,1,0:T(8,128)(2,1)S(1)}, u32[]{:S(2)}, u32[]{:S(2)}) %collective-permute-start.14) | collective-permute-done | bytes 262176 | tf_op jit(solution)/shard_map/ppermute | solution.py:391
  309.4 4.5 %collective-permute-done.19.refs_5_ = bf16[2,2,4,64,128]{4,3,2,1,0:T(8,128)(2,1)S(1)} collective-permute-done((bf16[2,2,4,64,128]{4,3,2,1,0:T(8,128)(2,1)}, bf16[2,2,4,64,128]{4,3,2,1,0:T(8,128)(2,1)S(1)}, u32[]{:S(2)}, u32[]{:S(2)}) %collective-permute-start.19) | collective-permute-done | bytes 262176 | tf_op jit(solution)/shard_map/ppermute | solution.py:391
  313.9 12.4 %collective-permute-done.20.refs_6_ = bf16[2,2,4,64,128]{4,3,2,1,0:T(8,128)(2,1)S(1)} collective-permute-done((bf16[2,2,4,64,128]{4,3,2,1,0:T(8,128)(2,1)}, bf16[2,2,4,64,128]{4,3,2,1,0:T(8,128)(2,1)S(1)}, u32[]{:S(2)}, u32[]{:S(2)}) %collective-permute-start.20) | collective-permute-done | bytes 262176 | tf_op jit(solution)/shard_map/ppermute | solution.py:391
  326.3 21.6 %collective-permute-done.21.refs_7_ = bf16[2,2,4,64,128]{4,3,2,1,0:T(8,128)(2,1)S(1)} collective-permute-done((bf16[2,2,4,64,128]{4,3,2,1,0:T(8,128)(2,1)}, bf16[2,2,4,64,128]{4,3,2,1,0:T(8,128)(2,1)S(1)}, u32[]{:S(2)}, u32[]{:S(2)}) %collective-permute-start.21) | collective-permute-done | bytes 262176 | tf_op jit(solution)/shard_map/ppermute | solution.py:391
  348.6 8.2 %mix_final.1 = bf16[2,64,4096]{2,1,0:T(8,128)(2,1)} custom-call(s32[2]{0:T(128)} %get-tuple-element.58.which, s32[1]{0:T(128)} %bitcast.me, s32[2]{0:T(128)} %get-tuple-element.57.target, bf16[2,2,4,64,128]{4,3,2,1,0:T(8,128)(2,1)} %copy-done.4, bf16[2,2,4,64,128]{4,3,2,1,0:T(8,128)(2,1)} %copy-done.5, bf16[2,2,4,64,128]{4,3,2,1,0:T(8,128)(2,1)} %copy-done.6, ...), custom_call_target="tpu_custom_call" | custom-call | flops 33554432 | bytes 4194304 | tf_op jit(solution)/shard_map/mix_final/pallas_call | solution.py:353
  (99 shorter events, 60.3 us)
Async XLA Ops:
  11.7 73.2 %all-to-all-start = ((bf16[8,2,64,512]{3,2,1,0:T(8,128)(2,1)}), bf16[8,2,64,512]{3,2,1,0:T(8,128)(2,1)S(1)}, u32[]{:S(2)}, u32[]{:S(2)}) async-start(bf16[8,2,64,512]{3,2,1,0:T(8,128)(2,1)} %norm.1), calls=%async_computation | async-start | bytes 2097152 | tf_op jit(solution)/shard_map/all_to_all | solution.py:380
  25.1 44.4 %collective-permute-start.1 = (bf16[2,2,16,1024]{3,2,1,0:T(8,128)(2,1)S(1)}, bf16[2,2,16,1024]{3,2,1,0:T(8,128)(2,1)S(1)}, u32[]{:S(2)}, u32[]{:S(2)}) collective-permute-start(bf16[2,2,16,1024]{3,2,1,0:T(8,128)(2,1)S(1)} %pad_maximum_fusion.2), channel_id=1, source_target_pairs={{0,2},{1,3},{2,0},{3,1},{4,6},{5,7},{6,4},{7,5},{8,10},{9,11},{10,... | collective-permute-start | bytes 393224 | tf_op jit(solution)/shard_map/ppermute | solution.py:128
  29.4 55.6 %collective-permute-start.2 = (bf16[1,2,16,1024]{3,2,1,0:T(8,128)(2,1)S(1)}, bf16[1,2,16,1024]{3,2,1,0:T(8,128)(2,1)S(1)}, u32[]{:S(2)}, u32[]{:S(2)}) collective-permute-start(bf16[1,2,16,1024]{3,2,1,0:T(8,128)(2,1)S(1)} %broadcast_select_fusion), channel_id=1, source_target_pairs={{0,8},{8,16},{16,24},{24,32},{32,40},{40,48},{48,56},{56,64},{64,7... | collective-permute-start | bytes 196616 | tf_op jit(solution)/shard_map/ppermute | solution.py:397
  85.0 15.0 %collective-permute-start.3 = (bf16[4,2,16,1024]{3,2,1,0:T(8,128)(2,1)S(1)}, bf16[4,2,16,1024]{3,2,1,0:T(8,128)(2,1)S(1)}, u32[]{:S(2)}, u32[]{:S(2)}) collective-permute-start(bf16[4,2,16,1024]{3,2,1,0:T(8,128)(2,1)S(1)} %pad_maximum_fusion.1), channel_id=1, source_target_pairs={{0,1},{1,0},{2,3},{3,2},{4,5},{5,4},{6,7},{7,6},{8,9},{9,8},{10,11... | collective-permute-start | bytes 786440 | tf_op jit(solution)/shard_map/ppermute | solution.py:128
  87.6 12.3 %collective-permute-start.4 = (bf16[1,2,16,1024]{3,2,1,0:T(8,128)(2,1)S(1)}, bf16[1,2,16,1024]{3,2,1,0:T(8,128)(2,1)S(1)}, u32[]{:S(2)}, u32[]{:S(2)}) collective-permute-start(bf16[1,2,16,1024]{3,2,1,0:T(8,128)(2,1)S(1)} %collective-permute-done.2), channel_id=1, source_target_pairs={{0,4},{1,5},{2,6},{3,7},{4,0},{5,1},{6,2},{7,3},{8,12},{9,13},{10,... | collective-permute-start | bytes 196616 | tf_op jit(solution)/shard_map/ppermute | solution.py:128
  100.8 45.4 %all-to-all-start.1 = ((bf16[8,2,64,512]{3,2,1,0:T(8,128)(2,1)}), bf16[8,2,64,512]{3,2,1,0:T(8,128)(2,1)S(1)}, u32[]{:S(2)}, u32[]{:S(2)}) async-start(bf16[8,2,64,512]{3,2,1,0:T(8,128)(2,1)} %attention.1), calls=%async_computation.1 | async-start | bytes 2097152 | tf_op jit(solution)/shard_map/all_to_all | solution.py:380
  110.7 32.7 %collective-permute-start.5 = (bf16[2,2,16,1024]{3,2,1,0:T(8,128)(2,1)S(1)}, bf16[2,2,16,1024]{3,2,1,0:T(8,128)(2,1)S(1)}, u32[]{:S(2)}, u32[]{:S(2)}) collective-permute-start(bf16[2,2,16,1024]{3,2,1,0:T(8,128)(2,1)S(1)} %get-tuple-element.54), channel_id=1, source_target_pairs={{0,2},{1,3},{2,0},{3,1},{4,6},{5,7},{6,4},{7,5},{8,10},{9,11},{10,... | collective-permute-start | bytes 393224 | tf_op jit(solution)/shard_map/ppermute | solution.py:128
  156.3 27.3 %collective-permute-start.6 = (bf16[2,17,16,128]{3,2,1,0:T(8,128)(2,1)}, bf16[2,17,16,128]{3,2,1,0:T(8,128)(2,1)S(1)}, u32[]{:S(2)}, u32[]{:S(2)}) collective-permute-start(bf16[2,17,16,128]{3,2,1,0:T(8,128)(2,1)} %get-tuple-element.36), channel_id=1, source_target_pairs={{0,8},{1,9},{2,10},{3,11},{4,12},{5,13},{6,14},{7,15},{8,16},{9,17... | collective-permute-start | bytes 417800 | tf_op jit(solution)/shard_map/ppermute | solution.py:391
  158.2 28.6 %collective-permute-start.7 = (bf16[2,17,16,128]{3,2,1,0:T(8,128)(2,1)}, bf16[2,17,16,128]{3,2,1,0:T(8,128)(2,1)S(1)}, u32[]{:S(2)}, u32[]{:S(2)}) collective-permute-start(bf16[2,17,16,128]{3,2,1,0:T(8,128)(2,1)} %get-tuple-element.37), channel_id=1, source_target_pairs={{0,9},{1,8},{2,11},{3,10},{4,13},{5,12},{6,15},{7,14},{8,17},{9,16... | collective-permute-start | bytes 417800 | tf_op jit(solution)/shard_map/ppermute | solution.py:391
  167.4 25.3 %collective-permute-start.8 = (bf16[2,17,16,128]{3,2,1,0:T(8,128)(2,1)}, bf16[2,17,16,128]{3,2,1,0:T(8,128)(2,1)S(1)}, u32[]{:S(2)}, u32[]{:S(2)}) collective-permute-start(bf16[2,17,16,128]{3,2,1,0:T(8,128)(2,1)} %get-tuple-element.38), channel_id=1, source_target_pairs={{0,10},{1,11},{2,8},{3,9},{4,14},{5,15},{6,12},{7,13},{8,18},{9,19... | collective-permute-start | bytes 417800 | tf_op jit(solution)/shard_map/ppermute | solution.py:391
  170.9 26.7 %collective-permute-start.9 = (bf16[2,17,16,128]{3,2,1,0:T(8,128)(2,1)}, bf16[2,17,16,128]{3,2,1,0:T(8,128)(2,1)S(1)}, u32[]{:S(2)}, u32[]{:S(2)}) collective-permute-start(bf16[2,17,16,128]{3,2,1,0:T(8,128)(2,1)} %get-tuple-element.39), channel_id=1, source_target_pairs={{0,11},{1,10},{2,9},{3,8},{4,15},{5,14},{6,13},{7,12},{8,19},{9,18... | collective-permute-start | bytes 417800 | tf_op jit(solution)/shard_map/ppermute | solution.py:391
  177.1 33.6 %collective-permute-start.10 = (bf16[2,17,16,128]{3,2,1,0:T(8,128)(2,1)}, bf16[2,17,16,128]{3,2,1,0:T(8,128)(2,1)S(1)}, u32[]{:S(2)}, u32[]{:S(2)}) collective-permute-start(bf16[2,17,16,128]{3,2,1,0:T(8,128)(2,1)} %get-tuple-element.40), channel_id=1, source_target_pairs={{0,12},{1,13},{2,14},{3,15},{4,8},{5,9},{6,10},{7,11},{8,20},{9,21... | collective-permute-start | bytes 417800 | tf_op jit(solution)/shard_map/ppermute | solution.py:391
  183.6 27.1 %collective-permute-start.11 = (bf16[2,17,16,128]{3,2,1,0:T(8,128)(2,1)}, bf16[2,17,16,128]{3,2,1,0:T(8,128)(2,1)S(1)}, u32[]{:S(2)}, u32[]{:S(2)}) collective-permute-start(bf16[2,17,16,128]{3,2,1,0:T(8,128)(2,1)} %get-tuple-element.41), channel_id=1, source_target_pairs={{0,13},{1,12},{2,15},{3,14},{4,9},{5,8},{6,11},{7,10},{8,21},{9,20... | collective-permute-start | bytes 417800 | tf_op jit(solution)/shard_map/ppermute | solution.py:391
  186.8 23.9 %collective-permute-start.12 = (bf16[2,17,16,128]{3,2,1,0:T(8,128)(2,1)}, bf16[2,17,16,128]{3,2,1,0:T(8,128)(2,1)S(1)}, u32[]{:S(2)}, u32[]{:S(2)}) collective-permute-start(bf16[2,17,16,128]{3,2,1,0:T(8,128)(2,1)} %get-tuple-element.42), channel_id=1, source_target_pairs={{0,14},{1,15},{2,12},{3,13},{4,10},{5,11},{6,8},{7,9},{8,22},{9,23... | collective-permute-start | bytes 417800 | tf_op jit(solution)/shard_map/ppermute | solution.py:391
  192.8 30.5 %collective-permute-start.13 = (bf16[2,17,16,128]{3,2,1,0:T(8,128)(2,1)}, bf16[2,17,16,128]{3,2,1,0:T(8,128)(2,1)S(1)}, u32[]{:S(2)}, u32[]{:S(2)}) collective-permute-start(bf16[2,17,16,128]{3,2,1,0:T(8,128)(2,1)} %get-tuple-element.43), channel_id=1, source_target_pairs={{0,15},{1,14},{2,13},{3,12},{4,11},{5,10},{6,9},{7,8},{8,23},{9,22... | collective-permute-start | bytes 417800 | tf_op jit(solution)/shard_map/ppermute | solution.py:391
  237.2 51.6 %collective-permute-start.14 = (bf16[2,2,4,64,128]{4,3,2,1,0:T(8,128)(2,1)}, bf16[2,2,4,64,128]{4,3,2,1,0:T(8,128)(2,1)S(1)}, u32[]{:S(2)}, u32[]{:S(2)}) collective-permute-start(bf16[2,2,4,64,128]{4,3,2,1,0:T(8,128)(2,1)} %get-tuple-element.44), channel_id=1, source_target_pairs={{0,8},{1,9},{2,10},{3,11},{4,12},{5,13},{6,14},{7,15},{8,16},{9,17... | collective-permute-start | bytes 786440 | tf_op jit(solution)/shard_map/ppermute | solution.py:391
  239.2 51.6 %collective-permute-start.15 = (bf16[2,2,4,64,128]{4,3,2,1,0:T(8,128)(2,1)}, bf16[2,2,4,64,128]{4,3,2,1,0:T(8,128)(2,1)S(1)}, u32[]{:S(2)}, u32[]{:S(2)}) collective-permute-start(bf16[2,2,4,64,128]{4,3,2,1,0:T(8,128)(2,1)} %get-tuple-element.45), channel_id=1, source_target_pairs={{0,9},{1,8},{2,11},{3,10},{4,13},{5,12},{6,15},{7,14},{8,17},{9,16... | collective-permute-start | bytes 786440 | tf_op jit(solution)/shard_map/ppermute | solution.py:391
  241.1 53.4 %collective-permute-start.16 = (bf16[2,2,4,64,128]{4,3,2,1,0:T(8,128)(2,1)}, bf16[2,2,4,64,128]{4,3,2,1,0:T(8,128)(2,1)S(1)}, u32[]{:S(2)}, u32[]{:S(2)}) collective-permute-start(bf16[2,2,4,64,128]{4,3,2,1,0:T(8,128)(2,1)} %get-tuple-element.46), channel_id=1, source_target_pairs={{0,10},{1,11},{2,8},{3,9},{4,14},{5,15},{6,12},{7,13},{8,18},{9,19... | collective-permute-start | bytes 786440 | tf_op jit(solution)/shard_map/ppermute | solution.py:391
  245.9 50.6 %collective-permute-start.22 = (bf16[4,2,16,1024]{3,2,1,0:T(8,128)(2,1)S(1)}, bf16[4,2,16,1024]{3,2,1,0:T(8,128)(2,1)S(1)}, u32[]{:S(2)}, u32[]{:S(2)}) collective-permute-start(bf16[4,2,16,1024]{3,2,1,0:T(8,128)(2,1)S(1)} %constant_dynamic-update-slice_fusion.4), channel_id=1, source_target_pairs={{0,1},{1,0},{2,3},{3,2},{4,5},{5,4},{6,7},{7,6},{8,9},{9,8},{10,11... | collective-permute-start | bytes 786440 | tf_op jit(solution)/shard_map/ppermute | solution.py:128
  247.8 58.2 %collective-permute-start.17 = (bf16[2,2,4,64,128]{4,3,2,1,0:T(8,128)(2,1)}, bf16[2,2,4,64,128]{4,3,2,1,0:T(8,128)(2,1)S(1)}, u32[]{:S(2)}, u32[]{:S(2)}) collective-permute-start(bf16[2,2,4,64,128]{4,3,2,1,0:T(8,128)(2,1)} %get-tuple-element.47), channel_id=1, source_target_pairs={{0,11},{1,10},{2,9},{3,8},{4,15},{5,14},{6,13},{7,12},{8,19},{9,18... | collective-permute-start | bytes 786440 | tf_op jit(solution)/shard_map/ppermute | solution.py:391
  288.8 20.6 %collective-permute-start.18 = (bf16[2,2,4,64,128]{4,3,2,1,0:T(8,128)(2,1)}, bf16[2,2,4,64,128]{4,3,2,1,0:T(8,128)(2,1)S(1)}, u32[]{:S(2)}, u32[]{:S(2)}) collective-permute-start(bf16[2,2,4,64,128]{4,3,2,1,0:T(8,128)(2,1)} %get-tuple-element.48), channel_id=1, source_target_pairs={{0,12},{1,13},{2,14},{3,15},{4,8},{5,9},{6,10},{7,11},{8,20},{9,21... | collective-permute-start | bytes 786440 | tf_op jit(solution)/shard_map/ppermute | solution.py:391
  290.7 23.1 %collective-permute-start.19 = (bf16[2,2,4,64,128]{4,3,2,1,0:T(8,128)(2,1)}, bf16[2,2,4,64,128]{4,3,2,1,0:T(8,128)(2,1)S(1)}, u32[]{:S(2)}, u32[]{:S(2)}) collective-permute-start(bf16[2,2,4,64,128]{4,3,2,1,0:T(8,128)(2,1)} %get-tuple-element.49), channel_id=1, source_target_pairs={{0,13},{1,12},{2,15},{3,14},{4,9},{5,8},{6,11},{7,10},{8,21},{9,20... | collective-permute-start | bytes 786440 | tf_op jit(solution)/shard_map/ppermute | solution.py:391
  294.5 31.8 %collective-permute-start.20 = (bf16[2,2,4,64,128]{4,3,2,1,0:T(8,128)(2,1)}, bf16[2,2,4,64,128]{4,3,2,1,0:T(8,128)(2,1)S(1)}, u32[]{:S(2)}, u32[]{:S(2)}) collective-permute-start(bf16[2,2,4,64,128]{4,3,2,1,0:T(8,128)(2,1)} %get-tuple-element.50), channel_id=1, source_target_pairs={{0,14},{1,15},{2,12},{3,13},{4,10},{5,11},{6,8},{7,9},{8,22},{9,23... | collective-permute-start | bytes 786440 | tf_op jit(solution)/shard_map/ppermute | solution.py:391
  296.4 51.4 %collective-permute-start.21 = (bf16[2,2,4,64,128]{4,3,2,1,0:T(8,128)(2,1)}, bf16[2,2,4,64,128]{4,3,2,1,0:T(8,128)(2,1)S(1)}, u32[]{:S(2)}, u32[]{:S(2)}) collective-permute-start(bf16[2,2,4,64,128]{4,3,2,1,0:T(8,128)(2,1)} %get-tuple-element.51), channel_id=1, source_target_pairs={{0,15},{1,14},{2,13},{3,12},{4,11},{5,10},{6,9},{7,8},{8,23},{9,22... | collective-permute-start | bytes 786440 | tf_op jit(solution)/shard_map/ppermute | solution.py:391
  (24 other events, 391.2 us)

commit v5 on v4

--- a/solution.py
+++ b/solution.py
@@ -46,7 +46,7 @@
     )(which, x, gain)
 
 
-def attend(wq, wk, wv, rows_ref, s_ref, p_ref, block, ids, base):
+def attend(wq, wk, wv, rows_ref, s_ref, p_ref, t_ref, block, ids, base):
     keys = s_ref.shape[1]
     width = rows_ref.shape[1]
     count = keys // block
@@ -57,13 +57,19 @@
     key = raw[:, width : 2 * width].astype(BF)
     value = raw[:, 2 * width :].astype(BF)
     s_ref[...] = lax.dot_general(query, key, (((1,), (1,)), ((), ())), preferred_element_type=F32)
-    listed = lax.broadcasted_iota(jnp.int32, (8, keys), 1) // block
+
+    @pl.when(pl.program_id(1) == 0)
+    def _():
+        listed = lax.broadcasted_iota(jnp.int32, (8, keys), 1) // block
+        for i in range(count):
+            times = jnp.zeros((8, keys), F32)
+            near = [(i - 1) % count, i, (i + 1) % count, 0]
+            for b in near + [ids[base + i * picks + r] for r in range(picks)]:
+                times = times + (listed == b).astype(F32)
+            t_ref[i] = times
+
     for i in range(count):
-        times = jnp.zeros((8, keys), F32)
-        near = [(i - 1) % count, i, (i + 1) % count, 0]
-        for b in near + [ids[base + i * picks + r] for r in range(picks)]:
-            times = times + (listed == b).astype(F32)
-        times = times[:1]
+        times = t_ref[i, :1]
         at = slice(i * block, (i + 1) * block)
         scores = jnp.where(times > 0, s_ref[at, :], -jnp.inf)
         powers = jnp.exp(scores - jnp.max(scores, axis=1, keepdims=True)) * times
@@ -83,7 +89,12 @@
 
 
 def attention_scratch(rows, width):
-    return [pltpu.VMEM((rows, width), BF), pltpu.VMEM((rows, rows), F32), pltpu.VMEM((rows, rows), BF)]
+    return [
+        pltpu.VMEM((rows, width), BF),
+        pltpu.VMEM((rows, rows), F32),
+        pltpu.VMEM((rows, rows), BF),
+        pltpu.VMEM((rows // BLK, 8, rows), F32),
+    ]
 
 
 def attention_cost(slots, heads, count, block, width):
@@ -250,10 +261,10 @@
 
 
 def attention_send_kernel(which, me, ids, *refs):
-    size = (len(refs) - 7) // 2
+    size = (len(refs) - 8) // 2
     in_refs, rest = refs[:size], refs[size:]
     gain_ref, wq_ref, wk_ref, wv_ref = rest[:4]
-    out_refs, scratch = rest[4:-3], rest[-3:]
+    out_refs, scratch = rest[4:-4], rest[-4:]
     rows_ref = scratch[0]
     slot, head = pl.program_id(0), pl.program_id(1)
     block, width = out_refs[0].shape[1:]
@@ -442,8 +453,9 @@
     here = send_on(mix_send(first, me, back, own, whole))
     left = partner(tie(left, *here), bits[2])
     attended = attention_send(second, me, ids, here, gain, wq, wk, wv)
+    *attended, left = lax.optimization_barrier((*attended, left))
+    last = send_on(attended)
     left = mix_weights(place, left)
-    last = send_on(attended)
     done = mix_final(mixing, me, target, last, left)
     return done[:, None]
 

time: 358 us -> 359 us (level)
  the two profiles are of different devices: /device:TPU:128 before, /device:TPU:32 now
where the time goes in v5:
time: 359 us; the launch traced here: 357 us
  waiting for transfers between devices  174 us (48%)
  starting transfers between devices  122 us (34%)
  Pallas kernels  52 us (14%)
  local copies, waits for them, and re-layouts  6.43 us (2%)
    ppermute x16, waiting for transfers between devices, send_on(): arrived.append(lax.ppermute(block, ('segment', 'fsdp'), pairs))  93.5 us
    ppermute x16, starting transfers between devices, send_on(): arrived.append(lax.ppermute(block, ('segment', 'fsdp'), pairs))  64.8 us
    ppermute x6, waiting for transfers between devices, partner(): other = lax.ppermute(value, 'fsdp', [(i, i ^ bit) for i in range(size)])  60.9 us
    ppermute x6, starting transfers between devices, partner(): other = lax.ppermute(value, 'fsdp', [(i, i ^ bit) for i in range(size)])  39.4 us
    all_to_all x2, waiting for transfers between devices, exchange(): lax.all_to_all(value, 'fsdp', split_axis=0, concat_axis=0, tiled=True)  19.1 us
    all_to_all x2, starting transfers between devices, exchange(): lax.all_to_all(value, 'fsdp', split_axis=0, concat_axis=0, tiled=True)  15.5 us
    pallas_call x1, Pallas kernels, attention_send(): pl.pallas_call(attention_send_kernel, out_shape=[jax.ShapeDtypeStruct((sl...  14.4 us
    pallas_call x1, Pallas kernels, attention(): pl.pallas_call(attention_kernel, out_shape=jax.ShapeDtypeStruct(rows.shap...  11.4 us
  transfers between devices with their start and end apart: 25, of which 15 were waited for; matrix products, arithmetic and copies ran while one was open for 1% of the time, Pallas kernels for 10%

profile of v5, /device:TPU:32, one launch (start us, length us, event | category | flops | bytes accessed | tf_op | source)
XLA Modules:
  0.0 357.4 jit_solution(16126325225730244232)
XLA Ops:
  2.0 9.1 %collective-permute-start = (bf16[1,2,16,1024]{3,2,1,0:T(8,128)(2,1)S(1)}, bf16[1,2,16,1024]{3,2,1,0:T(8,128)(2,1)S(1)}, u32[]{:S(2)}, u32[]{:S(2)}) collective-permute-start(bf16[1,2,16,1024]{3,2,1,0:T(8,128)(2,1)S(1)} %broadcast_select_fusion), channel_id=1, source_target_pairs={{0,4},{1,5},{2,6},{3,7},{4,0},{5,1},{6,2},{7,3},{8,12},{9,13},{10,... | collective-permute-start | bytes 196616 | tf_op jit(solution)/shard_map/ppermute | solution.py:139
  16.2 10.9 %all-to-all-start = ((bf16[8,2,64,512]{3,2,1,0:T(8,128)(2,1)}), bf16[8,2,64,512]{3,2,1,0:T(8,128)(2,1)S(1)}, u32[]{:S(2)}, u32[]{:S(2)}) async-start(bf16[8,2,64,512]{3,2,1,0:T(8,128)(2,1)} %norm.1), calls=%async_computation | async-start | bytes 2097152 | tf_op jit(solution)/shard_map/all_to_all | solution.py:391
  34.1 33.8 %collective-permute-done.1 = bf16[2,2,16,1024]{3,2,1,0:T(8,128)(2,1)S(1)} collective-permute-done((bf16[2,2,16,1024]{3,2,1,0:T(8,128)(2,1)S(1)}, bf16[2,2,16,1024]{3,2,1,0:T(8,128)(2,1)S(1)}, u32[]{:S(2)}, u32[]{:S(2)}) %collective-permute-start.1) | collective-permute-done | bytes 131104 | tf_op jit(solution)/shard_map/ppermute | solution.py:139
  67.9 12.8 %all-to-all-done.in_ref = bf16[8,2,64,512]{3,2,1,0:T(8,128)(2,1)S(1)} async-done(((bf16[8,2,64,512]{3,2,1,0:T(8,128)(2,1)}), bf16[8,2,64,512]{3,2,1,0:T(8,128)(2,1)S(1)}, u32[]{:S(2)}, u32[]{:S(2)}) %all-to-all-start) | async-done | bytes 1048608 | tf_op jit(solution)/shard_map/all_to_all | solution.py:391
  82.7 14.0 %collective-permute-start.4 = (bf16[1,2,16,1024]{3,2,1,0:T(8,128)(2,1)S(1)}, bf16[1,2,16,1024]{3,2,1,0:T(8,128)(2,1)S(1)}, u32[]{:S(2)}, u32[]{:S(2)}) collective-permute-start(bf16[1,2,16,1024]{3,2,1,0:T(8,128)(2,1)S(1)} %collective-permute-done.2), channel_id=1, source_target_pairs={{0,4},{1,5},{2,6},{3,7},{4,0},{5,1},{6,2},{7,3},{8,12},{9,13},{10,... | collective-permute-start | bytes 196616 | tf_op jit(solution)/shard_map/ppermute | solution.py:139
  96.8 11.4 %attention.1 = bf16[8,2,64,512]{3,2,1,0:T(8,128)(2,1)} custom-call(s32[2]{0:T(128)} %and_select_fusion.which, s32[32]{0:T(128)} %reshape_squeeze.3.ids, bf16[8,2,64,512]{3,2,1,0:T(8,128)(2,1)} %copy-done.3, bf16[2,4,128,128]{3,2,1,0:T(8,128)(2,1)} %bitcast.20, bf16[2,4,128,128]{3,2,1,0:T(8,128)(2,1)} %bitcast.22, bf16[2,4,128,128]{3,2,1,0:T(8,128)(2,1)} %bitcast.24), custom_call_target="tpu_custom_call" | custom-call | flops 1207959552 | bytes 2883584 | tf_op jit(solution)/shard_map/attention/pallas_call | solution.py:115
  119.2 26.4 %collective-permute-done.5 = bf16[2,2,16,1024]{3,2,1,0:T(8,128)(2,1)S(1)} collective-permute-done((bf16[2,2,16,1024]{3,2,1,0:T(8,128)(2,1)S(1)}, bf16[2,2,16,1024]{3,2,1,0:T(8,128)(2,1)S(1)}, u32[]{:S(2)}, u32[]{:S(2)}) %collective-permute-start.5) | collective-permute-done | bytes 131104 | tf_op jit(solution)/shard_map/ppermute | solution.py:139
  148.5 6.2 %all-to-all-done.1.att_ref = bf16[8,2,64,512]{3,2,1,0:T(8,128)(2,1)S(1)} async-done(((bf16[8,2,64,512]{3,2,1,0:T(8,128)(2,1)}), bf16[8,2,64,512]{3,2,1,0:T(8,128)(2,1)S(1)}, u32[]{:S(2)}, u32[]{:S(2)}) %all-to-all-start.1) | async-done | bytes 1048608 | tf_op jit(solution)/shard_map/all_to_all | solution.py:391
  155.7 9.1 %mix_send.1 = (bf16[2,17,16,128]{3,2,1,0:T(8,128)(2,1)}, bf16[2,17,16,128]{3,2,1,0:T(8,128)(2,1)}, bf16[2,17,16,128]{3,2,1,0:T(8,128)(2,1)}, bf16[2,17,16,128]{3...) custom-call(s32[2]{0:T(128)} %and_select_fusion.which, ...), custom_call_target="tpu_custom_call" | custom-call | flops 33554432 | bytes 4194304 | tf_op jit(solution)/shard_map/mix_send/pallas_call | solution.py:241
  170.6 5.1 %collective-permute-start.8 = (bf16[2,17,16,128]{3,2,1,0:T(8,128)(2,1)}, bf16[2,17,16,128]{3,2,1,0:T(8,128)(2,1)S(1)}, u32[]{:S(2)}, u32[]{:S(2)}) collective-permute-start(bf16[2,17,16,128]{3,2,1,0:T(8,128)(2,1)} %get-tuple-element.47), channel_id=1, source_target_pairs={{0,10},{1,11},{2,8},{3,9},{4,14},{5,15},{6,12},{7,13},{8,18},{9,19... | collective-permute-start | bytes 417800 | tf_op jit(solution)/shard_map/ppermute | solution.py:402
  175.7 8.9 %collective-permute-start.9 = (bf16[2,17,16,128]{3,2,1,0:T(8,128)(2,1)}, bf16[2,17,16,128]{3,2,1,0:T(8,128)(2,1)S(1)}, u32[]{:S(2)}, u32[]{:S(2)}) collective-permute-start(bf16[2,17,16,128]{3,2,1,0:T(8,128)(2,1)} %get-tuple-element.48), channel_id=1, source_target_pairs={{0,11},{1,10},{2,9},{3,8},{4,15},{5,14},{6,13},{7,12},{8,19},{9,18... | collective-permute-start | bytes 417800 | tf_op jit(solution)/shard_map/ppermute | solution.py:402
  187.7 9.1 %collective-permute-done.6.refs_0_ = bf16[2,17,16,128]{3,2,1,0:T(8,128)(2,1)S(1)} collective-permute-done((bf16[2,17,16,128]{3,2,1,0:T(8,128)(2,1)}, bf16[2,17,16,128]{3,2,1,0:T(8,128)(2,1)S(1)}, u32[]{:S(2)}, u32[]{:S(2)}) %collective-permute-start.6) | collective-permute-done | bytes 139296 | tf_op jit(solution)/shard_map/ppermute | solution.py:402
  204.6 6.4 %collective-permute-done.9.refs_3_ = bf16[2,17,16,128]{3,2,1,0:T(8,128)(2,1)S(1)} collective-permute-done((bf16[2,17,16,128]{3,2,1,0:T(8,128)(2,1)}, bf16[2,17,16,128]{3,2,1,0:T(8,128)(2,1)S(1)}, u32[]{:S(2)}, u32[]{:S(2)}) %collective-permute-start.9) | collective-permute-done | bytes 139296 | tf_op jit(solution)/shard_map/ppermute | solution.py:402
  215.1 5.6 %collective-permute-done.12.refs_6_ = bf16[2,17,16,128]{3,2,1,0:T(8,128)(2,1)S(1)} collective-permute-done((bf16[2,17,16,128]{3,2,1,0:T(8,128)(2,1)}, bf16[2,17,16,128]{3,2,1,0:T(8,128)(2,1)S(1)}, u32[]{:S(2)}, u32[]{:S(2)}) %collective-permute-start.12) | collective-permute-done | bytes 139296 | tf_op jit(solution)/shard_map/ppermute | solution.py:402
  220.8 5.8 %collective-permute-start.14 = (bf16[4,2,16,1024]{3,2,1,0:T(8,128)(2,1)S(1)}, bf16[4,2,16,1024]{3,2,1,0:T(8,128)(2,1)S(1)}, u32[]{:S(2)}, u32[]{:S(2)}) collective-permute-start(bf16[4,2,16,1024]{3,2,1,0:T(8,128)(2,1)S(1)} %constant_dynamic-update-slice_fusion.4), channel_id=1, source_target_pairs={{0,1},{1,0},{2,3},{3,2},{4,5},{5,4},{6,7},{7,6},{8,9},{9,8},{10,11... | collective-permute-start | bytes 786440 | tf_op jit(solution)/shard_map/ppermute | solution.py:139
  227.2 14.4 %attention_send.1 = (bf16[2,2,4,64,128]{4,3,2,1,0:T(8,128)(2,1)}, bf16[2,2,4,64,128]{4,3,2,1,0:T(8,128)(2,1)}, bf16[2,2,4,64,128]{4,3,2,1,0:T(8,128)(2,1)}, bf16...) custom-call(s32[2]{0:T(128)} %and_select_fusion.1.which, ...), custom_call_target="tpu_custom_call" | custom-call | flops 1207959552 | bytes 2883584 | tf_op jit(solution)/shard_map/attention_send/pallas_call | solution.py:307
  251.0 9.1 %collective-permute-start.18 = (bf16[2,2,4,64,128]{4,3,2,1,0:T(8,128)(2,1)}, bf16[2,2,4,64,128]{4,3,2,1,0:T(8,128)(2,1)S(1)}, u32[]{:S(2)}, u32[]{:S(2)}) collective-permute-start(bf16[2,2,4,64,128]{4,3,2,1,0:T(8,128)(2,1)} %get-tuple-element.65), channel_id=1, source_target_pairs={{0,11},{1,10},{2,9},{3,8},{4,15},{5,14},{6,13},{7,12},{8,19},{9,18... | collective-permute-start | bytes 786440 | tf_op jit(solution)/shard_map/ppermute | solution.py:402
  269.0 9.9 %collective-permute-done.16.refs_1_ = bf16[2,2,4,64,128]{4,3,2,1,0:T(8,128)(2,1)S(1)} collective-permute-done((bf16[2,2,4,64,128]{4,3,2,1,0:T(8,128)(2,1)}, bf16[2,2,4,64,128]{4,3,2,1,0:T(8,128)(2,1)S(1)}, u32[]{:S(2)}, u32[]{:S(2)}) %collective-permute-start.16) | collective-permute-done | bytes 262176 | tf_op jit(solution)/shard_map/ppermute | solution.py:402
  278.8 8.0 %collective-permute-start.21 = (bf16[2,2,4,64,128]{4,3,2,1,0:T(8,128)(2,1)S(1)}, bf16[2,2,4,64,128]{4,3,2,1,0:T(8,128)(2,1)S(1)}, u32[]{:S(2)}, u32[]{:S(2)}) collective-permute-start(bf16[2,2,4,64,128]{4,3,2,1,0:T(8,128)(2,1)S(1)} %copy-done.15), channel_id=1, source_target_pairs={{0,14},{1,15},{2,12},{3,13},{4,10},{5,11},{6,8},{7,9},{8,22},{9,23... | collective-permute-start | bytes 786440 | tf_op jit(solution)/shard_map/ppermute | solution.py:402
  286.9 23.7 %collective-permute-done.17.refs_2_ = bf16[2,2,4,64,128]{4,3,2,1,0:T(8,128)(2,1)S(1)} collective-permute-done((bf16[2,2,4,64,128]{4,3,2,1,0:T(8,128)(2,1)}, bf16[2,2,4,64,128]{4,3,2,1,0:T(8,128)(2,1)S(1)}, u32[]{:S(2)}, u32[]{:S(2)}) %collective-permute-start.17) | collective-permute-done | bytes 262176 | tf_op jit(solution)/shard_map/ppermute | solution.py:402
  316.1 9.0 %collective-permute-done.18.refs_3_ = bf16[2,2,4,64,128]{4,3,2,1,0:T(8,128)(2,1)S(1)} collective-permute-done((bf16[2,2,4,64,128]{4,3,2,1,0:T(8,128)(2,1)}, bf16[2,2,4,64,128]{4,3,2,1,0:T(8,128)(2,1)S(1)}, u32[]{:S(2)}, u32[]{:S(2)}) %collective-permute-start.18) | collective-permute-done | bytes 262176 | tf_op jit(solution)/shard_map/ppermute | solution.py:402
  325.1 9.8 %collective-permute-done.21.refs_6_ = bf16[2,2,4,64,128]{4,3,2,1,0:T(8,128)(2,1)S(1)} collective-permute-done((bf16[2,2,4,64,128]{4,3,2,1,0:T(8,128)(2,1)S(1)}, bf16[2,2,4,64,128]{4,3,2,1,0:T(8,128)(2,1)S(1)}, u32[]{:S(2)}, u32[]{:S(2)}) %collective-permute-start.21) | collective-permute-done | bytes 262176 | tf_op jit(solution)/shard_map/ppermute | solution.py:402
  334.9 13.7 %collective-permute-done.22.refs_7_ = bf16[2,2,4,64,128]{4,3,2,1,0:T(8,128)(2,1)S(1)} collective-permute-done((bf16[2,2,4,64,128]{4,3,2,1,0:T(8,128)(2,1)S(1)}, bf16[2,2,4,64,128]{4,3,2,1,0:T(8,128)(2,1)S(1)}, u32[]{:S(2)}, u32[]{:S(2)}) %collective-permute-start.22) | collective-permute-done | bytes 262176 | tf_op jit(solution)/shard_map/ppermute | solution.py:402
  349.2 8.2 %mix_final.1 = bf16[2,64,4096]{2,1,0:T(8,128)(2,1)} custom-call(s32[2]{0:T(128)} %get-tuple-element.76.which, s32[1]{0:T(128)} %bitcast.me, s32[2]{0:T(128)} %get-tuple-element.75.target, bf16[2,2,4,64,128]{4,3,2,1,0:T(8,128)(2,1)} %copy-done.4, bf16[2,2,4,64,128]{4,3,2,1,0:T(8,128)(2,1)} %copy-done.5, bf16[2,2,4,64,128]{4,3,2,1,0:T(8,128)(2,1)} %copy-done.6, ...), custom_call_target="tpu_custom_call" | custom-call | flops 33554432 | bytes 4194304 | tf_op jit(solution)/shard_map/mix_final/pallas_call | solution.py:364
  (105 shorter events, 76.5 us)
Async XLA Ops:
  16.2 64.5 %all-to-all-start = ((bf16[8,2,64,512]{3,2,1,0:T(8,128)(2,1)}), bf16[8,2,64,512]{3,2,1,0:T(8,128)(2,1)S(1)}, u32[]{:S(2)}, u32[]{:S(2)}) async-start(bf16[8,2,64,512]{3,2,1,0:T(8,128)(2,1)} %norm.1), calls=%async_computation | async-start | bytes 2097152 | tf_op jit(solution)/shard_map/all_to_all | solution.py:391
  27.1 40.8 %collective-permute-start.1 = (bf16[2,2,16,1024]{3,2,1,0:T(8,128)(2,1)S(1)}, bf16[2,2,16,1024]{3,2,1,0:T(8,128)(2,1)S(1)}, u32[]{:S(2)}, u32[]{:S(2)}) collective-permute-start(bf16[2,2,16,1024]{3,2,1,0:T(8,128)(2,1)S(1)} %pad_maximum_fusion.2), channel_id=1, source_target_pairs={{0,2},{1,3},{2,0},{3,1},{4,6},{5,7},{6,4},{7,5},{8,10},{9,11},{10,... | collective-permute-start | bytes 393224 | tf_op jit(solution)/shard_map/ppermute | solution.py:139
  31.4 36.5 %collective-permute-start.2 = (bf16[1,2,16,1024]{3,2,1,0:T(8,128)(2,1)S(1)}, bf16[1,2,16,1024]{3,2,1,0:T(8,128)(2,1)S(1)}, u32[]{:S(2)}, u32[]{:S(2)}) collective-permute-start(bf16[1,2,16,1024]{3,2,1,0:T(8,128)(2,1)S(1)} %broadcast_select_fusion), channel_id=1, source_target_pairs={{0,8},{8,16},{16,24},{24,32},{32,40},{40,48},{48,56},{56,64},{64,7... | collective-permute-start | bytes 196616 | tf_op jit(solution)/shard_map/ppermute | solution.py:408
  80.8 27.4 %collective-permute-start.3 = (bf16[4,2,16,1024]{3,2,1,0:T(8,128)(2,1)S(1)}, bf16[4,2,16,1024]{3,2,1,0:T(8,128)(2,1)S(1)}, u32[]{:S(2)}, u32[]{:S(2)}) collective-permute-start(bf16[4,2,16,1024]{3,2,1,0:T(8,128)(2,1)S(1)} %pad_maximum_fusion.1), channel_id=1, source_target_pairs={{0,1},{1,0},{2,3},{3,2},{4,5},{5,4},{6,7},{7,6},{8,9},{9,8},{10,11... | collective-permute-start | bytes 786440 | tf_op jit(solution)/shard_map/ppermute | solution.py:139
  82.7 25.5 %collective-permute-start.4 = (bf16[1,2,16,1024]{3,2,1,0:T(8,128)(2,1)S(1)}, bf16[1,2,16,1024]{3,2,1,0:T(8,128)(2,1)S(1)}, u32[]{:S(2)}, u32[]{:S(2)}) collective-permute-start(bf16[1,2,16,1024]{3,2,1,0:T(8,128)(2,1)S(1)} %collective-permute-done.2), channel_id=1, source_target_pairs={{0,4},{1,5},{2,6},{3,7},{4,0},{5,1},{6,2},{7,3},{8,12},{9,13},{10,... | collective-permute-start | bytes 196616 | tf_op jit(solution)/shard_map/ppermute | solution.py:139
  109.1 45.7 %all-to-all-start.1 = ((bf16[8,2,64,512]{3,2,1,0:T(8,128)(2,1)}), bf16[8,2,64,512]{3,2,1,0:T(8,128)(2,1)S(1)}, u32[]{:S(2)}, u32[]{:S(2)}) async-start(bf16[8,2,64,512]{3,2,1,0:T(8,128)(2,1)} %attention.1), calls=%async_computation.1 | async-start | bytes 2097152 | tf_op jit(solution)/shard_map/all_to_all | solution.py:391
  113.7 31.9 %collective-permute-start.5 = (bf16[2,2,16,1024]{3,2,1,0:T(8,128)(2,1)S(1)}, bf16[2,2,16,1024]{3,2,1,0:T(8,128)(2,1)S(1)}, u32[]{:S(2)}, u32[]{:S(2)}) collective-permute-start(bf16[2,2,16,1024]{3,2,1,0:T(8,128)(2,1)S(1)} %get-tuple-element.72), channel_id=1, source_target_pairs={{0,2},{1,3},{2,0},{3,1},{4,6},{5,7},{6,4},{7,5},{8,10},{9,11},{10,... | collective-permute-start | bytes 393224 | tf_op jit(solution)/shard_map/ppermute | solution.py:139
  164.7 32.1 %collective-permute-start.6 = (bf16[2,17,16,128]{3,2,1,0:T(8,128)(2,1)}, bf16[2,17,16,128]{3,2,1,0:T(8,128)(2,1)S(1)}, u32[]{:S(2)}, u32[]{:S(2)}) collective-permute-start(bf16[2,17,16,128]{3,2,1,0:T(8,128)(2,1)} %get-tuple-element.45), channel_id=1, source_target_pairs={{0,8},{1,9},{2,10},{3,11},{4,12},{5,13},{6,14},{7,15},{8,16},{9,17... | collective-permute-start | bytes 417800 | tf_op jit(solution)/shard_map/ppermute | solution.py:402
  166.7 32.1 %collective-permute-start.7 = (bf16[2,17,16,128]{3,2,1,0:T(8,128)(2,1)}, bf16[2,17,16,128]{3,2,1,0:T(8,128)(2,1)S(1)}, u32[]{:S(2)}, u32[]{:S(2)}) collective-permute-start(bf16[2,17,16,128]{3,2,1,0:T(8,128)(2,1)} %get-tuple-element.46), channel_id=1, source_target_pairs={{0,9},{1,8},{2,11},{3,10},{4,13},{5,12},{6,15},{7,14},{8,17},{9,16... | collective-permute-start | bytes 417800 | tf_op jit(solution)/shard_map/ppermute | solution.py:402
  170.6 30.1 %collective-permute-start.8 = (bf16[2,17,16,128]{3,2,1,0:T(8,128)(2,1)}, bf16[2,17,16,128]{3,2,1,0:T(8,128)(2,1)S(1)}, u32[]{:S(2)}, u32[]{:S(2)}) collective-permute-start(bf16[2,17,16,128]{3,2,1,0:T(8,128)(2,1)} %get-tuple-element.47), channel_id=1, source_target_pairs={{0,10},{1,11},{2,8},{3,9},{4,14},{5,15},{6,12},{7,13},{8,18},{9,19... | collective-permute-start | bytes 417800 | tf_op jit(solution)/shard_map/ppermute | solution.py:402
  175.7 35.2 %collective-permute-start.9 = (bf16[2,17,16,128]{3,2,1,0:T(8,128)(2,1)}, bf16[2,17,16,128]{3,2,1,0:T(8,128)(2,1)S(1)}, u32[]{:S(2)}, u32[]{:S(2)}) collective-permute-start(bf16[2,17,16,128]{3,2,1,0:T(8,128)(2,1)} %get-tuple-element.48), channel_id=1, source_target_pairs={{0,11},{1,10},{2,9},{3,8},{4,15},{5,14},{6,13},{7,12},{8,19},{9,18... | collective-permute-start | bytes 417800 | tf_op jit(solution)/shard_map/ppermute | solution.py:402
  184.6 26.4 %collective-permute-start.10 = (bf16[2,17,16,128]{3,2,1,0:T(8,128)(2,1)}, bf16[2,17,16,128]{3,2,1,0:T(8,128)(2,1)S(1)}, u32[]{:S(2)}, u32[]{:S(2)}) collective-permute-start(bf16[2,17,16,128]{3,2,1,0:T(8,128)(2,1)} %get-tuple-element.49), channel_id=1, source_target_pairs={{0,12},{1,13},{2,14},{3,15},{4,8},{5,9},{6,10},{7,11},{8,20},{9,21... | collective-permute-start | bytes 417800 | tf_op jit(solution)/shard_map/ppermute | solution.py:402
  196.8 18.3 %collective-permute-start.11 = (bf16[2,17,16,128]{3,2,1,0:T(8,128)(2,1)}, bf16[2,17,16,128]{3,2,1,0:T(8,128)(2,1)S(1)}, u32[]{:S(2)}, u32[]{:S(2)}) collective-permute-start(bf16[2,17,16,128]{3,2,1,0:T(8,128)(2,1)} %get-tuple-element.50), channel_id=1, source_target_pairs={{0,13},{1,12},{2,15},{3,14},{4,9},{5,8},{6,11},{7,10},{8,21},{9,20... | collective-permute-start | bytes 417800 | tf_op jit(solution)/shard_map/ppermute | solution.py:402
  198.7 22.0 %collective-permute-start.12 = (bf16[2,17,16,128]{3,2,1,0:T(8,128)(2,1)}, bf16[2,17,16,128]{3,2,1,0:T(8,128)(2,1)S(1)}, u32[]{:S(2)}, u32[]{:S(2)}) collective-permute-start(bf16[2,17,16,128]{3,2,1,0:T(8,128)(2,1)} %get-tuple-element.51), channel_id=1, source_target_pairs={{0,14},{1,15},{2,12},{3,13},{4,10},{5,11},{6,8},{7,9},{8,22},{9,23... | collective-permute-start | bytes 417800 | tf_op jit(solution)/shard_map/ppermute | solution.py:402
  200.7 20.1 %collective-permute-start.13 = (bf16[2,17,16,128]{3,2,1,0:T(8,128)(2,1)}, bf16[2,17,16,128]{3,2,1,0:T(8,128)(2,1)S(1)}, u32[]{:S(2)}, u32[]{:S(2)}) collective-permute-start(bf16[2,17,16,128]{3,2,1,0:T(8,128)(2,1)} %get-tuple-element.52), channel_id=1, source_target_pairs={{0,15},{1,14},{2,13},{3,12},{4,11},{5,10},{6,9},{7,8},{8,23},{9,22... | collective-permute-start | bytes 417800 | tf_op jit(solution)/shard_map/ppermute | solution.py:402
  220.8 20.9 %collective-permute-start.14 = (bf16[4,2,16,1024]{3,2,1,0:T(8,128)(2,1)S(1)}, bf16[4,2,16,1024]{3,2,1,0:T(8,128)(2,1)S(1)}, u32[]{:S(2)}, u32[]{:S(2)}) collective-permute-start(bf16[4,2,16,1024]{3,2,1,0:T(8,128)(2,1)S(1)} %constant_dynamic-update-slice_fusion.4), channel_id=1, source_target_pairs={{0,1},{1,0},{2,3},{3,2},{4,5},{5,4},{6,7},{7,6},{8,9},{9,8},{10,11... | collective-permute-start | bytes 786440 | tf_op jit(solution)/shard_map/ppermute | solution.py:139
  242.5 23.8 %collective-permute-start.15 = (bf16[2,2,4,64,128]{4,3,2,1,0:T(8,128)(2,1)}, bf16[2,2,4,64,128]{4,3,2,1,0:T(8,128)(2,1)S(1)}, u32[]{:S(2)}, u32[]{:S(2)}) collective-permute-start(bf16[2,2,4,64,128]{4,3,2,1,0:T(8,128)(2,1)} %get-tuple-element.62), channel_id=1, source_target_pairs={{0,8},{1,9},{2,10},{3,11},{4,12},{5,13},{6,14},{7,15},{8,16},{9,17... | collective-permute-start | bytes 786440 | tf_op jit(solution)/shard_map/ppermute | solution.py:402
  244.6 34.3 %collective-permute-start.16 = (bf16[2,2,4,64,128]{4,3,2,1,0:T(8,128)(2,1)}, bf16[2,2,4,64,128]{4,3,2,1,0:T(8,128)(2,1)S(1)}, u32[]{:S(2)}, u32[]{:S(2)}) collective-permute-start(bf16[2,2,4,64,128]{4,3,2,1,0:T(8,128)(2,1)} %get-tuple-element.63), channel_id=1, source_target_pairs={{0,9},{1,8},{2,11},{3,10},{4,13},{5,12},{6,15},{7,14},{8,17},{9,16... | collective-permute-start | bytes 786440 | tf_op jit(solution)/shard_map/ppermute | solution.py:402
  249.0 61.6 %collective-permute-start.17 = (bf16[2,2,4,64,128]{4,3,2,1,0:T(8,128)(2,1)}, bf16[2,2,4,64,128]{4,3,2,1,0:T(8,128)(2,1)S(1)}, u32[]{:S(2)}, u32[]{:S(2)}) collective-permute-start(bf16[2,2,4,64,128]{4,3,2,1,0:T(8,128)(2,1)} %get-tuple-element.64), channel_id=1, source_target_pairs={{0,10},{1,11},{2,8},{3,9},{4,14},{5,15},{6,12},{7,13},{8,18},{9,19... | collective-permute-start | bytes 786440 | tf_op jit(solution)/shard_map/ppermute | solution.py:402
  251.0 74.1 %collective-permute-start.18 = (bf16[2,2,4,64,128]{4,3,2,1,0:T(8,128)(2,1)}, bf16[2,2,4,64,128]{4,3,2,1,0:T(8,128)(2,1)S(1)}, u32[]{:S(2)}, u32[]{:S(2)}) collective-permute-start(bf16[2,2,4,64,128]{4,3,2,1,0:T(8,128)(2,1)} %get-tuple-element.65), channel_id=1, source_target_pairs={{0,11},{1,10},{2,9},{3,8},{4,15},{5,14},{6,13},{7,12},{8,19},{9,18... | collective-permute-start | bytes 786440 | tf_op jit(solution)/shard_map/ppermute | solution.py:402
  260.1 65.0 %collective-permute-start.19 = (bf16[2,2,4,64,128]{4,3,2,1,0:T(8,128)(2,1)S(1)}, bf16[2,2,4,64,128]{4,3,2,1,0:T(8,128)(2,1)S(1)}, u32[]{:S(2)}, u32[]{:S(2)}) collective-permute-start(bf16[2,2,4,64,128]{4,3,2,1,0:T(8,128)(2,1)S(1)} %copy-done.17), channel_id=1, source_target_pairs={{0,12},{1,13},{2,14},{3,15},{4,8},{5,9},{6,10},{7,11},{8,20},{9,21... | collective-permute-start | bytes 786440 | tf_op jit(solution)/shard_map/ppermute | solution.py:402
  266.3 58.7 %collective-permute-start.20 = (bf16[2,2,4,64,128]{4,3,2,1,0:T(8,128)(2,1)S(1)}, bf16[2,2,4,64,128]{4,3,2,1,0:T(8,128)(2,1)S(1)}, u32[]{:S(2)}, u32[]{:S(2)}) collective-permute-start(bf16[2,2,4,64,128]{4,3,2,1,0:T(8,128)(2,1)S(1)} %copy-done.16), channel_id=1, source_target_pairs={{0,13},{1,12},{2,15},{3,14},{4,9},{5,8},{6,11},{7,10},{8,21},{9,20... | collective-permute-start | bytes 786440 | tf_op jit(solution)/shard_map/ppermute | solution.py:402
  278.8 56.0 %collective-permute-start.21 = (bf16[2,2,4,64,128]{4,3,2,1,0:T(8,128)(2,1)S(1)}, bf16[2,2,4,64,128]{4,3,2,1,0:T(8,128)(2,1)S(1)}, u32[]{:S(2)}, u32[]{:S(2)}) collective-permute-start(bf16[2,2,4,64,128]{4,3,2,1,0:T(8,128)(2,1)S(1)} %copy-done.15), channel_id=1, source_target_pairs={{0,14},{1,15},{2,12},{3,13},{4,10},{5,11},{6,8},{7,9},{8,22},{9,23... | collective-permute-start | bytes 786440 | tf_op jit(solution)/shard_map/ppermute | solution.py:402
  310.6 37.9 %collective-permute-start.22 = (bf16[2,2,4,64,128]{4,3,2,1,0:T(8,128)(2,1)S(1)}, bf16[2,2,4,64,128]{4,3,2,1,0:T(8,128)(2,1)S(1)}, u32[]{:S(2)}, u32[]{:S(2)}) collective-permute-start(bf16[2,2,4,64,128]{4,3,2,1,0:T(8,128)(2,1)S(1)} %copy-done.14), channel_id=1, source_target_pairs={{0,15},{1,14},{2,13},{3,12},{4,11},{5,10},{6,9},{7,8},{8,23},{9,22... | collective-permute-start | bytes 786440 | tf_op jit(solution)/shard_map/ppermute | solution.py:402
  (27 other events, 537.2 us)
